TPU v7x, 512 devices: a whole 4x8x8 slice. The times are simulated.
512 devices in a mesh: seq: 64 (over y, z), mp: 8 (over x, core).
Axes of the slice: x: 4, y: 8, z: 8, core: 2. Of those that a mesh axis runs over, the one named last changes fastest.
Arguments:
- patch_states: bfloat16 [32768, 2048], P('seq'), may hold values from -6 to 6
- mlp_gain: bfloat16 [2048], replicated, may hold values from 0.099609375 to 1.8984375
- up_weight: bfloat16 [2048, 7168], P('seq', 'mp')
- down_weight: bfloat16 [7168, 2048], P('mp', 'seq')
- kv_gain: bfloat16 [2048], replicated, may hold values from 0.099609375 to 1.8984375
- kv_weight: bfloat16 [2048, 2048], P(None, 'mp'), may hold values from -0.125 to 0.125
- byte_states: bfloat16 [65536, 1024], P('seq'), may hold values from -6 to 6
- query_weight: bfloat16 [1024, 1024], P(None, 'mp'), may hold values from -0.1875 to 0.1875
- out_weight: bfloat16 [1024, 1024], P('mp'), may hold values from -0.75 to 0.75
- patch_counts: int32 [64], P('seq'), may hold values from 256 to 512, as said below
- byte_patch: int32 [65536], P('seq'), may hold values from 0 to 511, as said below
Outputs:
- decoded: bfloat16 [65536, 1024], P(('seq', 'mp'))
Inputs may be any that keep to these rules, and one draw needn't show every extreme that they name: `patch_counts`: exactly 512 in some block and exactly 256 in another, in every draw. `byte_patch`: within each seq block of 1024 bytes the values start at 0, never fall, rise by at most one from one byte to the next, and end at that block's patch count minus one.
All inputs are finite; a program needn't handle non-finite values.
Results may differ from a plain program's by a relative error of at most 0.02.
Values may be sent and summed in bfloat16 or wider, within the bound.
No kernel may reach another device: no remote copies, remote signals or barrier semaphores. Data moves between devices by JAX's collectives and lax.ppermute only.
A program may use at most 64 MiB of HBM per device.

v0:
```python
import math

import jax
import jax.numpy as jnp
from jax import lax
from jax.sharding import PartitionSpec as P

HS = 128
WIN = 1024


def entering(value, axis, join, neutral):
    count, mine = (lax.axis_size(axis), lax.axis_index(axis))
    pieces = jax.tree.map(lambda part: lax.all_gather(part, axis), value)
    so_far = jax.tree.map(
        lambda part, zero: jnp.full_like(part, 0) + jnp.asarray(zero, part.dtype), value, neutral
    )

    def step(position, so_far):
        longer = join(so_far, jax.tree.map(lambda part: part[position], pieces))
        return jax.tree.map(lambda new, old: jnp.where(position < mine, new, old), longer, so_far)

    return lax.fori_loop(0, count - 1, step, so_far)


def from_behind(value, axis, steps):
    count = lax.axis_size(axis)
    leading, last = (max(0, -steps), min(count, count - steps))
    return lax.ppermute(value, axis, [(source, source + steps) for source in range(leading, last)])


def scale_rows(values, gain):
    return values * lax.rsqrt(jnp.mean(values * values, axis=-1, keepdims=True) + 1e-05) * gain


def unit_rows(values):
    return values * lax.rsqrt(jnp.mean(values * values, axis=-1, keepdims=True) + 1e-06)


def on_device(
    patch_states,
    mlp_gain,
    up_weight,
    down_weight,
    kv_gain,
    kv_weight,
    byte_states,
    query_weight,
    out_weight,
    patch_counts,
    byte_patch,
):
    patch_rows = patch_states.shape[0]
    normed = scale_rows(patch_states.astype(jnp.float32), mlp_gain.astype(jnp.float32)).astype(
        jnp.bfloat16
    )
    preact = jnp.dot(
        normed,
        lax.all_gather(up_weight, "seq", axis=0, tiled=True),
        preferred_element_type=jnp.float32,
    )
    hidden = jax.nn.gelu(preact, approximate=False).astype(jnp.bfloat16)
    kv_scale = kv_gain.astype(jnp.float32)
    partial_value = jnp.dot(
        hidden,
        lax.all_gather(down_weight, "seq", axis=1, tiled=True),
        preferred_element_type=jnp.float32,
    )
    mixed_out = lax.psum(partial_value.astype(jnp.bfloat16), "mp").astype(jnp.float32)
    kv_in = scale_rows(patch_states.astype(jnp.float32) + mixed_out, kv_scale).astype(jnp.bfloat16)
    heads_here = kv_weight.shape[1] // (2 * HS)
    projected = jnp.dot(kv_in, kv_weight, preferred_element_type=jnp.float32).reshape(
        patch_rows, heads_here, 2, HS
    )
    keys = unit_rows(projected[:, :, 0])
    kv_pack = (
        jnp.stack([keys, projected[:, :, 1]], axis=2)
        .astype(jnp.bfloat16)
        .reshape(patch_rows, heads_here * 2 * HS)
    )
    bytes_here = byte_states.shape[0]
    query_proj = jnp.dot(byte_states, query_weight, preferred_element_type=jnp.float32).reshape(
        bytes_here, heads_here, HS
    )
    queries = unit_rows(query_proj).astype(jnp.bfloat16)
    depth_back = (WIN + patch_rows // 2 - 2) // (patch_rows // 2)
    own_count = patch_counts[0]
    slots = jnp.arange(depth_back, dtype=jnp.int32)

    def join_windows(earlier_part, later_part):
        early_vals, early_len = earlier_part
        late_vals, late_len = later_part
        from_late = slots >= depth_back - late_len
        wanted = slots + late_len
        early_pick = jnp.sum(
            jnp.where(slots[None, :] == wanted[:, None], early_vals[None, :], 0), axis=1
        ).astype(jnp.int32)
        joined = jnp.where(from_late, late_vals, early_pick).astype(jnp.int32)
        return (joined, jnp.minimum(early_len + late_len, depth_back).astype(jnp.int32))

    own_window = jnp.where(slots == depth_back - 1, own_count, 0)
    empty_window = (jnp.zeros((depth_back,), jnp.int32), jnp.zeros((), jnp.int32))
    prior_counts, prior_len = entering(
        (own_window, jnp.ones((), jnp.int32)), "seq", join_windows, empty_window
    )
    earlier = []
    forwarded = kv_pack
    for offset_back in range(1, depth_back + 1):
        forwarded = from_behind(forwarded, "seq", 1)
        earlier.append(forwarded)
    score_scale = 2.0 / math.sqrt(HS)
    positions = jnp.arange(patch_rows, dtype=jnp.int32)
    numerator = jnp.zeros((bytes_here, heads_here, HS), jnp.float32)
    denominator = jnp.zeros((heads_here, bytes_here), jnp.float32)
    for distance, kv_block in enumerate([kv_pack] + earlier):
        if distance == 0:
            first_id = jnp.zeros((), jnp.int32)
            live_count = own_count
        else:
            first_id = -jnp.sum(prior_counts[depth_back - distance :]).astype(jnp.int32)
            live_count = prior_counts[depth_back - distance]
        key_ids = first_id + positions
        usable = (
            (positions < live_count)[None, :]
            & (key_ids[None, :] <= byte_patch[:, None])
            & (key_ids[None, :] > byte_patch[:, None] - WIN)
        )
        kv_parts = kv_block.reshape(patch_rows, heads_here, 2, HS)
        scores = (
            jnp.einsum(
                "bhd,phd->hbp", queries, kv_parts[:, :, 0], preferred_element_type=jnp.float32
            )
            * score_scale
        )
        weights = jnp.where(usable[None], jnp.exp(scores), 0.0)
        numerator = numerator + jnp.einsum(
            "hbp,phd->bhd",
            weights.astype(jnp.bfloat16),
            kv_parts[:, :, 1],
            preferred_element_type=jnp.float32,
        )
        denominator = denominator + jnp.sum(weights, axis=-1)
    attended = (
        (numerator / jnp.transpose(denominator)[:, :, None])
        .astype(jnp.bfloat16)
        .reshape(bytes_here, heads_here * HS)
    )
    decoded = lax.psum_scatter(
        jnp.dot(attended, out_weight, preferred_element_type=jnp.float32).astype(jnp.bfloat16),
        "mp",
        scatter_dimension=0,
        tiled=True,
    )
    return decoded


def solution(mesh):
    in_specs = (
        P("seq", None),
        P(),
        P("seq", "mp"),
        P("mp", "seq"),
        P(),
        P(None, "mp"),
        P("seq", None),
        P(None, "mp"),
        P("mp", None),
        P("seq"),
        P("seq"),
    )
    out_specs = P(("seq", "mp"), None)
    return jax.shard_map(
        on_device, mesh=mesh, in_specs=in_specs, out_specs=out_specs, check_vma=False
    )
```

profile of v0, /device:TPU:8, one launch (start us, length us, event | category | flops | bytes accessed | tf_op | source)
XLA Modules:
  0.0 416.1 jit_solution(15715362171986909808)
XLA Ops:
  6.5 0.7 all-gather.4.cloned.1.call-update
  7.3 0.7 all-gather.6.cloned.1.call-update
  8.7 48.6 %all-gather = s32[64,1,4]{2,1,0:T(1,128)S(1)} all-gather(s32[1,1,4]{2,1,0:T(1,128)S(1)} %fusion.71), channel_id=1, replica_groups=mesh['seq'=64,'mp'=8] {'seq'}, dimensions={0}, use_global_device_ids=true | all-gather | bytes 1040 | tf_op jit(solution)/shard_map/all_gather | solution.py:14
  57.3 1.3 dynamic-slice
  58.7 0.8 dynamic-update-slice
  59.5 23.7 %all-reduce = s32[64]{0:T(128)S(1)} all-reduce(s32[64]{0:T(128)S(1)} %dynamic-update-slice), channel_id=1, replica_groups=mesh['seq'=64,'mp'=8] {'seq'}, use_global_device_ids=true, to_apply=%add | all-reduce | flops 64 | bytes 512
  83.2 130.9 %while.15 = (s32[]{:T(128)}, s32[4]{0:T(128)S(1)}, s32[]{:T(128)}, s32[64]{0:T(128)S(1)}, s32[64,4]{1,0:T(8,128)S(1)}, /*index=5*/s32[]{:T(128)}, s32[]{:T(128)}, s32[]{:T(128)}) while((s32[]{:T(128)}, s32[4]{0:T(128)S(1)}, s32[]{:T(128)}, s32[64]{0:T(128)S(1)}, s32[64,4]{1,0:T(8,128)S(1)}, /*index=5*/s32[]{:T(128)}, ...), condition=%wide.region_7.8_spmd.clone.clone, body=%wide.region_5.7_spmd.clone.clone.sunk | while | flops 69 | bytes 301 | solution.py:23
  85.3 0.6 dynamic_slice.22
  87.4 0.6 dynamic_slice.22
  91.5 0.6 dynamic_slice.22
  95.7 0.6 dynamic_slice.22
  97.8 0.6 dynamic_slice.22
  101.9 0.6 dynamic_slice.22
  106.1 0.6 dynamic_slice.22
  108.1 0.6 dynamic_slice.22
  110.2 0.6 dynamic_slice.22
  112.3 0.6 dynamic_slice.22
  116.5 0.6 dynamic_slice.22
  120.6 0.6 dynamic_slice.22
  122.7 0.6 dynamic_slice.22
  124.8 0.6 dynamic_slice.22
  126.8 0.6 dynamic_slice.22
  128.9 0.6 dynamic_slice.22
  133.1 0.6 dynamic_slice.22
  137.2 0.6 dynamic_slice.22
  139.3 0.6 dynamic_slice.22
  143.5 0.6 dynamic_slice.22
  147.6 0.6 dynamic_slice.22
  149.7 0.6 dynamic_slice.22
  151.8 0.6 dynamic_slice.22
  153.9 0.6 dynamic_slice.22
  155.9 0.6 dynamic_slice.22
  158.0 0.6 dynamic_slice.22
  162.2 0.6 dynamic_slice.22
  214.1 0.7 convert_element_type.71
  214.8 0.7 convert_element_type.76
  215.5 0.7 reduce_sum.131
  216.2 0.7 fusion.102
  218.1 0.8 slice_reduce_fusion
  219.6 0.8 slice_reduce_fusion.1
  221.0 0.7 iota_compare_fusion.6
  221.7 0.7 iota_compare_fusion.3
  223.6 2.1 fusion.2
  225.8 13.4 %convolution_convert_fusion = bf16[512,2048]{1,0:T(8,128)(2,1)} fusion(bf16[896,2048]{0,1:T(8,128)(2,1)} %all-gather.6.cloned.1.call-done, bf16[2048,896]{1,0:T(8,128)(2,1)} %all-gather.4.cloned.1.call-done, bf16[512,2048]{1,0:T(8,128)(2,1)} %param.13, f32[2048]{0:T(1024)S(1)} %convert_element_type.71, f32[512]{0:T(512)S(1)} %add_rsqrt_fusion.3), kind=kOutput, calls=%fused_computation.15 | convolution fusion | flops 3793158144 | bytes 11544576 | tf_op jit(solution)/shard_map/dot_general | solution.py:64
  239.3 0.8 copy-done.4
  240.1 0.8 multiply_reduce_fusion.1
  241.1 70.2 %all-reduce.3.cloned.1.call-done = bf16[512,2048]{1,0:T(8,128)(2,1)} async-done(((bf16[512,2048]{1,0:T(8,128)(2,1)}), bf16[512,2048]{1,0:T(8,128)(2,1)}) %all-reduce.3.cloned.1.call-update) | async-done | bytes 2097168 | tf_op jit(solution)/shard_map/psum | solution.py:69
  311.2 3.1 multiply_reduce_fusion
  314.7 1.2 fusion.5
  316.0 3.7 collective-permute-start
  319.7 1.1 fusion.106
  321.2 5.2 %collective-permute-done = bf16[512,256]{0,1:T(8,128)(2,1)S(1)} collective-permute-done((bf16[512,256]{0,1:T(8,128)(2,1)S(1)}, bf16[512,256]{0,1:T(8,128)(2,1)S(1)}, u32[]{:S(2)}, u32[]{:S(2)}) %collective-permute-start) | collective-permute-done | bytes 262176 | tf_op jit(solution)/shard_map/ppermute | solution.py:29
  326.4 1.0 fusion.107
  327.4 1.9 collective-permute-start.1
  329.7 8.1 %collective-permute-done.1 = bf16[512,256]{0,1:T(8,128)(2,1)S(1)} collective-permute-done((bf16[512,256]{0,1:T(8,128)(2,1)S(1)}, bf16[512,256]{0,1:T(8,128)(2,1)S(1)}, u32[]{:S(2)}, u32[]{:S(2)}) %collective-permute-start.1) | collective-permute-done | bytes 262176 | tf_op jit(solution)/shard_map/ppermute | solution.py:29
  337.8 1.0 fusion.105
  338.8 1.9 collective-permute-start.2
  341.1 8.1 %collective-permute-done.2 = bf16[512,256]{0,1:T(8,128)(2,1)S(1)} collective-permute-done((bf16[512,256]{0,1:T(8,128)(2,1)S(1)}, bf16[512,256]{0,1:T(8,128)(2,1)S(1)}, u32[]{:S(2)}, u32[]{:S(2)}) %collective-permute-start.2) | collective-permute-done | bytes 262176 | tf_op jit(solution)/shard_map/ppermute | solution.py:29
  349.2 1.0 fusion.104
  350.3 1.9 collective-permute-start.3
  352.5 8.1 %collective-permute-done.3 = bf16[512,256]{0,1:T(8,128)(2,1)S(1)} collective-permute-done((bf16[512,256]{0,1:T(8,128)(2,1)S(1)}, bf16[512,256]{0,1:T(8,128)(2,1)S(1)}, u32[]{:S(2)}, u32[]{:S(2)}) %collective-permute-start.3) | collective-permute-done | bytes 262176 | tf_op jit(solution)/shard_map/ppermute | solution.py:29
  360.7 2.0 fusion.103
  362.7 3.5 convolution_convert_fusion.1
  366.3 43.3 %reduce-scatter.2.cloned.1.call-done = bf16[128,1024]{1,0:T(8,128)(2,1)} async-done(((bf16[1024,1024]{1,0:T(8,128)(2,1)}), bf16[128,1024]{1,0:T(8,128)(2,1)}) %reduce-scatter.2.cloned.1.call-update) | async-done | bytes 262160 | tf_op jit(solution)/shard_map/reduce_scatter | solution.py:148
  (270 shorter events, 76.2 us)
Async XLA Ops:
  6.5 232.7 %copy-start = (bf16[1024,1024]{1,0:T(8,128)(2,1)S(1)}, bf16[1024,1024]{1,0:T(8,128)(2,1)}, u32[]{:S(2)}) copy-start(bf16[1024,1024]{1,0:T(8,128)(2,1)} %param.19) | copy-start | bytes 6291460
  6.5 219.2 %all-gather.4.cloned.1.call-start = ((), (), s32[]{:S(2)}) async-start(), calls=%async_computation.1 | async-start | bytes 3727360 | tf_op jit(solution)/shard_map/all_gather | solution.py:59
  7.3 218.5 %all-gather.6.cloned.1.call-start = ((), (), s32[]{:S(2)}) async-start(), calls=%async_computation.2 | async-start | bytes 3727360 | tf_op jit(solution)/shard_map/all_gather | solution.py:66
  8.0 303.2 %all-reduce.3.cloned.1.call-start = ((), (), s32[]{:S(2)}) async-start(), calls=%async_computation.3 | async-start | bytes 4194304 | tf_op jit(solution)/shard_map/psum | solution.py:69
  239.2 0.9 copy-start.4
  239.2 1.8 copy-start.5
  239.2 170.4 %reduce-scatter.2.cloned.1.call-start = ((), (), s32[]{:S(2)}) async-start(), calls=%async_computation.4 | async-start | bytes 2359296 | tf_op jit(solution)/shard_map/reduce_scatter | solution.py:148
  240.1 74.2 %copy-start.6 = (bf16[2048,256]{1,0:T(8,128)(2,1)S(1)}, bf16[2048,256]{1,0:T(8,128)(2,1)}, u32[]{:S(2)}) copy-start(bf16[2048,256]{1,0:T(8,128)(2,1)} %param.18) | copy-start | bytes 3145732
  311.2 3.1 copy-start.1
  311.2 3.5 copy-start.2
  316.0 10.4 %collective-permute-start = (bf16[512,256]{0,1:T(8,128)(2,1)S(1)}, bf16[512,256]{0,1:T(8,128)(2,1)S(1)}, u32[]{:S(2)}, u32[]{:S(2)}) collective-permute-start(bf16[512,256]{0,1:T(8,128)(2,1)S(1)} %bitcast.99), channel_id=1, source_target_pairs={{0,8},{8,16},{16,24},{24,32},{32,40},{40,48},{48,56},{56,64},{64,7... | collective-permute-start | bytes 786440 | tf_op jit(solution)/shard_map/ppermute | solution.py:29
  327.4 10.4 %collective-permute-start.1 = (bf16[512,256]{0,1:T(8,128)(2,1)S(1)}, bf16[512,256]{0,1:T(8,128)(2,1)S(1)}, u32[]{:S(2)}, u32[]{:S(2)}) collective-permute-start(bf16[512,256]{0,1:T(8,128)(2,1)S(1)} %collective-permute-done), channel_id=1, source_target_pairs={{0,8},{8,16},{16,24},{24,32},{32,40},{40,48},{48,56},{56,64},{64,7... | collective-permute-start | bytes 786440 | tf_op jit(solution)/shard_map/ppermute | solution.py:29
  338.8 10.4 %collective-permute-start.2 = (bf16[512,256]{0,1:T(8,128)(2,1)S(1)}, bf16[512,256]{0,1:T(8,128)(2,1)S(1)}, u32[]{:S(2)}, u32[]{:S(2)}) collective-permute-start(bf16[512,256]{0,1:T(8,128)(2,1)S(1)} %collective-permute-done.1), channel_id=1, source_target_pairs={{0,8},{8,16},{16,24},{24,32},{32,40},{40,48},{48,56},{56,64},{64,7... | collective-permute-start | bytes 786440 | tf_op jit(solution)/shard_map/ppermute | solution.py:29
  350.3 10.4 %collective-permute-start.3 = (bf16[512,256]{0,1:T(8,128)(2,1)S(1)}, bf16[512,256]{0,1:T(8,128)(2,1)S(1)}, u32[]{:S(2)}, u32[]{:S(2)}) collective-permute-start(bf16[512,256]{0,1:T(8,128)(2,1)S(1)} %collective-permute-done.2), channel_id=1, source_target_pairs={{0,8},{8,16},{16,24},{24,32},{32,40},{40,48},{48,56},{56,64},{64,7... | collective-permute-start | bytes 786440 | tf_op jit(solution)/shard_map/ppermute | solution.py:29
  360.7 2.0 copy-start.3
Sparse Core Ops, SparseCore 0:
  10.4 90.1 all-gather.3
  103.6 82.9 all-gather.5
  239.3 71.8 all-reduce.2
  366.4 43.1 reduce-scatter.1
where the time goes:
time: 418 us; the launch traced here: 416 us
  waiting for transfers between devices  145 us (35%)
  blocking collectives  72.3 us (17%)
  other arithmetic  62.3 us (15%)
  local copies, waits for them, and re-layouts  43 us (10%)
  loops' own time  41.1 us (10%)
  matrix products  26.5 us (6%)
  between operations  16.7 us (4%)
  starting transfers between devices  9.62 us (2%)
    psum x1, waiting for transfers between devices, on_device(): lax.psum(partial_value.astype(jnp.bfloat16), 'mp').astype(jnp.float32)  70.2 us
    all_gather x1, blocking collectives, entering(): pieces = jax.tree.map(lambda part: lax.all_gather(part, axis), value)  48.6 us
    reduce_scatter x1, waiting for transfers between devices, on_device(): lax.psum_scatter(jnp.dot(attended, out_weight, preferred_element_type=jnp...  43.3 us
    another operation x1, loops' own time, entering(): return lax.fori_loop(0, count - 1, step, so_far)  41.1 us
    dynamic_slice x63, local copies, waits for them, and re-layouts, step(): longer = join(so_far, jax.tree.map(lambda part: part[position], pieces))  39 us
    while x63, other arithmetic  38.5 us
    ppermute x4, waiting for transfers between devices, from_behind(): lax.ppermute(value, axis, [(source, source + steps) for source in range(l...  29.6 us
    unnamed x1, blocking collectives  23.7 us
  transfers between devices with their start and end apart: 8, of which 6 were waited for; matrix products, arithmetic and copies ran while one was open for 25% of the time, Pallas kernels for 0%

commit v1 on v0

v1 whole, which is shorter than its diff:
```python
import functools
import math

import jax
import jax.numpy as jnp
from jax import lax
from jax.sharding import PartitionSpec as P
from jax.experimental import pallas as pl
from jax.experimental.pallas import tpu as pltpu

HS = 128
WIN = 1024


def scale_rows(values, gain):
    return values * lax.rsqrt(jnp.mean(values * values, axis=-1, keepdims=True) + 1e-05) * gain


def unit_rows(values):
    return values * lax.rsqrt(jnp.mean(values * values, axis=-1, keepdims=True) + 1e-06)


def from_behind(value, steps):
    count = lax.axis_size("seq")
    return lax.ppermute(value, "seq", [(source, source + steps) for source in range(count - steps)])


def spread(value, groups=None):
    size = lax.axis_size("mp") if groups is None else len(groups[0])
    copies = jnp.broadcast_to(value[None], (size,) + value.shape)
    return lax.all_to_all(copies, "mp", 0, 0, axis_index_groups=groups)


def feed_forward_kernel(n_early, parity, rows, gain, weights, *rest):
    out, up, down, normed, hidden, sems = rest[n_early:]
    features, width = up.shape
    step = 256
    starts = list(range(0, width, step))
    copies = []
    for index, start in enumerate(starts):
        size = min(step, width - start)
        copies.append(
            pltpu.make_async_copy(
                weights.at[:, pl.ds(start, size)], up.at[:, pl.ds(start, size)], sems.at[index]
            )
        )
    copies.append(
        pltpu.make_async_copy(weights.at[:, pl.ds(width, width)], down, sems.at[len(starts)])
    )
    for copy in copies:
        copy.start()
    values = rows[...].reshape(normed.shape).astype(jnp.float32)
    normed[...] = scale_rows(values, gain[...].astype(jnp.float32)).astype(jnp.bfloat16)
    for index, start in enumerate(starts):
        size = min(step, width - start)
        copies[index].wait()
        preact = jnp.dot(
            normed[...], up[:, pl.ds(start, size)], preferred_element_type=jnp.float32
        )
        activated = 0.5 * preact * (1.0 + lax.erf(preact * math.sqrt(0.5)))
        hidden[:, pl.ds(start, size)] = activated.astype(jnp.bfloat16)
    copies[-1].wait()

    @pl.loop(0, features // 512)
    def _(tile):
        span = pl.ds(pl.multiple_of(tile * 512, 512), 512)
        out[:, span] = lax.dot_general(
            hidden[...],
            down[span, :],
            (((1,), (1,)), ((), ())),
            preferred_element_type=jnp.float32,
        ).astype(out.dtype)


def feed_forward(parity, by_core, gain, weights, early):
    chips, _, own, features = by_core.shape
    rows, width = chips * own, weights.shape[1] // 2
    anywhere = pl.BlockSpec(memory_space=pl.ANY)
    counts = [pl.BlockSpec(memory_space=pltpu.SMEM)] if early else []
    return pl.pallas_call(
        functools.partial(feed_forward_kernel, len(early)),
        out_shape=jax.ShapeDtypeStruct((rows, features), jnp.bfloat16),
        grid_spec=pltpu.PrefetchScalarGridSpec(
            num_scalar_prefetch=1,
            grid=(1,),
            in_specs=[
                pl.BlockSpec((chips, 1, own, features), lambda i, p: (0, p[0], 0, 0)),
                pl.BlockSpec((1, features), lambda i, p: (0, 0)),
                anywhere,
            ]
            + counts
            + [anywhere] * (len(early) - len(counts)),
            out_specs=pl.BlockSpec((rows, features), lambda i, p: (0, 0)),
            scratch_shapes=[
                pltpu.VMEM((features, width), jnp.bfloat16),
                pltpu.VMEM((features, width), jnp.bfloat16),
                pltpu.VMEM((rows, features), jnp.bfloat16),
                pltpu.VMEM((rows, width), jnp.bfloat16),
                pltpu.SemaphoreType.DMA((pl.cdiv(width, 256) + 1,)),
            ],
        ),
        cost_estimate=pl.CostEstimate(
            flops=4 * rows * features * width,
            bytes_accessed=4 * features * (rows + width),
            transcendentals=rows * width,
        ),
        name="feed_forward",
    )(parity.astype(jnp.int32).reshape(1), by_core, gain.reshape(1, features), weights, *early)


def on_device(
    patch_states,
    mlp_gain,
    up_weight,
    down_weight,
    kv_gain,
    kv_weight,
    byte_states,
    query_weight,
    out_weight,
    patch_counts,
    byte_patch,
):
    rows, features = patch_states.shape
    n_mp = lax.axis_size("mp")
    me = lax.axis_index("mp")
    core = lax.rem(me, 2)
    chips = n_mp // 2
    own = rows // n_mp
    same_core = [list(range(parity, n_mp, 2)) for parity in range(2)]
    core_swap = [(source, source ^ 1) for source in range(n_mp)]

    joined = jnp.concatenate([up_weight, down_weight.T], axis=1)
    with jax.named_scope("gather_w"):
        weights_all = lax.all_gather(joined, "seq", axis=0, tiled=True)

    with jax.named_scope("spread_kv"):
        kv_same = spread(kv_weight, same_core)
    with jax.named_scope("swap_kv"):
        kv_other = lax.ppermute(kv_same, "mp", core_swap)
    with jax.named_scope("spread_out"):
        out_all = spread(out_weight)

    depth_back = (WIN + rows // 2 - 2) // (rows // 2)
    own_count = patch_counts[0]
    with jax.named_scope("counts"):
        prior = [from_behind(patch_counts, k) for k in range(1, depth_back + 1)]

    with jax.named_scope("queries"):
        queries = unit_rows(
            jnp.dot(byte_states, query_weight, preferred_element_type=jnp.float32)
        ).astype(jnp.bfloat16)

    by_core = patch_states.reshape(chips, 2, own, features)
    early = (jnp.concatenate(prior), kv_same, kv_other, out_all, queries)
    theirs = feed_forward(1 - core, by_core, mlp_gain, weights_all, early)
    arrived = lax.ppermute(theirs, "mp", core_swap)
    mine = feed_forward(core, by_core, mlp_gain, weights_all, ())
    paired = (mine.astype(jnp.float32) + arrived.astype(jnp.float32)).astype(jnp.bfloat16)
    terms = lax.all_to_all(
        paired.reshape(chips, own, features), "mp", 0, 0, axis_index_groups=same_core
    )
    mixed = jnp.sum(terms.astype(jnp.float32), axis=0)

    mine_rows = lax.dynamic_slice_in_dim(patch_states, me * own, own, 0)
    kv_in = scale_rows(mine_rows.astype(jnp.float32) + mixed, kv_gain.astype(jnp.float32)).astype(
        jnp.bfloat16
    )

    def project(stack):
        made = jnp.einsum("rd,xde->xre", kv_in, stack, preferred_element_type=jnp.float32)
        keys = unit_rows(made[..., :HS])
        return jnp.concatenate([keys, made[..., HS:]], axis=-1).astype(jnp.bfloat16)

    same, other = project(kv_same), project(kv_other)
    even = jnp.where(core == 0, same, other)
    odd = jnp.where(core == 0, other, same)
    by_head = jnp.stack([even, odd], axis=1).reshape(n_mp, own, 2 * HS)
    kv_pack = lax.all_to_all(by_head, "mp", 0, 0).reshape(rows, 2 * HS)

    tail = rows // 2
    blocks = [(kv_pack, jnp.zeros((), jnp.int32), own_count, jnp.zeros((), jnp.int32))]
    first = jnp.zeros((), jnp.int32)
    sent_tail = lax.dynamic_slice_in_dim(kv_pack, own_count - tail, tail, 0)
    for k in range(1, depth_back + 1):
        first = first - prior[k - 1][0]
        if k < depth_back:
            blocks.append((from_behind(kv_pack, k), first, prior[k - 1][0], jnp.zeros((), jnp.int32)))
        else:
            blocks.append((from_behind(sent_tail, k), first, prior[k - 1][0], prior[k - 1][0] - tail))

    score_scale = 2.0 / math.sqrt(HS)
    numerator = denominator = 0.0
    for kv_block, first_id, live, start in blocks:
        positions = start + jnp.arange(kv_block.shape[0], dtype=jnp.int32)
        key_ids = first_id + positions
        usable = (
            ((positions >= 0) & (positions < live))[None, :]
            & (key_ids[None, :] <= byte_patch[:, None])
            & (key_ids[None, :] > byte_patch[:, None] - WIN)
        )
        scores = (
            lax.dot_general(
                queries,
                kv_block[:, :HS],
                (((1,), (1,)), ((), ())),
                preferred_element_type=jnp.float32,
            )
            * score_scale
        )
        weights = jnp.where(usable, jnp.exp(scores), 0.0)
        numerator = numerator + jnp.dot(
            weights.astype(jnp.bfloat16), kv_block[:, HS:], preferred_element_type=jnp.float32
        )
        denominator = denominator + jnp.sum(weights, axis=-1)
    attended = (numerator / denominator[:, None]).astype(jnp.bfloat16)

    bytes_own = attended.shape[0] // n_mp
    gathered = lax.all_to_all(attended.reshape(n_mp, bytes_own, HS), "mp", 0, 0)
    return jnp.einsum(
        "hrd,hdo->ro", gathered, out_all, preferred_element_type=jnp.float32
    ).astype(jnp.bfloat16)


def solution(mesh):
    in_specs = (
        P("seq", None),
        P(),
        P("seq", "mp"),
        P("mp", "seq"),
        P(),
        P(None, "mp"),
        P("seq", None),
        P(None, "mp"),
        P("mp", None),
        P("seq"),
        P("seq"),
    )
    return jax.shard_map(
        on_device,
        mesh=mesh,
        in_specs=in_specs,
        out_specs=P(("seq", "mp"), None),
        check_vma=False,
    )
```

time: 418 us -> 245 us (0.59)
  the two profiles are of different devices: /device:TPU:8 before, /device:TPU:416 now
where the time goes in v1:
time: 245 us; the launch traced here: 244 us
  waiting for transfers between devices  64.3 us (26%)
  blocking collectives  63 us (26%)
  starting transfers between devices  47.6 us (19%)
  between operations  17.7 us (7%)
  matrix products  16.5 us (7%)
  Pallas kernels  16.4 us (7%)
  other arithmetic  13.7 us (6%)
  local copies, waits for them, and re-layouts  4.71 us (2%)
    all_to_all x1, blocking collectives, spread(): return lax.all_to_all(copies, 'mp', 0, 0, axis_index_groups=groups)  53.1 us
    ppermute x8, waiting for transfers between devices, from_behind(): lax.ppermute(value, 'seq', [(source, source + steps) for source in range(...  39.3 us
    ppermute x8, starting transfers between devices, from_behind(): lax.ppermute(value, 'seq', [(source, source + steps) for source in range(...  31.7 us
    pallas_call x2, Pallas kernels, feed_forward(): pl.pallas_call(functools.partial(feed_forward_kernel, len(early)), out_sh...  16.4 us
    all_to_all x1, waiting for transfers between devices, on_device(): lax.all_to_all(paired.reshape(chips, own, features), 'mp', 0, 0, axis_ind...  10.6 us
    all_to_all x1, blocking collectives, on_device(): gathered = lax.all_to_all(attended.reshape(n_mp, bytes_own, HS), 'mp', 0, 0)  9.91 us
    all_to_all x1, waiting for transfers between devices, on_device(): kv_pack = lax.all_to_all(by_head, 'mp', 0, 0).reshape(rows, 2 * HS)  6.77 us
    dot_general x2, matrix products, project(): jnp.einsum('rd,xde->xre', kv_in, stack, preferred_element_type=jnp.float32)  5.99 us
  transfers between devices with their start and end apart: 14, of which 7 were waited for; matrix products, arithmetic and copies ran while one was open for 7% of the time, Pallas kernels for 3%

profile of v1, /device:TPU:416, one launch (start us, length us, event | category | flops | bytes accessed | tf_op | source)
XLA Modules:
  0.0 243.9 jit_solution(3950320372636777180)
XLA Ops:
  6.5 1.6 pad_maximum_fusion.3
  8.2 0.0 all-gather.2.cloned.1.call-update
  8.2 1.5 broadcast_in_dim.13
  9.7 0.0 copy-start.2
  9.7 53.1 %all_to_all.25.rest_1_ = bf16[4,2048,256]{2,1,0:T(8,128)(2,1)} all-to-all(bf16[4,2048,256]{2,1,0:T(8,128)(2,1)S(1)} %broadcast_in_dim.13), channel_id=1, replica_groups={{0,2,4,6},{1,3,5,7},{8,10,12,14},{9,11,13,15},{16,18,20,22},{17,19,21,2..., dimensions={0} | all-to-all | bytes 8388608 | tf_op jit(solution)/shard_map/spread_kv/all_to_all | solution.py:31
  62.9 1.9 collective-permute-start.4
  64.8 1.6 broadcast_in_dim.14
  66.4 4.5 %all-to-all-start.1 = ((bf16[8,128,1024]{2,1,0:T(8,128)(2,1)}), bf16[8,128,1024]{2,1,0:T(8,128)(2,1)}, u32[]{:S(2)}, u32[]{:S(2)}) async-start(bf16[8,128,1024]{2,1,0:T(8,128)(2,1)} %broadcast_in_dim.14), calls=%async_computation.1 | async-start | bytes 4194304 | tf_op jit(solution)/shard_map/spread_out/all_to_all | solution.py:31
  70.9 0.0 copy-start.4
  70.9 3.4 %collective-permute-start = (s32[1]{0:T(128)}, s32[1]{0:T(128)}, u32[]{:S(2)}, u32[]{:S(2)}) collective-permute-start(s32[1]{0:T(128)} %param.20), channel_id=1, source_target_pairs={{0,8},{8,16},{16,24},{24,32},{32,40},{40,48},{48,56},{56,64},{64,7... | collective-permute-start | bytes 20 | tf_op jit(solution)/shard_map/counts/ppermute | solution.py:25
  74.3 1.9 collective-permute-start.1
  76.2 5.2 %collective-permute-start.2 = (s32[1]{0:T(128)}, s32[1]{0:T(128)}, u32[]{:S(2)}, u32[]{:S(2)}) collective-permute-start(s32[1]{0:T(128)} %param.20), channel_id=1, source_target_pairs={{0,24},{8,32},{16,40},{24,48},{32,56},{40,64},{48,72},{56,80},{64,... | collective-permute-start | bytes 20 | tf_op jit(solution)/shard_map/counts/ppermute | solution.py:25
  81.4 4.7 %collective-permute-start.3 = (s32[1]{0:T(128)}, s32[1]{0:T(128)}, u32[]{:S(2)}, u32[]{:S(2)}) collective-permute-start(s32[1]{0:T(128)} %param.20), channel_id=1, source_target_pairs={{0,32},{8,40},{16,48},{24,56},{32,64},{40,72},{48,80},{56,88},{64,... | collective-permute-start | bytes 20 | tf_op jit(solution)/shard_map/counts/ppermute | solution.py:25
  86.1 0.8 multiply_reduce_fusion.1
  87.0 0.2 copy.13
  87.2 0.6 reshape.201.gain
  87.8 0.9 multiply_convert_fusion.1.rest_4_
  88.7 2.3 collective-permute-done.3
  91.0 3.2 %pad_add_fusion.rest_0_ = s32[4]{0:T(128)} fusion(s32[1]{0:T(128)} %collective-permute-done.3, s32[1]{0:T(128)} %collective-permute-done.2, s32[1]{0:T(128)} %collective-permute-done.1, s32[1]{0:T(128)} %collective-permute-done), kind=kLoop, calls=%fused_computation.78 | loop fusion | flops 12 | bytes 32 | tf_op jit(solution)/shard_map/concatenate | solution.py:155
  94.2 3.8 %all-to-all-done.1.rest_3_ = bf16[8,128,1024]{2,1,0:T(8,128)(2,1)} async-done(((bf16[8,128,1024]{2,1,0:T(8,128)(2,1)}), bf16[8,128,1024]{2,1,0:T(8,128)(2,1)}, u32[]{:S(2)}, u32[]{:S(2)}) %all-to-all-start.1) | async-done | bytes 2097184 | tf_op jit(solution)/shard_map/spread_out/all_to_all | solution.py:31
  98.1 3.7 %all-gather.2.cloned.1.call-done.weights = bf16[2048,1792]{1,0:T(8,128)(2,1)} async-done(((bf16[32,1792]{1,0:T(8,128)(2,1)}), bf16[2048,1792]{1,0:T(8,128)(2,1)}) %all-gather.2.cloned.1.call-update) | async-done | bytes 7340048 | tf_op jit(solution)/shard_map/gather_w/all_gather | solution.py:135
  101.7 8.2 %feed_forward.3 = bf16[256,2048]{1,0:T(8,128)(2,1)} custom-call(s32[1]{0:T(128)} %bitcast.4.parity, bf16[4,2,64,2048]{3,2,1,0:T(8,128)(2,1)} %bitcast.52, bf16[1,2048]{1,0:T(2,128)(2,1)} %reshape.201.gain, bf16[2048,1792]{1,0:T(8,128)(2,1)} %all-gather.2.cloned.1.call-done.weights, s32[4]{0:T(128)} %pad_add_fusion.rest_0_, ...), custom_call_target="tpu_custom_call" | custom-call | flops 1879048192 | bytes 9437184 | tf_op jit(solution)/shard_map/feed_forward/pallas_call | solution.py:80
  109.9 1.9 collective-permute-start.5
  112.5 8.2 %feed_forward.2 = bf16[256,2048]{1,0:T(8,128)(2,1)} custom-call(s32[1]{0:T(128)} %bitcast.1.parity, bf16[4,2,64,2048]{3,2,1,0:T(8,128)(2,1)} %bitcast.53, bf16[1,2048]{1,0:T(2,128)(2,1)} %reshape.201.gain, bf16[2048,1792]{1,0:T(8,128)(2,1)} %all-gather.2.cloned.1.call-done.weights), custom_call_target="tpu_custom_call" | custom-call | flops 1879048192 | bytes 9437184 | tf_op jit(solution)/shard_map/feed_forward/pallas_call | solution.py:80
  120.7 0.0 copy-start.5
  120.7 0.0 copy-start.6
  120.7 2.6 %add_convert_fusion = bf16[256,2048]{1,0:T(8,128)(2,1)} fusion(bf16[256,2048]{1,0:T(8,128)(2,1)S(1)} %collective-permute-done.5, bf16[256,2048]{1,0:T(8,128)(2,1)} %feed_forward.2), kind=kLoop, calls=%fused_computation.5 | loop fusion | flops 2097152 | bytes 3145728 | tf_op jit(solution)/shard_map/convert_element_type | solution.py:159
  123.3 4.2 %all-to-all-start.2 = ((bf16[4,64,2048]{2,1,0:T(8,128)(2,1)}), bf16[4,64,2048]{2,1,0:T(8,128)(2,1)S(1)}, u32[]{:S(2)}, u32[]{:S(2)}) async-start(bf16[4,64,2048]{2,1,0:T(8,128)(2,1)} %bitcast.5), calls=%async_computation.2 | async-start | bytes 2097152 | tf_op jit(solution)/shard_map/all_to_all | solution.py:160
  130.8 0.6 iota_compare_fusion.3
  131.3 0.6 iota_compare_fusion.4
  132.0 0.7 iota_compare_fusion.2
  132.7 10.6 %all-to-all-done.2 = bf16[4,64,2048]{2,1,0:T(8,128)(2,1)S(1)} async-done(((bf16[4,64,2048]{2,1,0:T(8,128)(2,1)}), bf16[4,64,2048]{2,1,0:T(8,128)(2,1)S(1)}, u32[]{:S(2)}, u32[]{:S(2)}) %all-to-all-start.2) | async-done | bytes 1048608 | tf_op jit(solution)/shard_map/all_to_all | solution.py:160
  143.3 0.2 convert_reduce_fusion
  143.5 1.1 multiply_reduce_fusion
  144.6 1.1 fusion.17
  145.7 3.0 %convolution_bitcast_fusion.1 = f32[4,64,256]{2,1,0:T(8,128)S(1)} fusion(bf16[64,2048,1]{1,0,2:T(8,128)(2,1)S(1)} %fusion.17, bf16[4,2048,256]{2,1,0:T(8,128)(2,1)} %collective-permute-done.4.rest_2_), kind=kOutput, calls=%fused_computation.21 | convolution fusion | flops 268435456 | bytes 4718592 | tf_op jit(solution)/shard_map/rd,xde->xre/dot_general | solution.py:171
  148.7 0.1 multiply_reduce_fusion.2
  148.8 3.0 %convolution_bitcast_fusion.2 = f32[4,64,256]{2,1,0:T(8,128)S(1)} fusion(bf16[64,2048,1]{1,0,2:T(8,128)(2,1)S(1)} %fusion.17, bf16[4,2048,256]{2,1,0:T(8,128)(2,1)} %all_to_all.25.rest_1_), kind=kOutput, calls=%fused_computation.22 | convolution fusion | flops 268435456 | bytes 4718592 | tf_op jit(solution)/shard_map/rd,xde->xre/dot_general | solution.py:171
  151.8 0.0 copy-start.1
  151.8 0.1 multiply_reduce_fusion.3
  152.0 0.1 fusion.26
  152.2 0.1 broadcast_select_fusion.1
  152.3 0.7 copy.14
  153.0 3.4 %all-to-all-start.3 = ((bf16[8,64,256]{2,1,0:T(8,128)(2,1)}), bf16[8,64,256]{2,1,0:T(8,128)(2,1)S(1)}, u32[]{:S(2)}, u32[]{:S(2)}) async-start(bf16[8,64,256]{2,1,0:T(8,128)(2,1)} %bitcast.13), calls=%async_computation.3 | async-start | bytes 524288 | tf_op jit(solution)/shard_map/all_to_all | solution.py:179
  156.4 0.6 compare_and_fusion
  157.1 6.8 %all-to-all-done.3 = bf16[8,64,256]{2,1,0:T(8,128)(2,1)S(1)} async-done(((bf16[8,64,256]{2,1,0:T(8,128)(2,1)}), bf16[8,64,256]{2,1,0:T(8,128)(2,1)S(1)}, u32[]{:S(2)}, u32[]{:S(2)}) %all-to-all-start.3) | async-done | bytes 262176 | tf_op jit(solution)/shard_map/all_to_all | solution.py:179
  163.8 4.1 %collective-permute-start.7 = (bf16[512,256]{1,0:T(8,128)(2,1)S(1)}, bf16[512,256]{1,0:T(8,128)(2,1)S(1)}, u32[]{:S(2)}, u32[]{:S(2)}) collective-permute-start(bf16[512,256]{1,0:T(8,128)(2,1)S(1)} %bitcast.54), channel_id=1, source_target_pairs={{0,16},{8,24},{16,32},{24,40},{32,48},{40,56},{48,64},{56,72},{64,... | collective-permute-start | bytes 786440 | tf_op jit(solution)/shard_map/ppermute | solution.py:25
  167.9 1.9 collective-permute-start.6
  169.8 6.0 %collective-permute-start.8 = (bf16[512,256]{1,0:T(8,128)(2,1)S(1)}, bf16[512,256]{1,0:T(8,128)(2,1)S(1)}, u32[]{:S(2)}, u32[]{:S(2)}) collective-permute-start(bf16[512,256]{1,0:T(8,128)(2,1)S(1)} %bitcast.56), channel_id=1, source_target_pairs={{0,24},{8,32},{16,40},{24,48},{32,56},{40,64},{48,72},{56,80},{64,... | collective-permute-start | bytes 786440 | tf_op jit(solution)/shard_map/ppermute | solution.py:25
  175.8 4.5 %collective-permute-start.9 = (bf16[256,256]{1,0:T(8,128)(2,1)S(1)}, bf16[256,256]{1,0:T(8,128)(2,1)S(1)}, u32[]{:S(2)}, u32[]{:S(2)}) collective-permute-start(bf16[256,256]{1,0:T(8,128)(2,1)S(1)} %constant_dynamic-slice_fusion), channel_id=1, source_target_pairs={{0,32},{8,40},{16,48},{24,56},{32,64},{40,72},{48,80},{56,88},{64,... | collective-permute-start | bytes 393224 | tf_op jit(solution)/shard_map/ppermute | solution.py:25
  180.4 1.1 fusion.36
  181.5 0.5 fusion.13
  182.0 28.1 %collective-permute-done.9 = bf16[256,256]{1,0:T(8,128)(2,1)S(1)} collective-permute-done((bf16[256,256]{1,0:T(8,128)(2,1)S(1)}, bf16[256,256]{1,0:T(8,128)(2,1)S(1)}, u32[]{:S(2)}, u32[]{:S(2)}) %collective-permute-start.9) | collective-permute-done | bytes 131104 | tf_op jit(solution)/shard_map/ppermute | solution.py:25
  210.1 0.6 fusion.33
  210.6 0.3 fusion.15
  211.0 1.0 fusion.35
  212.0 8.9 %collective-permute-done.6 = bf16[512,256]{1,0:T(8,128)(2,1)S(1)} collective-permute-done((bf16[512,256]{1,0:T(8,128)(2,1)S(1)}, bf16[512,256]{1,0:T(8,128)(2,1)S(1)}, u32[]{:S(2)}, u32[]{:S(2)}) %collective-permute-start.6) | collective-permute-done | bytes 262176 | tf_op jit(solution)/shard_map/ppermute | solution.py:25
  220.9 1.0 fusion.37
  221.9 1.0 fusion.34
  222.9 0.5 fusion.9
  223.4 0.5 convolution_add_fusion.1
  223.9 0.5 fusion.8
  224.4 9.9 %all_to_all.26 = bf16[8,128,128]{2,1,0:T(8,128)(2,1)S(1)} all-to-all(bf16[8,128,128]{2,1,0:T(8,128)(2,1)S(1)} %bitcast.60), channel_id=1, replica_groups=mesh['seq'=64,'mp'=8] {'mp'}, dimensions={0} | all-to-all | bytes 524288 | tf_op jit(solution)/shard_map/all_to_all | solution.py:219
  234.3 2.7 %fusion.7 = bf16[128,1024]{1,0:T(8,128)(2,1)} fusion(bf16[8,128,128]{2,1,0:T(8,128)(2,1)S(1)} %all_to_all.26, bf16[8,128,1024]{2,1,0:T(8,128)(2,1)} %all-to-all-done.1.rest_3_), kind=kOutput, calls=%fused_computation.19 | convolution fusion | flops 268566528 | bytes 2621440 | tf_op jit(solution)/shard_map/hrd,hdo->ro/dot_general | solution.py:220
  (32 shorter events, 0.2 us)
Async XLA Ops:
  6.5 79.6 %copy-start = (bf16[1024,1024]{1,0:T(8,128)(2,1)S(1)}, bf16[1024,1024]{1,0:T(8,128)(2,1)}, u32[]{:S(2)}) copy-start(bf16[1024,1024]{1,0:T(8,128)(2,1)} %param.17) | copy-start | bytes 6291460
  6.5 95.2 %all-gather.2.cloned.1.call-start = ((), (), s32[]{:S(2)}) async-start(), calls=%async_computation.5 | async-start | bytes 7454720 | tf_op jit(solution)/shard_map/gather_w/all_gather | solution.py:135
  9.7 55.1 %copy-start.2 = (bf16[128,1024]{1,0:T(8,128)(2,1)S(1)}, bf16[128,1024]{1,0:T(8,128)(2,1)}, u32[]{:S(2)}) copy-start(bf16[128,1024]{1,0:T(8,128)(2,1)} %param.19) | copy-start | bytes 786436
  62.9 35.2 %collective-permute-start.4 = (bf16[4,2048,256]{2,1,0:T(8,128)(2,1)}, bf16[4,2048,256]{2,1,0:T(8,128)(2,1)}, u32[]{:S(2)}, u32[]{:S(2)}) collective-permute-start(bf16[4,2048,256]{2,1,0:T(8,128)(2,1)} %all_to_all.25.rest_1_), channel_id=1, source_target_pairs={{0,1},{1,0},{2,3},{3,2},{4,5},{5,4},{6,7},{7,6},{8,9},{9,8},{10,11... | collective-permute-start | bytes 12582920 | tf_op jit(solution)/shard_map/swap_kv/ppermute | solution.py:140
  66.4 19.7 %copy-start.3 = (bf16[1024,128]{1,0:T(8,128)(2,1)S(1)}, bf16[1024,128]{1,0:T(8,128)(2,1)}, u32[]{:S(2)}) copy-start(bf16[1024,128]{1,0:T(8,128)(2,1)} %param.18) | copy-start | bytes 786436
  66.4 31.7 %all-to-all-start.1 = ((bf16[8,128,1024]{2,1,0:T(8,128)(2,1)}), bf16[8,128,1024]{2,1,0:T(8,128)(2,1)}, u32[]{:S(2)}, u32[]{:S(2)}) async-start(bf16[8,128,1024]{2,1,0:T(8,128)(2,1)} %broadcast_in_dim.14), calls=%async_computation.1 | async-start | bytes 4194304 | tf_op jit(solution)/shard_map/spread_out/all_to_all | solution.py:31
  70.9 16.3 %copy-start.4 = (bf16[2048]{0:T(1024)(128)(2,1)S(1)}, bf16[2048]{0:T(1024)(128)(2,1)}, u32[]{:S(2)}) copy-start(bf16[2048]{0:T(1024)(128)(2,1)} %param.12) | copy-start | bytes 12292
  70.9 17.8 %collective-permute-start = (s32[1]{0:T(128)}, s32[1]{0:T(128)}, u32[]{:S(2)}, u32[]{:S(2)}) collective-permute-start(s32[1]{0:T(128)} %param.20), channel_id=1, source_target_pairs={{0,8},{8,16},{16,24},{24,32},{32,40},{40,48},{48,56},{56,64},{64,7... | collective-permute-start | bytes 20 | tf_op jit(solution)/shard_map/counts/ppermute | solution.py:25
  74.3 14.4 %collective-permute-start.1 = (s32[1]{0:T(128)}, s32[1]{0:T(128)}, u32[]{:S(2)}, u32[]{:S(2)}) collective-permute-start(s32[1]{0:T(128)} %param.20), channel_id=1, source_target_pairs={{0,16},{8,24},{16,32},{24,40},{32,48},{40,56},{48,64},{56,72},{64,... | collective-permute-start | bytes 20 | tf_op jit(solution)/shard_map/counts/ppermute | solution.py:25
  76.2 12.5 %collective-permute-start.2 = (s32[1]{0:T(128)}, s32[1]{0:T(128)}, u32[]{:S(2)}, u32[]{:S(2)}) collective-permute-start(s32[1]{0:T(128)} %param.20), channel_id=1, source_target_pairs={{0,24},{8,32},{16,40},{24,48},{32,56},{40,64},{48,72},{56,80},{64,... | collective-permute-start | bytes 20 | tf_op jit(solution)/shard_map/counts/ppermute | solution.py:25
  81.4 9.6 %collective-permute-start.3 = (s32[1]{0:T(128)}, s32[1]{0:T(128)}, u32[]{:S(2)}, u32[]{:S(2)}) collective-permute-start(s32[1]{0:T(128)} %param.20), channel_id=1, source_target_pairs={{0,32},{8,40},{16,48},{24,56},{32,64},{40,72},{48,80},{56,88},{64,... | collective-permute-start | bytes 20 | tf_op jit(solution)/shard_map/counts/ppermute | solution.py:25
  109.9 10.8 %collective-permute-start.5 = (bf16[256,2048]{1,0:T(8,128)(2,1)}, bf16[256,2048]{1,0:T(8,128)(2,1)S(1)}, u32[]{:S(2)}, u32[]{:S(2)}) collective-permute-start(bf16[256,2048]{1,0:T(8,128)(2,1)} %feed_forward.3), channel_id=1, source_target_pairs={{0,1},{1,0},{2,3},{3,2},{4,5},{5,4},{6,7},{7,6},{8,9},{9,8},{10,11... | collective-permute-start | bytes 3145736 | tf_op jit(solution)/shard_map/ppermute | solution.py:157
  120.7 6.9 %copy-start.5 = (bf16[2048]{0:T(1024)(128)(2,1)S(1)}, bf16[2048]{0:T(1024)(128)(2,1)}, u32[]{:S(2)}) copy-start(bf16[2048]{0:T(1024)(128)(2,1)} %param.15) | copy-start | bytes 12292
  120.7 6.9 %copy-start.6 = (s32[1024]{0:T(1024)S(1)}, s32[1024]{0:T(1024)}, u32[]{:S(2)}) copy-start(s32[1024]{0:T(1024)} %param.21) | copy-start | bytes 12292
  123.3 20.0 %all-to-all-start.2 = ((bf16[4,64,2048]{2,1,0:T(8,128)(2,1)}), bf16[4,64,2048]{2,1,0:T(8,128)(2,1)S(1)}, u32[]{:S(2)}, u32[]{:S(2)}) async-start(bf16[4,64,2048]{2,1,0:T(8,128)(2,1)} %bitcast.5), calls=%async_computation.2 | async-start | bytes 2097152 | tf_op jit(solution)/shard_map/all_to_all | solution.py:160
  151.8 28.6 %copy-start.1 = (bf16[1024,128]{1,0:T(8,128)(2,1)S(1)}, bf16[1024,128]{1,0:T(8,128)(2,1)}, u32[]{:S(2)}) copy-start(bf16[1024,128]{1,0:T(8,128)(2,1)} %multiply_convert_fusion.1.rest_4_) | copy-start | bytes 786436
  153.0 10.8 %all-to-all-start.3 = ((bf16[8,64,256]{2,1,0:T(8,128)(2,1)}), bf16[8,64,256]{2,1,0:T(8,128)(2,1)S(1)}, u32[]{:S(2)}, u32[]{:S(2)}) async-start(bf16[8,64,256]{2,1,0:T(8,128)(2,1)} %bitcast.13), calls=%async_computation.3 | async-start | bytes 524288 | tf_op jit(solution)/shard_map/all_to_all | solution.py:179
  163.8 47.2 %collective-permute-start.7 = (bf16[512,256]{1,0:T(8,128)(2,1)S(1)}, bf16[512,256]{1,0:T(8,128)(2,1)S(1)}, u32[]{:S(2)}, u32[]{:S(2)}) collective-permute-start(bf16[512,256]{1,0:T(8,128)(2,1)S(1)} %bitcast.54), channel_id=1, source_target_pairs={{0,16},{8,24},{16,32},{24,40},{32,48},{40,56},{48,64},{56,72},{64,... | collective-permute-start | bytes 786440 | tf_op jit(solution)/shard_map/ppermute | solution.py:25
  167.9 53.0 %collective-permute-start.6 = (bf16[512,256]{1,0:T(8,128)(2,1)S(1)}, bf16[512,256]{1,0:T(8,128)(2,1)S(1)}, u32[]{:S(2)}, u32[]{:S(2)}) collective-permute-start(bf16[512,256]{1,0:T(8,128)(2,1)S(1)} %bitcast.55), channel_id=1, source_target_pairs={{0,8},{8,16},{16,24},{24,32},{32,40},{40,48},{48,56},{56,64},{64,7... | collective-permute-start | bytes 786440 | tf_op jit(solution)/shard_map/ppermute | solution.py:25
  169.8 52.0 %collective-permute-start.8 = (bf16[512,256]{1,0:T(8,128)(2,1)S(1)}, bf16[512,256]{1,0:T(8,128)(2,1)S(1)}, u32[]{:S(2)}, u32[]{:S(2)}) collective-permute-start(bf16[512,256]{1,0:T(8,128)(2,1)S(1)} %bitcast.56), channel_id=1, source_target_pairs={{0,24},{8,32},{16,40},{24,48},{32,56},{40,64},{48,72},{56,80},{64,... | collective-permute-start | bytes 786440 | tf_op jit(solution)/shard_map/ppermute | solution.py:25
  175.8 34.2 %collective-permute-start.9 = (bf16[256,256]{1,0:T(8,128)(2,1)S(1)}, bf16[256,256]{1,0:T(8,128)(2,1)S(1)}, u32[]{:S(2)}, u32[]{:S(2)}) collective-permute-start(bf16[256,256]{1,0:T(8,128)(2,1)S(1)} %constant_dynamic-slice_fusion), channel_id=1, source_target_pairs={{0,32},{8,40},{16,48},{24,56},{32,64},{40,72},{48,80},{56,88},{64,... | collective-permute-start | bytes 393224 | tf_op jit(solution)/shard_map/ppermute | solution.py:25
Sparse Core Ops, SparseCore 0:
  10.4 91.3 all-gather.1

commit v2 on v1

--- a/solution.py
+++ b/solution.py
@@ -178,24 +178,31 @@
     by_head = jnp.stack([even, odd], axis=1).reshape(n_mp, own, 2 * HS)
     kv_pack = lax.all_to_all(by_head, "mp", 0, 0).reshape(rows, 2 * HS)
 
-    tail = rows // 2
-    blocks = [(kv_pack, jnp.zeros((), jnp.int32), own_count, jnp.zeros((), jnp.int32))]
-    first = jnp.zeros((), jnp.int32)
-    sent_tail = lax.dynamic_slice_in_dim(kv_pack, own_count - tail, tail, 0)
-    for k in range(1, depth_back + 1):
-        first = first - prior[k - 1][0]
-        if k < depth_back:
-            blocks.append((from_behind(kv_pack, k), first, prior[k - 1][0], jnp.zeros((), jnp.int32)))
-        else:
-            blocks.append((from_behind(sent_tail, k), first, prior[k - 1][0], prior[k - 1][0] - tail))
+    c1, c2, c3, c4 = (count[0] for count in prior)
+    before2 = from_behind(kv_pack, 2)
+    before1 = from_behind(kv_pack, 1)
+    slot = jnp.arange(rows, dtype=jnp.int32)
+    source = slot[:, None] + (c1 - rows)
+    pick2 = (slot[None, :] == source + c2) & (source < 0)
+    pick1 = slot[None, :] == source
+    packed = jnp.dot(
+        jnp.concatenate([pick2, pick1], axis=1).astype(jnp.bfloat16),
+        jnp.concatenate([before2, before1], axis=0),
+        preferred_element_type=jnp.float32,
+    ).astype(jnp.bfloat16)
+    before34 = from_behind(packed, 2)
+    blocks = [
+        (kv_pack, slot, slot < own_count),
+        (before1, slot - c1, slot < c1),
+        (before2, slot - (c1 + c2), slot < c2),
+        (before34, slot - (c1 + c2 + rows), slot >= rows - (c3 + c4)),
+    ]
 
     score_scale = 2.0 / math.sqrt(HS)
     numerator = denominator = 0.0
-    for kv_block, first_id, live, start in blocks:
-        positions = start + jnp.arange(kv_block.shape[0], dtype=jnp.int32)
-        key_ids = first_id + positions
+    for kv_block, key_ids, live in blocks:
         usable = (
-            ((positions >= 0) & (positions < live))[None, :]
+            live[None, :]
             & (key_ids[None, :] <= byte_patch[:, None])
             & (key_ids[None, :] > byte_patch[:, None] - WIN)
         )

time: 245 us -> 234 us (0.955)
  the two profiles are of different devices: /device:TPU:416 before, /device:TPU:32 now
where the time goes in v2:
time: 234 us; the launch traced here: 233 us
  blocking collectives  63 us (27%)
  waiting for transfers between devices  55.4 us (24%)
  starting transfers between devices  45.6 us (19%)
  between operations  17.8 us (8%)
  Pallas kernels  16.4 us (7%)
  matrix products  16 us (7%)
  other arithmetic  14.1 us (6%)
  local copies, waits for them, and re-layouts  4.65 us (2%)
    all_to_all x1, blocking collectives, spread(): return lax.all_to_all(copies, 'mp', 0, 0, axis_index_groups=groups)  53.1 us
    ppermute x7, waiting for transfers between devices, from_behind(): lax.ppermute(value, 'seq', [(source, source + steps) for source in range(...  32.6 us
    ppermute x7, starting transfers between devices, from_behind(): lax.ppermute(value, 'seq', [(source, source + steps) for source in range(...  29.6 us
    pallas_call x2, Pallas kernels, feed_forward(): pl.pallas_call(functools.partial(feed_forward_kernel, len(early)), out_sh...  16.4 us
    all_to_all x1, waiting for transfers between devices, on_device(): lax.all_to_all(paired.reshape(chips, own, features), 'mp', 0, 0, axis_ind...  10.5 us
    all_to_all x1, blocking collectives, on_device(): gathered = lax.all_to_all(attended.reshape(n_mp, bytes_own, HS), 'mp', 0, 0)  9.91 us
    all_to_all x1, waiting for transfers between devices, on_device(): kv_pack = lax.all_to_all(by_head, 'mp', 0, 0).reshape(rows, 2 * HS)  7.04 us
    dot_general x2, matrix products, project(): jnp.einsum('rd,xde->xre', kv_in, stack, preferred_element_type=jnp.float32)  5.98 us
  transfers between devices with their start and end apart: 13, of which 7 were waited for; matrix products, arithmetic and copies ran while one was open for 7% of the time, Pallas kernels for 4%

profile of v2, /device:TPU:32, one launch (start us, length us, event | category | flops | bytes accessed | tf_op | source)
XLA Modules:
  0.0 232.9 jit_solution(15754018969775049686)
XLA Ops:
  6.5 1.6 pad_maximum_fusion.3
  8.2 0.0 all-gather.2.cloned.1.call-update
  8.2 1.5 broadcast_in_dim.10
  9.7 0.0 copy-start.2
  9.7 53.1 %all_to_all.25.rest_1_ = bf16[4,2048,256]{2,1,0:T(8,128)(2,1)} all-to-all(bf16[4,2048,256]{2,1,0:T(8,128)(2,1)S(1)} %broadcast_in_dim.10), channel_id=1, replica_groups={{0,2,4,6},{1,3,5,7},{8,10,12,14},{9,11,13,15},{16,18,20,22},{17,19,21,2..., dimensions={0} | all-to-all | bytes 8388608 | tf_op jit(solution)/shard_map/spread_kv/all_to_all | solution.py:31
  62.9 1.9 collective-permute-start.4
  64.8 1.6 broadcast_in_dim.11
  66.4 4.5 %all-to-all-start.1 = ((bf16[8,128,1024]{2,1,0:T(8,128)(2,1)}), bf16[8,128,1024]{2,1,0:T(8,128)(2,1)}, u32[]{:S(2)}, u32[]{:S(2)}) async-start(bf16[8,128,1024]{2,1,0:T(8,128)(2,1)} %broadcast_in_dim.11), calls=%async_computation.1 | async-start | bytes 4194304 | tf_op jit(solution)/shard_map/spread_out/all_to_all | solution.py:31
  70.9 0.0 copy-start.4
  70.9 4.3 %collective-permute-start = (s32[1]{0:T(128)}, s32[1]{0:T(128)}, u32[]{:S(2)}, u32[]{:S(2)}) collective-permute-start(s32[1]{0:T(128)} %param.20), channel_id=1, source_target_pairs={{0,8},{8,16},{16,24},{24,32},{32,40},{40,48},{48,56},{56,64},{64,7... | collective-permute-start | bytes 20 | tf_op jit(solution)/shard_map/counts/ppermute | solution.py:25
  75.2 6.1 %collective-permute-start.1 = (s32[1]{0:T(128)}, s32[1]{0:T(128)}, u32[]{:S(2)}, u32[]{:S(2)}) collective-permute-start(s32[1]{0:T(128)} %param.20), channel_id=1, source_target_pairs={{0,16},{8,24},{16,32},{24,40},{32,48},{40,56},{48,64},{56,72},{64,... | collective-permute-start | bytes 20 | tf_op jit(solution)/shard_map/counts/ppermute | solution.py:25
  81.3 7.3 %collective-permute-start.2 = (s32[1]{0:T(128)}, s32[1]{0:T(128)}, u32[]{:S(2)}, u32[]{:S(2)}) collective-permute-start(s32[1]{0:T(128)} %param.20), channel_id=1, source_target_pairs={{0,24},{8,32},{16,40},{24,48},{32,56},{40,64},{48,72},{56,80},{64,... | collective-permute-start | bytes 20 | tf_op jit(solution)/shard_map/counts/ppermute | solution.py:25
  88.6 2.8 %collective-permute-start.3 = (s32[1]{0:T(128)}, s32[1]{0:T(128)}, u32[]{:S(2)}, u32[]{:S(2)}) collective-permute-start(s32[1]{0:T(128)} %param.20), channel_id=1, source_target_pairs={{0,32},{8,40},{16,48},{24,56},{32,64},{40,72},{48,80},{56,88},{64,... | collective-permute-start | bytes 20 | tf_op jit(solution)/shard_map/counts/ppermute | solution.py:25
  91.5 0.8 multiply_reduce_fusion.1
  92.3 0.2 copy.13
  92.5 0.6 reshape.202.gain
  93.1 0.9 multiply_convert_fusion.1.rest_4_
  94.0 0.0 collective-permute-done
  94.0 0.0 collective-permute-done.1
  94.0 0.0 collective-permute-done.2
  94.0 6.3 %collective-permute-done.3 = s32[1]{0:T(128)} collective-permute-done((s32[1]{0:T(128)}, s32[1]{0:T(128)}, u32[]{:S(2)}, u32[]{:S(2)}) %collective-permute-start.3) | collective-permute-done | bytes 36 | tf_op jit(solution)/shard_map/counts/ppermute | solution.py:25
  100.3 3.2 %pad_add_fusion.rest_0_ = s32[4]{0:T(128)} fusion(s32[1]{0:T(128)} %collective-permute-done.3, s32[1]{0:T(128)} %collective-permute-done.2, s32[1]{0:T(128)} %collective-permute-done.1, s32[1]{0:T(128)} %collective-permute-done), kind=kLoop, calls=%fused_computation.81 | loop fusion | flops 12 | bytes 32 | tf_op jit(solution)/shard_map/concatenate | solution.py:155
  103.5 5.3 %all-gather.2.cloned.1.call-done.weights = bf16[2048,1792]{1,0:T(8,128)(2,1)} async-done(((bf16[32,1792]{1,0:T(8,128)(2,1)}), bf16[2048,1792]{1,0:T(8,128)(2,1)}) %all-gather.2.cloned.1.call-update) | async-done | bytes 7340048 | tf_op jit(solution)/shard_map/gather_w/all_gather | solution.py:135
  108.8 8.2 %feed_forward.3 = bf16[256,2048]{1,0:T(8,128)(2,1)} custom-call(s32[1]{0:T(128)} %bitcast.4.parity, bf16[4,2,64,2048]{3,2,1,0:T(8,128)(2,1)} %bitcast.47, bf16[1,2048]{1,0:T(2,128)(2,1)} %reshape.202.gain, bf16[2048,1792]{1,0:T(8,128)(2,1)} %all-gather.2.cloned.1.call-done.weights, s32[4]{0:T(128)} %pad_add_fusion.rest_0_, ...), custom_call_target="tpu_custom_call" | custom-call | flops 1879048192 | bytes 9437184 | tf_op jit(solution)/shard_map/feed_forward/pallas_call | solution.py:80
  117.0 1.9 collective-permute-start.5
  119.6 0.6 iota_compare_fusion.5
  120.2 8.2 %feed_forward.2 = bf16[256,2048]{1,0:T(8,128)(2,1)} custom-call(s32[1]{0:T(128)} %bitcast.1.parity, bf16[4,2,64,2048]{3,2,1,0:T(8,128)(2,1)} %bitcast.48, bf16[1,2048]{1,0:T(2,128)(2,1)} %reshape.202.gain, bf16[2048,1792]{1,0:T(8,128)(2,1)} %all-gather.2.cloned.1.call-done.weights), custom_call_target="tpu_custom_call" | custom-call | flops 1879048192 | bytes 9437184 | tf_op jit(solution)/shard_map/feed_forward/pallas_call | solution.py:80
  128.4 2.6 %add_convert_fusion = bf16[256,2048]{1,0:T(8,128)(2,1)} fusion(bf16[256,2048]{1,0:T(8,128)(2,1)S(1)} %collective-permute-done.5, bf16[256,2048]{1,0:T(8,128)(2,1)} %feed_forward.2), kind=kLoop, calls=%fused_computation.5 | loop fusion | flops 2097152 | bytes 3145728 | tf_op jit(solution)/shard_map/convert_element_type | solution.py:159
  131.0 4.2 %all-to-all-start.2 = ((bf16[4,64,2048]{2,1,0:T(8,128)(2,1)}), bf16[4,64,2048]{2,1,0:T(8,128)(2,1)S(1)}, u32[]{:S(2)}, u32[]{:S(2)}) async-start(bf16[4,64,2048]{2,1,0:T(8,128)(2,1)} %bitcast.5), calls=%async_computation.2 | async-start | bytes 2097152 | tf_op jit(solution)/shard_map/all_to_all | solution.py:160
  135.2 0.7 iota_compare_fusion.6
  139.2 0.7 iota_subtract_fusion.2
  139.9 0.6 fusion.37
  140.5 10.5 %all-to-all-done.2 = bf16[4,64,2048]{2,1,0:T(8,128)(2,1)S(1)} async-done(((bf16[4,64,2048]{2,1,0:T(8,128)(2,1)}), bf16[4,64,2048]{2,1,0:T(8,128)(2,1)S(1)}, u32[]{:S(2)}, u32[]{:S(2)}) %all-to-all-start.2) | async-done | bytes 1048608 | tf_op jit(solution)/shard_map/all_to_all | solution.py:160
  151.0 0.2 convert_reduce_fusion
  151.2 1.1 multiply_reduce_fusion
  152.3 1.1 fusion.23
  153.4 3.0 %convolution_bitcast_fusion.1 = f32[4,64,256]{2,1,0:T(8,128)S(1)} fusion(bf16[64,2048,1]{1,0,2:T(8,128)(2,1)S(1)} %fusion.23, bf16[4,2048,256]{2,1,0:T(8,128)(2,1)} %collective-permute-done.4.rest_2_), kind=kOutput, calls=%fused_computation.22 | convolution fusion | flops 268435456 | bytes 4718592 | tf_op jit(solution)/shard_map/rd,xde->xre/dot_general | solution.py:171
  156.4 0.1 multiply_reduce_fusion.2
  156.5 3.0 %convolution_bitcast_fusion.2 = f32[4,64,256]{2,1,0:T(8,128)S(1)} fusion(bf16[64,2048,1]{1,0,2:T(8,128)(2,1)S(1)} %fusion.23, bf16[4,2048,256]{2,1,0:T(8,128)(2,1)} %all_to_all.25.rest_1_), kind=kOutput, calls=%fused_computation.23 | convolution fusion | flops 268435456 | bytes 4718592 | tf_op jit(solution)/shard_map/rd,xde->xre/dot_general | solution.py:171
  159.5 0.0 copy-start.1
  159.5 0.1 multiply_reduce_fusion.3
  159.7 0.1 fusion.32
  159.8 0.1 broadcast_select_fusion.1
  159.9 0.7 copy.14
  160.6 3.4 %all-to-all-start.3 = ((bf16[8,64,256]{2,1,0:T(8,128)(2,1)}), bf16[8,64,256]{2,1,0:T(8,128)(2,1)S(1)}, u32[]{:S(2)}, u32[]{:S(2)}) async-start(bf16[8,64,256]{2,1,0:T(8,128)(2,1)} %bitcast.13), calls=%async_computation.3 | async-start | bytes 524288 | tf_op jit(solution)/shard_map/all_to_all | solution.py:179
  164.1 0.4 iota_compare_fusion.2
  164.5 7.0 %all-to-all-done.3 = bf16[8,64,256]{2,1,0:T(8,128)(2,1)S(1)} async-done(((bf16[8,64,256]{2,1,0:T(8,128)(2,1)}), bf16[8,64,256]{2,1,0:T(8,128)(2,1)S(1)}, u32[]{:S(2)}, u32[]{:S(2)}) %all-to-all-start.3) | async-done | bytes 262176 | tf_op jit(solution)/shard_map/all_to_all | solution.py:179
  171.5 3.0 %collective-permute-start.7 = (bf16[512,256]{1,0:T(8,128)(2,1)S(1)}, bf16[512,256]{1,0:T(8,128)(2,1)S(1)}, u32[]{:S(2)}, u32[]{:S(2)}) collective-permute-start(bf16[512,256]{1,0:T(8,128)(2,1)S(1)} %bitcast.49), channel_id=1, source_target_pairs={{0,16},{8,24},{16,32},{24,40},{32,48},{40,56},{48,64},{56,72},{64,... | collective-permute-start | bytes 786440 | tf_op jit(solution)/shard_map/ppermute | solution.py:25
  174.5 4.2 %collective-permute-start.6 = (bf16[512,256]{1,0:T(8,128)(2,1)S(1)}, bf16[512,256]{1,0:T(8,128)(2,1)S(1)}, u32[]{:S(2)}, u32[]{:S(2)}) collective-permute-start(bf16[512,256]{1,0:T(8,128)(2,1)S(1)} %bitcast.50), channel_id=1, source_target_pairs={{0,8},{8,16},{16,24},{24,32},{32,40},{40,48},{48,56},{56,64},{64,7... | collective-permute-start | bytes 786440 | tf_op jit(solution)/shard_map/ppermute | solution.py:25
  178.7 1.1 fusion.42
  179.8 0.5 fusion.17
  180.3 11.1 %collective-permute-done.7 = bf16[512,256]{1,0:T(8,128)(2,1)S(1)} collective-permute-done((bf16[512,256]{1,0:T(8,128)(2,1)S(1)}, bf16[512,256]{1,0:T(8,128)(2,1)S(1)}, u32[]{:S(2)}, u32[]{:S(2)}) %collective-permute-start.7) | collective-permute-done | bytes 262176 | tf_op jit(solution)/shard_map/ppermute | solution.py:25
  191.3 3.6 %collective-permute-done.6 = bf16[512,256]{1,0:T(8,128)(2,1)S(1)} collective-permute-done((bf16[512,256]{1,0:T(8,128)(2,1)S(1)}, bf16[512,256]{1,0:T(8,128)(2,1)S(1)}, u32[]{:S(2)}, u32[]{:S(2)}) %collective-permute-start.6) | collective-permute-done | bytes 262176 | tf_op jit(solution)/shard_map/ppermute | solution.py:25
  194.9 0.4 fusion.10
  195.4 1.9 collective-permute-start.8
  197.3 1.0 fusion.43
  198.3 0.5 convolution_add_fusion.1
  198.8 1.0 fusion.41
  199.8 11.6 %collective-permute-done.8 = bf16[512,256]{1,0:T(8,128)(2,1)S(1)} collective-permute-done((bf16[512,256]{1,0:T(8,128)(2,1)S(1)}, bf16[512,256]{1,0:T(8,128)(2,1)S(1)}, u32[]{:S(2)}, u32[]{:S(2)}) %collective-permute-start.8) | collective-permute-done | bytes 262176 | tf_op jit(solution)/shard_map/ppermute | solution.py:25
  211.4 1.0 fusion.40
  212.4 0.5 fusion.13
  212.9 0.5 fusion.9
  213.4 9.9 %all_to_all.26 = bf16[8,128,128]{2,1,0:T(8,128)(2,1)S(1)} all-to-all(bf16[8,128,128]{2,1,0:T(8,128)(2,1)S(1)} %bitcast.53), channel_id=1, replica_groups=mesh['seq'=64,'mp'=8] {'mp'}, dimensions={0} | all-to-all | bytes 524288 | tf_op jit(solution)/shard_map/all_to_all | solution.py:226
  223.3 2.7 %fusion.8 = bf16[128,1024]{1,0:T(8,128)(2,1)} fusion(bf16[8,128,128]{2,1,0:T(8,128)(2,1)S(1)} %all_to_all.26, bf16[8,128,1024]{2,1,0:T(8,128)(2,1)} %all-to-all-done.1.rest_3_), kind=kOutput, calls=%fused_computation.19 | convolution fusion | flops 268566528 | bytes 2621440 | tf_op jit(solution)/shard_map/hrd,hdo->ro/dot_general | solution.py:227
  (30 shorter events, 0.1 us)
Async XLA Ops:
  6.5 84.9 %copy-start = (bf16[1024,1024]{1,0:T(8,128)(2,1)S(1)}, bf16[1024,1024]{1,0:T(8,128)(2,1)}, u32[]{:S(2)}) copy-start(bf16[1024,1024]{1,0:T(8,128)(2,1)} %param.17) | copy-start | bytes 6291460
  6.5 102.2 %all-gather.2.cloned.1.call-start = ((), (), s32[]{:S(2)}) async-start(), calls=%async_computation.5 | async-start | bytes 7454720 | tf_op jit(solution)/shard_map/gather_w/all_gather | solution.py:135
  9.7 55.1 %copy-start.2 = (bf16[128,1024]{1,0:T(8,128)(2,1)S(1)}, bf16[128,1024]{1,0:T(8,128)(2,1)}, u32[]{:S(2)}) copy-start(bf16[128,1024]{1,0:T(8,128)(2,1)} %param.19) | copy-start | bytes 786436
  62.9 40.6 %collective-permute-start.4 = (bf16[4,2048,256]{2,1,0:T(8,128)(2,1)}, bf16[4,2048,256]{2,1,0:T(8,128)(2,1)}, u32[]{:S(2)}, u32[]{:S(2)}) collective-permute-start(bf16[4,2048,256]{2,1,0:T(8,128)(2,1)} %all_to_all.25.rest_1_), channel_id=1, source_target_pairs={{0,1},{1,0},{2,3},{3,2},{4,5},{5,4},{6,7},{7,6},{8,9},{9,8},{10,11... | collective-permute-start | bytes 12582920 | tf_op jit(solution)/shard_map/swap_kv/ppermute | solution.py:140
  66.4 25.1 %copy-start.3 = (bf16[1024,128]{1,0:T(8,128)(2,1)S(1)}, bf16[1024,128]{1,0:T(8,128)(2,1)}, u32[]{:S(2)}) copy-start(bf16[1024,128]{1,0:T(8,128)(2,1)} %param.18) | copy-start | bytes 786436
  66.4 37.1 %all-to-all-start.1 = ((bf16[8,128,1024]{2,1,0:T(8,128)(2,1)}), bf16[8,128,1024]{2,1,0:T(8,128)(2,1)}, u32[]{:S(2)}, u32[]{:S(2)}) async-start(bf16[8,128,1024]{2,1,0:T(8,128)(2,1)} %broadcast_in_dim.11), calls=%async_computation.1 | async-start | bytes 4194304 | tf_op jit(solution)/shard_map/spread_out/all_to_all | solution.py:31
  70.9 21.6 %copy-start.4 = (bf16[2048]{0:T(1024)(128)(2,1)S(1)}, bf16[2048]{0:T(1024)(128)(2,1)}, u32[]{:S(2)}) copy-start(bf16[2048]{0:T(1024)(128)(2,1)} %param.12) | copy-start | bytes 12292
  70.9 23.2 %collective-permute-start = (s32[1]{0:T(128)}, s32[1]{0:T(128)}, u32[]{:S(2)}, u32[]{:S(2)}) collective-permute-start(s32[1]{0:T(128)} %param.20), channel_id=1, source_target_pairs={{0,8},{8,16},{16,24},{24,32},{32,40},{40,48},{48,56},{56,64},{64,7... | collective-permute-start | bytes 20 | tf_op jit(solution)/shard_map/counts/ppermute | solution.py:25
  75.2 18.8 %collective-permute-start.1 = (s32[1]{0:T(128)}, s32[1]{0:T(128)}, u32[]{:S(2)}, u32[]{:S(2)}) collective-permute-start(s32[1]{0:T(128)} %param.20), channel_id=1, source_target_pairs={{0,16},{8,24},{16,32},{24,40},{32,48},{40,56},{48,64},{56,72},{64,... | collective-permute-start | bytes 20 | tf_op jit(solution)/shard_map/counts/ppermute | solution.py:25
  81.3 12.8 %collective-permute-start.2 = (s32[1]{0:T(128)}, s32[1]{0:T(128)}, u32[]{:S(2)}, u32[]{:S(2)}) collective-permute-start(s32[1]{0:T(128)} %param.20), channel_id=1, source_target_pairs={{0,24},{8,32},{16,40},{24,48},{32,56},{40,64},{48,72},{56,80},{64,... | collective-permute-start | bytes 20 | tf_op jit(solution)/shard_map/counts/ppermute | solution.py:25
  88.6 11.7 %collective-permute-start.3 = (s32[1]{0:T(128)}, s32[1]{0:T(128)}, u32[]{:S(2)}, u32[]{:S(2)}) collective-permute-start(s32[1]{0:T(128)} %param.20), channel_id=1, source_target_pairs={{0,32},{8,40},{16,48},{24,56},{32,64},{40,72},{48,80},{56,88},{64,... | collective-permute-start | bytes 20 | tf_op jit(solution)/shard_map/counts/ppermute | solution.py:25
  108.8 10.8 %copy-start.5 = (bf16[2048]{0:T(1024)(128)(2,1)S(1)}, bf16[2048]{0:T(1024)(128)(2,1)}, u32[]{:S(2)}) copy-start(bf16[2048]{0:T(1024)(128)(2,1)} %param.15) | copy-start | bytes 12292
  108.8 10.9 %copy-start.6 = (s32[1024]{0:T(1024)S(1)}, s32[1024]{0:T(1024)}, u32[]{:S(2)}) copy-start(s32[1024]{0:T(1024)} %param.21) | copy-start | bytes 12292
  117.0 11.4 %collective-permute-start.5 = (bf16[256,2048]{1,0:T(8,128)(2,1)}, bf16[256,2048]{1,0:T(8,128)(2,1)S(1)}, u32[]{:S(2)}, u32[]{:S(2)}) collective-permute-start(bf16[256,2048]{1,0:T(8,128)(2,1)} %feed_forward.3), channel_id=1, source_target_pairs={{0,1},{1,0},{2,3},{3,2},{4,5},{5,4},{6,7},{7,6},{8,9},{9,8},{10,11... | collective-permute-start | bytes 3145736 | tf_op jit(solution)/shard_map/ppermute | solution.py:157
  131.0 20.0 %all-to-all-start.2 = ((bf16[4,64,2048]{2,1,0:T(8,128)(2,1)}), bf16[4,64,2048]{2,1,0:T(8,128)(2,1)S(1)}, u32[]{:S(2)}, u32[]{:S(2)}) async-start(bf16[4,64,2048]{2,1,0:T(8,128)(2,1)} %bitcast.5), calls=%async_computation.2 | async-start | bytes 2097152 | tf_op jit(solution)/shard_map/all_to_all | solution.py:160
  159.5 19.2 %copy-start.1 = (bf16[1024,128]{1,0:T(8,128)(2,1)S(1)}, bf16[1024,128]{1,0:T(8,128)(2,1)}, u32[]{:S(2)}) copy-start(bf16[1024,128]{1,0:T(8,128)(2,1)} %multiply_convert_fusion.1.rest_4_) | copy-start | bytes 786436
  160.6 10.8 %all-to-all-start.3 = ((bf16[8,64,256]{2,1,0:T(8,128)(2,1)}), bf16[8,64,256]{2,1,0:T(8,128)(2,1)S(1)}, u32[]{:S(2)}, u32[]{:S(2)}) async-start(bf16[8,64,256]{2,1,0:T(8,128)(2,1)} %bitcast.13), calls=%async_computation.3 | async-start | bytes 524288 | tf_op jit(solution)/shard_map/all_to_all | solution.py:179
  171.5 19.8 %collective-permute-start.7 = (bf16[512,256]{1,0:T(8,128)(2,1)S(1)}, bf16[512,256]{1,0:T(8,128)(2,1)S(1)}, u32[]{:S(2)}, u32[]{:S(2)}) collective-permute-start(bf16[512,256]{1,0:T(8,128)(2,1)S(1)} %bitcast.49), channel_id=1, source_target_pairs={{0,16},{8,24},{16,32},{24,40},{32,48},{40,56},{48,64},{56,72},{64,... | collective-permute-start | bytes 786440 | tf_op jit(solution)/shard_map/ppermute | solution.py:25
  174.5 20.5 %collective-permute-start.6 = (bf16[512,256]{1,0:T(8,128)(2,1)S(1)}, bf16[512,256]{1,0:T(8,128)(2,1)S(1)}, u32[]{:S(2)}, u32[]{:S(2)}) collective-permute-start(bf16[512,256]{1,0:T(8,128)(2,1)S(1)} %bitcast.50), channel_id=1, source_target_pairs={{0,8},{8,16},{16,24},{24,32},{32,40},{40,48},{48,56},{56,64},{64,7... | collective-permute-start | bytes 786440 | tf_op jit(solution)/shard_map/ppermute | solution.py:25
  195.4 16.0 %collective-permute-start.8 = (bf16[512,256]{1,0:T(8,128)(2,1)S(1)}, bf16[512,256]{1,0:T(8,128)(2,1)S(1)}, u32[]{:S(2)}, u32[]{:S(2)}) collective-permute-start(bf16[512,256]{1,0:T(8,128)(2,1)S(1)} %fusion.10), channel_id=1, source_target_pairs={{0,16},{8,24},{16,32},{24,40},{32,48},{40,56},{48,64},{56,72},{64,... | collective-permute-start | bytes 786440 | tf_op jit(solution)/shard_map/ppermute | solution.py:25
Sparse Core Ops, SparseCore 0:
  10.4 98.3 all-gather.1

commit v3 on v2

v3 whole, which is shorter than its diff:
```python
import functools
import math

import jax
import jax.numpy as jnp
from jax import lax
from jax.sharding import PartitionSpec as P

from jax.experimental import pallas as pl
from jax.experimental.pallas import tpu as pltpu

HS = 128
WIN = 1024


def scale_rows(values, gain):
    return values * lax.rsqrt(jnp.mean(values * values, axis=-1, keepdims=True) + 1e-05) * gain


def unit_rows(values):
    return values * lax.rsqrt(jnp.mean(values * values, axis=-1, keepdims=True) + 1e-06)


def from_behind(value, steps):
    count = lax.axis_size("seq")
    return lax.ppermute(value, "seq", [(source, source + steps) for source in range(count - steps)])


def spread(value, axis, groups=None):
    size = lax.axis_size(axis) if groups is None else len(groups[0])
    copies = jnp.broadcast_to(value[None], (size,) + value.shape)
    return lax.all_to_all(copies, axis, 0, 0, axis_index_groups=groups)


def down_kernel(n_pieces, hidden, *rest):
    pieces, out = rest[:n_pieces], rest[n_pieces]
    at = 0
    for piece in pieces:
        size = piece.shape[0]
        out[:, at : at + size] = lax.dot_general(
            hidden[...], piece[...], (((1,), (1,)), ((), ())), preferred_element_type=jnp.float32
        ).astype(out.dtype)
        at += size


def down_project(hidden, pieces):
    rows, width = hidden.shape
    features = sum(piece.shape[0] for piece in pieces)
    whole = pl.BlockSpec(memory_space=pltpu.VMEM)
    return pl.pallas_call(
        functools.partial(down_kernel, len(pieces)),
        out_shape=jax.ShapeDtypeStruct((rows, features), jnp.bfloat16),
        in_specs=[whole] * (1 + len(pieces)),
        out_specs=whole,
        cost_estimate=pl.CostEstimate(
            flops=2 * rows * features * width,
            bytes_accessed=2 * (rows * width + features * width + rows * features),
            transcendentals=0,
        ),
        compiler_params=pltpu.CompilerParams(vmem_limit_bytes=16 * 2**20),
        name="down_project",
    )(hidden, *pieces)


def ring_gather(piece, first, second):
    half = piece.shape[0] // 2
    ahead, behind = [piece], [piece]
    for _ in range(3):
        behind.append(lax.ppermute(behind[-1], "seq", first))
        ahead.append(lax.ppermute(ahead[-1], "seq", second))
    low = lax.ppermute(behind[3][:half], "seq", first)
    high = lax.ppermute(ahead[3][half:], "seq", second)
    return ahead[:4] + [jnp.concatenate([low, high], axis=0)] + behind[3:0:-1]


def block(
    patch_states,
    mlp_gain,
    up_weight,
    down_weight,
    kv_gain,
    kv_weight,
    byte_states,
    query_weight,
    out_weight,
    patch_counts,
    byte_patch,
):
    rows, features = patch_states.shape
    n_mp = lax.axis_size("mp")
    me = lax.axis_index("mp")
    core = lax.rem(me, 2)
    chips = n_mp // 2
    own = rows // n_mp
    hidden_here = up_weight.shape[1]
    same_core = [list(range(parity, n_mp, 2)) for parity in range(2)]
    core_swap = [(source, source ^ 1) for source in range(n_mp)]

    seq = lax.axis_index("seq")
    side = 8
    lines = lax.axis_size("seq") // side
    at_y, at_z = seq // side, lax.rem(seq, side)
    along_z = [[y * side + z for z in range(side)] for y in range(lines)]
    along_y = [[y * side + z for y in range(lines)] for z in range(side)]

    def moved(dy, dz):
        return [
            (y * side + z, (y + dy) % lines * side + (z + dz) % side)
            for y in range(lines)
            for z in range(side)
        ]

    up_line = spread(up_weight, "seq", along_z).reshape(-1, hidden_here)
    down_line = spread(down_weight.T, "seq", along_y).reshape(-1, hidden_here)
    up_pieces = ring_gather(up_line, moved(1, 0), moved(-1, 0))
    down_pieces = ring_gather(down_line, moved(0, 1), moved(0, -1))
    shard = features // lax.axis_size("seq")

    def as_gathered(values, axis):
        shape = values.shape
        split = values.reshape(shape[:axis] + (lines, side, shard) + shape[axis + 1 :])
        turned = jnp.roll(jnp.swapaxes(split, axis, axis + 1), -at_z, axis)
        return turned.reshape(shape)

    kv_same = spread(as_gathered(kv_weight, 0), "mp", same_core)
    out_all = spread(out_weight, "mp")

    own_count = patch_counts[0]
    near = from_behind(patch_counts, 1)
    near = jnp.concatenate([near, from_behind(near, 1)])
    prior = jnp.concatenate([near, from_behind(near, 2)])

    queries = unit_rows(
        jnp.dot(byte_states, query_weight, preferred_element_type=jnp.float32)
    ).astype(jnp.bfloat16)

    by_core = patch_states.reshape(chips, 2, own, features)
    ordered = jnp.concatenate(
        [
            lax.dynamic_index_in_dim(by_core, parity, 1, keepdims=False).reshape(-1, features)
            for parity in (1 - core, core)
        ],
        axis=0,
    )
    normed = scale_rows(ordered.astype(jnp.float32), mlp_gain.astype(jnp.float32)).astype(
        jnp.bfloat16
    )
    line = features // lines
    turned = jnp.roll(normed.reshape(rows, lines, line).swapaxes(0, 1), -at_y, 0)
    parts = [turned[j] for j in range(lines)]
    mine_rows = as_gathered(lax.dynamic_slice_in_dim(patch_states, me * own, own, 0), 1)
    kv_scale = as_gathered(kv_gain, 0).astype(jnp.float32)
    mine_rows, kv_scale = lax.optimization_barrier((mine_rows, kv_scale))
    preact = 0.0
    for place in (0, 1, 7, 2, 6, 3, 5, 4):
        preact = preact + jnp.dot(
            parts[place], up_pieces[place], preferred_element_type=jnp.float32
        )
    hidden = jax.nn.gelu(preact, approximate=False).astype(jnp.bfloat16)
    theirs = down_project(hidden[: rows // 2], down_pieces)
    arrived = lax.ppermute(theirs, "mp", core_swap)
    mine = down_project(hidden[rows // 2 :], down_pieces)
    paired = (mine.astype(jnp.float32) + arrived.astype(jnp.float32)).astype(jnp.bfloat16)
    terms = lax.all_to_all(
        paired.reshape(chips, own, features), "mp", 0, 0, axis_index_groups=same_core
    )
    mixed = jnp.sum(terms.astype(jnp.float32), axis=0)

    kv_in = scale_rows(mine_rows.astype(jnp.float32) + mixed, kv_scale).astype(jnp.bfloat16)
    kv_partner = lax.ppermute(kv_in, "mp", core_swap)
    kv_rows = jnp.where(
        core == 0,
        jnp.concatenate([kv_in, kv_partner], axis=0),
        jnp.concatenate([kv_partner, kv_in], axis=0),
    )
    made = jnp.einsum("rd,xde->xre", kv_rows, kv_same, preferred_element_type=jnp.float32)
    by_head = jnp.concatenate([unit_rows(made[..., :HS]), made[..., HS:]], axis=-1).astype(
        jnp.bfloat16
    )
    kv_pack = lax.all_to_all(by_head, "mp", 0, 0, axis_index_groups=same_core).reshape(
        rows, 2 * HS
    )

    c1, c2, c3, c4 = (prior[k] for k in range(4))
    before2 = from_behind(kv_pack, 2)
    before1 = from_behind(kv_pack, 1)
    slot = jnp.arange(rows, dtype=jnp.int32)
    source = slot[:, None] + (c1 - rows)
    pick2 = (slot[None, :] == source + c2) & (source < 0)
    pick1 = slot[None, :] == source
    packed = jnp.dot(
        jnp.concatenate([pick2, pick1], axis=1).astype(jnp.bfloat16),
        jnp.concatenate([before2, before1], axis=0),
        preferred_element_type=jnp.float32,
    ).astype(jnp.bfloat16)
    before34 = from_behind(packed, 2)
    blocks = [
        (kv_pack, slot, slot < own_count),
        (before1, slot - c1, slot < c1),
        (before2, slot - (c1 + c2), slot < c2),
        (before34, slot - (c1 + c2 + rows), slot >= rows - (c3 + c4)),
    ]

    score_scale = 2.0 / math.sqrt(HS)
    numerator = denominator = 0.0
    for kv_block, key_ids, live in blocks:
        usable = (
            live[None, :]
            & (key_ids[None, :] <= byte_patch[:, None])
            & (key_ids[None, :] > byte_patch[:, None] - WIN)
        )
        scores = (
            lax.dot_general(
                queries,
                kv_block[:, :HS],
                (((1,), (1,)), ((), ())),
                preferred_element_type=jnp.float32,
            )
            * score_scale
        )
        weights = jnp.where(usable, jnp.exp(scores), 0.0)
        numerator = numerator + jnp.dot(
            weights.astype(jnp.bfloat16), kv_block[:, HS:], preferred_element_type=jnp.float32
        )
        denominator = denominator + jnp.sum(weights, axis=-1)
    attended = (numerator / denominator[:, None]).astype(jnp.bfloat16)

    bytes_own = attended.shape[0] // n_mp
    gathered = lax.all_to_all(attended.reshape(n_mp, bytes_own, HS), "mp", 0, 0)
    return jnp.einsum(
        "hrd,hdo->ro", gathered, out_all, preferred_element_type=jnp.float32
    ).astype(jnp.bfloat16)


def solution(mesh):
    in_specs = (
        P("seq", None),
        P(),
        P("seq", "mp"),
        P("mp", "seq"),
        P(),
        P(None, "mp"),
        P("seq", None),
        P(None, "mp"),
        P("mp", None),
        P("seq"),
        P("seq"),
    )
    return jax.shard_map(
        block,
        mesh=mesh,
        in_specs=in_specs,
        out_specs=P(("seq", "mp"), None),
        check_vma=False,
    )
```

time: 234 us -> 312 us (1.33)
  starting transfers between devices: 45.6 us -> 105 us
  blocking collectives: 63 us -> 11.7 us
  waiting for transfers between devices: 55.4 us -> 98.4 us
  local copies, waits for them, and re-layouts: 4.65 us -> 40.5 us
  between operations: 17.8 us -> 4.78 us
  Pallas kernels: 16.4 us -> 3.56 us
  matrix products: 16 us -> 24.6 us
  other arithmetic: 14.1 us -> 21.7 us
    ppermute x2 -> x18, starting transfers between devices: 3.83 us -> 57.8 us  [the longest x6 25.9 us: ring_gather(): ahead.append(lax.ppermute(ahead[-1], 'seq', second))]
    all_to_all x2 -> x1, blocking collectives: 63 us -> 11.7 us  [block(): gathered = lax.all_to_all(attended.reshape(n_mp, bytes_own, HS), 'mp', 0, 0)]
    all_to_all x3 -> x6, waiting for transfers between devices: 17.5 us -> 59 us  [the longest x4 45.7 us: spread(): return lax.all_to_all(copies, axis, 0, 0, axis_index_groups=groups)]
    all_to_all x3 -> x6, starting transfers between devices: 12.1 us -> 34.7 us  [the longest x4 26.8 us: spread(): return lax.all_to_all(copies, axis, 0, 0, axis_index_groups=groups)]
    ppermute x7 -> x6, starting transfers between devices: 29.6 us -> 12.2 us  [from_behind(): lax.ppermute(value, 'seq', [(source, source + steps) for source in range(...]
    slice x0 -> x8, local copies, waits for them, and re-layouts: none -> 13 us  [the longest x1 11.4 us: block(): parts = [turned[j] for j in range(lines)]]
    pallas_call x2, Pallas kernels: 16.4 us -> 3.56 us  [down_project(): pl.pallas_call(functools.partial(down_kernel, len(pieces)), out_shape=jax...]
    unnamed x14 -> x46, local copies, waits for them, and re-layouts: 0.03 us -> 12.1 us
  transfers between devices with their start and end apart: 13 -> 30, of which waited for: 7 -> 10; matrix products, arithmetic and copies ran while one was open for 7% -> 24% of each run, Pallas kernels for 4% -> 0%
where the time goes in v3:
time: 312 us; the launch traced here: 310 us
  starting transfers between devices  105 us (34%)
  waiting for transfers between devices  98.4 us (32%)
  local copies, waits for them, and re-layouts  40.5 us (13%)
  matrix products  24.6 us (8%)
  other arithmetic  21.7 us (7%)
  blocking collectives  11.7 us (4%)
  between operations  4.78 us (2%)
  Pallas kernels  3.56 us (1%)
    all_to_all x4, waiting for transfers between devices, spread(): return lax.all_to_all(copies, axis, 0, 0, axis_index_groups=groups)  45.7 us
    ppermute x6, waiting for transfers between devices, from_behind(): lax.ppermute(value, 'seq', [(source, source + steps) for source in range(...  35.4 us
    all_to_all x4, starting transfers between devices, spread(): return lax.all_to_all(copies, axis, 0, 0, axis_index_groups=groups)  26.8 us
    ppermute x6, starting transfers between devices, ring_gather(): ahead.append(lax.ppermute(ahead[-1], 'seq', second))  25.9 us
    ppermute x6, starting transfers between devices, ring_gather(): behind.append(lax.ppermute(behind[-1], 'seq', first))  13.8 us
    ppermute x6, starting transfers between devices, from_behind(): lax.ppermute(value, 'seq', [(source, source + steps) for source in range(...  12.2 us
    unnamed x46, local copies, waits for them, and re-layouts  12.1 us
    all_to_all x1, blocking collectives, block(): gathered = lax.all_to_all(attended.reshape(n_mp, bytes_own, HS), 'mp', 0, 0)  11.7 us
  transfers between devices with their start and end apart: 30, of which 10 were waited for; matrix products, arithmetic and copies ran while one was open for 24% of the time, Pallas kernels for 0%

profile of v3, /device:TPU:32, one launch (start us, length us, event | category | flops | bytes accessed | tf_op | source)
XLA Modules:
  0.0 309.9 jit_solution(15532382273026154490)
XLA Ops:
  0.0 1.8 broadcast_in_dim.18
  1.8 10.3 %all-to-all-start.1 = ((bf16[8,32,896]{2,1,0:T(8,128)(2,1)}), bf16[8,32,896]{2,1,0:T(8,128)(2,1)S(1)}, u32[]{:S(2)}, u32[]{:S(2)}) async-start(bf16[8,32,896]{2,1,0:T(8,128)(2,1)} %broadcast_in_dim.18), calls=%async_computation.1 | async-start | bytes 917504 | tf_op jit(solution)/shard_map/all_to_all | solution.py:32
  12.1 16.1 %all-to-all-done.1 = bf16[8,32,896]{2,1,0:T(8,128)(2,1)S(1)} async-done(((bf16[8,32,896]{2,1,0:T(8,128)(2,1)}), bf16[8,32,896]{2,1,0:T(8,128)(2,1)S(1)}, u32[]{:S(2)}, u32[]{:S(2)}) %all-to-all-start.1) | async-done | bytes 458784 | tf_op jit(solution)/shard_map/all_to_all | solution.py:32
  28.2 1.6 broadcast_in_dim.19
  29.8 7.2 %all-to-all-start.2 = ((bf16[8,32,896]{2,1,0:T(8,128)(2,1)}), bf16[8,32,896]{2,1,0:T(8,128)(2,1)S(1)}, u32[]{:S(2)}, u32[]{:S(2)}) async-start(bf16[8,32,896]{2,1,0:T(8,128)(2,1)} %broadcast_in_dim.19), calls=%async_computation.2 | async-start | bytes 917504 | tf_op jit(solution)/shard_map/all_to_all | solution.py:32
  37.0 3.2 %constant_dynamic-slice_fusion.1 = (bf16[4,1,64,2048]{3,2,1,0:T(8,128)(2,1)}, bf16[4,1,64,2048]{3,2,1,0:T(8,128)(2,1)}) fusion(bf16[4,2,64,2048]{3,2,1,0:T(8,128)(2,1)} %bitcast.104, s32[]{:T(128)S(6)} %select_n.74, s32[]{:T(128)S(6)} %select_n.75), kind=kLoop, calls=%fused_computation.136 | loop fusion | bytes 4194312 | tf_op jit(solution)/shard_map/jit(dynamic_index_in_dim)/dynamic_slice | solution.py:140
  40.2 2.6 copy.47
  44.1 2.2 multiply_reduce_fusion
  46.4 5.4 %fusion = bf16[8,512,256]{2,0,1:T(8,128)(2,1)S(1)} fusion(bf16[256,8,256]{2,1,0:T(8,128)(2,1)S(1)} %bitcast.103, bf16[256,8,256]{2,1,0:T(8,128)(2,1)S(1)} %bitcast.102, f32[8,256]{1,0:T(8,128)S(1)} %reshape.164, f32[512]{0:T(512)S(1)} %add_rsqrt_fusion.2), kind=kLoop, calls=%fused_computation.5 | loop fusion | flops 5242880 | bytes 4204544 | tf_op jit(solution)/shard_map/transpose | solution.py:149
  51.7 2.8 fusion.1
  54.5 2.5 collective-permute-start
  57.0 3.4 %collective-permute-start.1 = (bf16[256,896]{1,0:T(8,128)(2,1)S(1)}, bf16[256,896]{1,0:T(8,128)(2,1)S(1)}, u32[]{:S(2)}, u32[]{:S(2)}) collective-permute-start(bf16[256,896]{1,0:T(8,128)(2,1)S(1)} %bitcast.108), channel_id=1, source_target_pairs={{0,64},{8,72},{16,80},{24,88},{32,96},{40,104},{48,112},{56,120},{... | collective-permute-start | bytes 1376264 | tf_op jit(solution)/shard_map/ppermute | solution.py:69
  60.4 2.5 collective-permute-start.11
  62.9 4.6 %collective-permute-start.8 = (bf16[256,896]{1,0:T(8,128)(2,1)S(1)}, bf16[256,896]{1,0:T(8,128)(2,1)S(1)}, u32[]{:S(2)}, u32[]{:S(2)}) collective-permute-start(bf16[256,896]{1,0:T(8,128)(2,1)S(1)} %bitcast.94), channel_id=1, source_target_pairs={{0,56},{8,0},{16,8},{24,16},{32,24},{40,32},{48,40},{56,48},{64,12... | collective-permute-start | bytes 1376264 | tf_op jit(solution)/shard_map/ppermute | solution.py:70
  67.4 11.4 %fusion.101 = (bf16[1,512,256]{2,0,1:T(2,128)(2,1)S(1)}, bf16[1,512,256]{2,0,1:T(2,128)(2,1)S(1)}, bf16[1,512,256]{2,0,1:T(2,128)(2,1)S(1)}, bf16[1,512,256]{2,0...) fusion(bf16[8,512,256]{2,0,1:T(8,128)(2,1)} %fusion.1), kind=kLoop, calls=%fused_computation.159 | loop fusion | bytes 4194304 | tf_op jit(solution)/shard_map/slice | solution.py:150
  79.3 3.7 %collective-permute-start.2 = (bf16[256,896]{1,0:T(8,128)(2,1)}, bf16[256,896]{1,0:T(8,128)(2,1)S(1)}, u32[]{:S(2)}, u32[]{:S(2)}) collective-permute-start(bf16[256,896]{1,0:T(8,128)(2,1)} %collective-permute-done), channel_id=1, source_target_pairs={{0,448},{8,456},{16,464},{24,472},{32,480},{40,488},{48,496},{56,5... | collective-permute-start | bytes 1376264 | tf_op jit(solution)/shard_map/ppermute | solution.py:70
  83.0 2.2 collective-permute-start.3
  85.2 1.9 collective-permute-start.12
  87.2 5.1 %collective-permute-start.9 = (bf16[256,896]{1,0:T(8,128)(2,1)S(1)}, bf16[256,896]{1,0:T(8,128)(2,1)S(1)}, u32[]{:S(2)}, u32[]{:S(2)}) collective-permute-start(bf16[256,896]{1,0:T(8,128)(2,1)S(1)} %collective-permute-done.8.rest_1_), channel_id=1, source_target_pairs={{0,56},{8,0},{16,8},{24,16},{32,24},{40,32},{48,40},{56,48},{64,12... | collective-permute-start | bytes 1376264 | tf_op jit(solution)/shard_map/ppermute | solution.py:70
  92.7 1.5 fusion.76
  94.2 4.9 %collective-permute-start.4 = (bf16[256,896]{1,0:T(8,128)(2,1)S(1)}, bf16[256,896]{1,0:T(8,128)(2,1)S(1)}, u32[]{:S(2)}, u32[]{:S(2)}) collective-permute-start(bf16[256,896]{1,0:T(8,128)(2,1)S(1)} %collective-permute-done.2), channel_id=1, source_target_pairs={{0,448},{8,456},{16,464},{24,472},{32,480},{40,488},{48,496},{56,5... | collective-permute-start | bytes 1376264 | tf_op jit(solution)/shard_map/ppermute | solution.py:70
  99.1 1.9 collective-permute-start.5
  101.1 1.9 collective-permute-start.13
  103.0 5.1 %collective-permute-start.10 = (bf16[256,896]{1,0:T(8,128)(2,1)S(1)}, bf16[256,896]{1,0:T(8,128)(2,1)S(1)}, u32[]{:S(2)}, u32[]{:S(2)}) collective-permute-start(bf16[256,896]{1,0:T(8,128)(2,1)S(1)} %collective-permute-done.9.rest_2_), channel_id=1, source_target_pairs={{0,56},{8,0},{16,8},{24,16},{32,24},{40,32},{48,40},{56,48},{64,12... | collective-permute-start | bytes 1376264 | tf_op jit(solution)/shard_map/ppermute | solution.py:70
  109.0 2.5 collective-permute-done.5
  111.5 1.9 collective-permute-start.6
  113.5 5.1 %collective-permute-start.7 = (bf16[128,896]{1,0:T(8,128)(2,1)S(1)}, bf16[128,896]{1,0:T(8,128)(2,1)S(1)}, u32[]{:S(2)}, u32[]{:S(2)}) collective-permute-start(bf16[128,896]{1,0:T(8,128)(2,1)S(1)} %slice.114), channel_id=1, source_target_pairs={{0,448},{8,456},{16,464},{24,472},{32,480},{40,488},{48,496},{56,5... | collective-permute-start | bytes 688136 | tf_op jit(solution)/shard_map/ppermute | solution.py:72
  118.7 1.9 collective-permute-start.14
  120.6 5.3 %collective-permute-start.15 = (bf16[128,896]{1,0:T(8,128)(2,1)S(1)}, bf16[128,896]{1,0:T(8,128)(2,1)S(1)}, u32[]{:S(2)}, u32[]{:S(2)}) collective-permute-start(bf16[128,896]{1,0:T(8,128)(2,1)S(1)} %slice.117), channel_id=1, source_target_pairs={{0,56},{8,0},{16,8},{24,16},{32,24},{40,32},{48,40},{56,48},{64,12... | collective-permute-start | bytes 688136 | tf_op jit(solution)/shard_map/ppermute | solution.py:72
  126.4 1.4 collective-permute-done.14
  128.3 4.7 %fusion.10 = bf16[512,896]{1,0:T(8,128)(2,1)S(1)} fusion(f32[512,896]{1,0:T(8,128)S(1)} %fusion.53, f32[512,896]{1,0:T(8,128)S(1)} %fusion.64, f32[512,896]{1,0:T(8,128)S(1)} %fusion.67, f32[512,896]{1,0:T(8,128)S(1)} %fusion.70, f32[512,896]{1,0:T(8,128)S(1)} %fusion.73, f32[512,896]{1,0:T(8,128)S(1)} %fusion.79, f32[512,896]{1,0:T(8,128)S(1)} %fusion.76, ...), kind=kOutput, calls=%fused_computation.25 | convolution fusion | flops 267911168 | bytes 14483456 | tf_op jit(solution)/shard_map/dot_general | solution.py:156
  133.9 2.3 down_project.3
  136.2 1.9 collective-permute-start.16
  138.1 1.9 collective-permute-start.18
  140.8 1.7 constant_dynamic-slice_fusion.2
  142.5 2.0 copy.46
  151.8 2.6 add_convert_fusion
  154.4 4.4 %all-to-all-start.3 = ((bf16[4,64,2048]{2,1,0:T(8,128)(2,1)}), bf16[4,64,2048]{2,1,0:T(8,128)(2,1)}, u32[]{:S(2)}, u32[]{:S(2)}) async-start(bf16[4,64,2048]{2,1,0:T(8,128)(2,1)} %bitcast.15), calls=%async_computation.3 | async-start | bytes 2097152 | tf_op jit(solution)/shard_map/all_to_all | solution.py:164
  159.6 1.6 fusion.28
  162.3 1.5 copy.28
  163.8 2.6 multiply_reduce_fusion.2
  166.4 8.6 %all-to-all-done.3 = bf16[4,64,2048]{2,1,0:T(8,128)(2,1)} async-done(((bf16[4,64,2048]{2,1,0:T(8,128)(2,1)}), bf16[4,64,2048]{2,1,0:T(8,128)(2,1)}, u32[]{:S(2)}, u32[]{:S(2)}) %all-to-all-start.3) | async-done | bytes 1048608 | tf_op jit(solution)/shard_map/all_to_all | solution.py:164
  174.9 2.6 broadcast_in_dim.17
  177.5 5.0 %all-to-all-start = ((bf16[4,2048,256]{1,2,0:T(8,128)(2,1)}), bf16[4,2048,256]{1,2,0:T(8,128)(2,1)}, u32[]{:S(2)}, u32[]{:S(2)}) async-start(bf16[4,2048,256]{1,2,0:T(8,128)(2,1)} %broadcast_in_dim.17), calls=%async_computation | async-start | bytes 8388608 | tf_op jit(solution)/shard_map/all_to_all | solution.py:32
  183.3 1.9 collective-permute-start.20
  186.9 5.4 %collective-permute-done.20 = s32[1]{0:T(128)} collective-permute-done((s32[1]{0:T(128)}, s32[1]{0:T(128)}, u32[]{:S(2)}, u32[]{:S(2)}) %collective-permute-start.20) | collective-permute-done | bytes 36 | tf_op jit(solution)/shard_map/ppermute | solution.py:26
  194.6 1.4 convert_reduce_fusion
  196.3 1.9 collective-permute-start.17
  198.3 1.3 pad_add_fusion
  199.6 1.9 collective-permute-start.22
  201.8 29.6 %all-to-all-done = bf16[4,2048,256]{1,2,0:T(8,128)(2,1)} async-done(((bf16[4,2048,256]{1,2,0:T(8,128)(2,1)}), bf16[4,2048,256]{1,2,0:T(8,128)(2,1)}, u32[]{:S(2)}, u32[]{:S(2)}) %all-to-all-start) | async-done | bytes 4194336 | tf_op jit(solution)/shard_map/all_to_all | solution.py:32
  231.4 3.6 %convolution_bitcast_fusion.1 = f32[4,128,256]{1,2,0:T(8,128)S(1)} fusion(bf16[4,2048,256]{1,2,0:T(8,128)(2,1)} %all-to-all-done, bf16[64,2048]{1,0:T(8,128)(2,1)} %collective-permute-done.17, bf16[64,2048]{1,0:T(8,128)(2,1)S(1)} %multiply_convert_fusion.1, pred[]{:T(512)S(6)} %eq.38), kind=kOutput, calls=%fused_computation.47 | convolution fusion | flops 539230208 | bytes 5242881 | tf_op jit(solution)/shard_map/rd,xde->xre/dot_general | solution.py:176
  235.8 3.4 %all-to-all-start.4 = ((bf16[4,128,256]{1,2,0:T(8,128)(2,1)}), bf16[4,128,256]{1,2,0:T(8,128)(2,1)S(1)}, u32[]{:S(2)}, u32[]{:S(2)}) async-start(bf16[4,128,256]{1,2,0:T(8,128)(2,1)} %pad_maximum_fusion), calls=%async_computation.4 | async-start | bytes 524288 | tf_op jit(solution)/shard_map/all_to_all | solution.py:180
  241.1 4.8 %all-to-all-done.4 = bf16[4,128,256]{1,2,0:T(8,128)(2,1)S(1)} async-done(((bf16[4,128,256]{1,2,0:T(8,128)(2,1)}), bf16[4,128,256]{1,2,0:T(8,128)(2,1)S(1)}, u32[]{:S(2)}, u32[]{:S(2)}) %all-to-all-start.4) | async-done | bytes 262176 | tf_op jit(solution)/shard_map/all_to_all | solution.py:180
  245.8 1.6 broadcast_in_dim.21
  247.4 4.3 %all-to-all-start.6 = ((bf16[8,128,1024]{2,1,0:T(8,128)(2,1)}), bf16[8,128,1024]{2,1,0:T(8,128)(2,1)}, u32[]{:S(2)}, u32[]{:S(2)}) async-start(bf16[8,128,1024]{2,1,0:T(8,128)(2,1)} %broadcast_in_dim.21), calls=%async_computation.6 | async-start | bytes 4194304 | tf_op jit(solution)/shard_map/all_to_all | solution.py:32
  251.9 1.9 collective-permute-start.21
  253.9 2.6 collective-permute-start.19
  258.0 14.6 %collective-permute-done.21 = bf16[512,256]{1,0:T(8,128)(2,1)S(1)} collective-permute-done((bf16[512,256]{1,0:T(8,128)(2,1)S(1)}, bf16[512,256]{1,0:T(8,128)(2,1)S(1)}, u32[]{:S(2)}, u32[]{:S(2)}) %collective-permute-start.21) | collective-permute-done | bytes 262176 | tf_op jit(solution)/shard_map/ppermute | solution.py:26
  272.6 4.1 %collective-permute-done.19 = bf16[512,256]{1,0:T(8,128)(2,1)S(1)} collective-permute-done((bf16[512,256]{1,0:T(8,128)(2,1)S(1)}, bf16[512,256]{1,0:T(8,128)(2,1)S(1)}, u32[]{:S(2)}, u32[]{:S(2)}) %collective-permute-start.19) | collective-permute-done | bytes 262176 | tf_op jit(solution)/shard_map/ppermute | solution.py:26
  277.1 1.9 collective-permute-start.23
  281.5 11.4 %collective-permute-done.23 = bf16[512,256]{1,0:T(8,128)(2,1)S(1)} collective-permute-done((bf16[512,256]{1,0:T(8,128)(2,1)S(1)}, bf16[512,256]{1,0:T(8,128)(2,1)S(1)}, u32[]{:S(2)}, u32[]{:S(2)}) %collective-permute-start.23) | collective-permute-done | bytes 262176 | tf_op jit(solution)/shard_map/ppermute | solution.py:26
  295.4 11.7 %all_to_all.35 = bf16[8,128,128]{2,1,0:T(8,128)(2,1)S(1)} all-to-all(bf16[8,128,128]{2,1,0:T(8,128)(2,1)S(1)} %bitcast.115), channel_id=1, replica_groups=mesh['seq'=64,'mp'=8] {'mp'}, dimensions={0} | all-to-all | bytes 524288 | tf_op jit(solution)/shard_map/all_to_all | solution.py:229
  307.1 2.7 fusion.22
  (122 shorter events, 26.0 us)
Async XLA Ops:
  0.0 163.8 %copy-start = (bf16[1024,1024]{1,0:T(8,128)(2,1)S(1)}, bf16[1024,1024]{1,0:T(8,128)(2,1)}, u32[]{:S(2)}) copy-start(bf16[1024,1024]{1,0:T(8,128)(2,1)} %param.17) | copy-start | bytes 6291460
  1.8 26.4 %all-to-all-start.1 = ((bf16[8,32,896]{2,1,0:T(8,128)(2,1)}), bf16[8,32,896]{2,1,0:T(8,128)(2,1)S(1)}, u32[]{:S(2)}, u32[]{:S(2)}) async-start(bf16[8,32,896]{2,1,0:T(8,128)(2,1)} %broadcast_in_dim.18), calls=%async_computation.1 | async-start | bytes 917504 | tf_op jit(solution)/shard_map/all_to_all | solution.py:32
  29.8 30.5 %all-to-all-start.2 = ((bf16[8,32,896]{2,1,0:T(8,128)(2,1)}), bf16[8,32,896]{2,1,0:T(8,128)(2,1)S(1)}, u32[]{:S(2)}, u32[]{:S(2)}) async-start(bf16[8,32,896]{2,1,0:T(8,128)(2,1)} %broadcast_in_dim.19), calls=%async_computation.2 | async-start | bytes 917504 | tf_op jit(solution)/shard_map/all_to_all | solution.py:32
  40.2 2.6 copy-start.12
  40.2 3.9 %copy-start.18 = (bf16[2048]{0:T(1024)(128)(2,1)S(1)}, bf16[2048]{0:T(1024)(128)(2,1)}, u32[]{:S(2)}) copy-start(bf16[2048]{0:T(1024)(128)(2,1)} %param.12) | copy-start | bytes 12292
  44.1 2.2 copy-start.13
  44.1 2.2 copy-start.14
  54.5 24.8 %collective-permute-start = (bf16[256,896]{1,0:T(8,128)(2,1)S(1)}, bf16[256,896]{1,0:T(8,128)(2,1)}, u32[]{:S(2)}, u32[]{:S(2)}) collective-permute-start(bf16[256,896]{1,0:T(8,128)(2,1)S(1)} %bitcast.107), channel_id=1, source_target_pairs={{0,448},{8,456},{16,464},{24,472},{32,480},{40,488},{48,496},{56,5... | collective-permute-start | bytes 1376264 | tf_op jit(solution)/shard_map/ppermute | solution.py:70
  57.0 26.0 %collective-permute-start.1 = (bf16[256,896]{1,0:T(8,128)(2,1)S(1)}, bf16[256,896]{1,0:T(8,128)(2,1)S(1)}, u32[]{:S(2)}, u32[]{:S(2)}) collective-permute-start(bf16[256,896]{1,0:T(8,128)(2,1)S(1)} %bitcast.108), channel_id=1, source_target_pairs={{0,64},{8,72},{16,80},{24,88},{32,96},{40,104},{48,112},{56,120},{... | collective-permute-start | bytes 1376264 | tf_op jit(solution)/shard_map/ppermute | solution.py:69
  60.4 24.8 %collective-permute-start.11 = (bf16[256,896]{1,0:T(8,128)(2,1)S(1)}, bf16[256,896]{1,0:T(8,128)(2,1)S(1)}, u32[]{:S(2)}, u32[]{:S(2)}) collective-permute-start(bf16[256,896]{1,0:T(8,128)(2,1)S(1)} %bitcast.93), channel_id=1, source_target_pairs={{0,8},{8,16},{16,24},{24,32},{32,40},{40,48},{48,56},{56,0},{64,72... | collective-permute-start | bytes 1376264 | tf_op jit(solution)/shard_map/ppermute | solution.py:69
  62.9 24.3 %collective-permute-start.8 = (bf16[256,896]{1,0:T(8,128)(2,1)S(1)}, bf16[256,896]{1,0:T(8,128)(2,1)S(1)}, u32[]{:S(2)}, u32[]{:S(2)}) collective-permute-start(bf16[256,896]{1,0:T(8,128)(2,1)S(1)} %bitcast.94), channel_id=1, source_target_pairs={{0,56},{8,0},{16,8},{24,16},{32,24},{40,32},{48,40},{56,48},{64,12... | collective-permute-start | bytes 1376264 | tf_op jit(solution)/shard_map/ppermute | solution.py:70
  79.3 14.9 %collective-permute-start.2 = (bf16[256,896]{1,0:T(8,128)(2,1)}, bf16[256,896]{1,0:T(8,128)(2,1)S(1)}, u32[]{:S(2)}, u32[]{:S(2)}) collective-permute-start(bf16[256,896]{1,0:T(8,128)(2,1)} %collective-permute-done), channel_id=1, source_target_pairs={{0,448},{8,456},{16,464},{24,472},{32,480},{40,488},{48,496},{56,5... | collective-permute-start | bytes 1376264 | tf_op jit(solution)/shard_map/ppermute | solution.py:70
  83.0 16.1 %collective-permute-start.3 = (bf16[256,896]{1,0:T(8,128)(2,1)S(1)}, bf16[256,896]{1,0:T(8,128)(2,1)S(1)}, u32[]{:S(2)}, u32[]{:S(2)}) collective-permute-start(bf16[256,896]{1,0:T(8,128)(2,1)S(1)} %collective-permute-done.1), channel_id=1, source_target_pairs={{0,64},{8,72},{16,80},{24,88},{32,96},{40,104},{48,112},{56,120},{... | collective-permute-start | bytes 1376264 | tf_op jit(solution)/shard_map/ppermute | solution.py:69
  85.2 48.7 %copy-start.3 = (bf16[256,896]{1,0:T(8,128)(2,1)}, bf16[256,896]{1,0:T(8,128)(2,1)S(1)}, u32[]{:S(2)}) copy-start(bf16[256,896]{1,0:T(8,128)(2,1)S(1)} %collective-permute-done.11.rest_7_) | copy-start | bytes 1376260
  85.2 15.8 %collective-permute-start.12 = (bf16[256,896]{1,0:T(8,128)(2,1)S(1)}, bf16[256,896]{1,0:T(8,128)(2,1)S(1)}, u32[]{:S(2)}, u32[]{:S(2)}) collective-permute-start(bf16[256,896]{1,0:T(8,128)(2,1)S(1)} %collective-permute-done.11.rest_7_), channel_id=1, source_target_pairs={{0,8},{8,16},{16,24},{24,32},{32,40},{40,48},{48,56},{56,0},{64,72... | collective-permute-start | bytes 1376264 | tf_op jit(solution)/shard_map/ppermute | solution.py:69
  87.2 46.8 %copy-start.5 = (bf16[256,896]{1,0:T(8,128)(2,1)}, bf16[256,896]{1,0:T(8,128)(2,1)S(1)}, u32[]{:S(2)}) copy-start(bf16[256,896]{1,0:T(8,128)(2,1)S(1)} %collective-permute-done.8.rest_1_) | copy-start | bytes 1376260
  87.2 15.8 %collective-permute-start.9 = (bf16[256,896]{1,0:T(8,128)(2,1)S(1)}, bf16[256,896]{1,0:T(8,128)(2,1)S(1)}, u32[]{:S(2)}, u32[]{:S(2)}) collective-permute-start(bf16[256,896]{1,0:T(8,128)(2,1)S(1)} %collective-permute-done.8.rest_1_), channel_id=1, source_target_pairs={{0,56},{8,0},{16,8},{24,16},{32,24},{40,32},{48,40},{56,48},{64,12... | collective-permute-start | bytes 1376264 | tf_op jit(solution)/shard_map/ppermute | solution.py:70
  94.2 19.2 %collective-permute-start.4 = (bf16[256,896]{1,0:T(8,128)(2,1)S(1)}, bf16[256,896]{1,0:T(8,128)(2,1)S(1)}, u32[]{:S(2)}, u32[]{:S(2)}) collective-permute-start(bf16[256,896]{1,0:T(8,128)(2,1)S(1)} %collective-permute-done.2), channel_id=1, source_target_pairs={{0,448},{8,456},{16,464},{24,472},{32,480},{40,488},{48,496},{56,5... | collective-permute-start | bytes 1376264 | tf_op jit(solution)/shard_map/ppermute | solution.py:70
  99.1 12.4 %collective-permute-start.5 = (bf16[256,896]{1,0:T(8,128)(2,1)S(1)}, bf16[256,896]{1,0:T(8,128)(2,1)S(1)}, u32[]{:S(2)}, u32[]{:S(2)}) collective-permute-start(bf16[256,896]{1,0:T(8,128)(2,1)S(1)} %collective-permute-done.3), channel_id=1, source_target_pairs={{0,64},{8,72},{16,80},{24,88},{32,96},{40,104},{48,112},{56,120},{... | collective-permute-start | bytes 1376264 | tf_op jit(solution)/shard_map/ppermute | solution.py:69
  101.1 32.9 %copy-start.7 = (bf16[256,896]{1,0:T(8,128)(2,1)}, bf16[256,896]{1,0:T(8,128)(2,1)S(1)}, u32[]{:S(2)}) copy-start(bf16[256,896]{1,0:T(8,128)(2,1)S(1)} %collective-permute-done.12.rest_6_) | copy-start | bytes 1376260
  101.1 17.6 %collective-permute-start.13 = (bf16[256,896]{1,0:T(8,128)(2,1)S(1)}, bf16[256,896]{1,0:T(8,128)(2,1)S(1)}, u32[]{:S(2)}, u32[]{:S(2)}) collective-permute-start(bf16[256,896]{1,0:T(8,128)(2,1)S(1)} %collective-permute-done.12.rest_6_), channel_id=1, source_target_pairs={{0,8},{8,16},{16,24},{24,32},{32,40},{40,48},{48,56},{56,0},{64,72... | collective-permute-start | bytes 1376264 | tf_op jit(solution)/shard_map/ppermute | solution.py:69
  103.0 30.9 %copy-start.9 = (bf16[256,896]{1,0:T(8,128)(2,1)}, bf16[256,896]{1,0:T(8,128)(2,1)S(1)}, u32[]{:S(2)}) copy-start(bf16[256,896]{1,0:T(8,128)(2,1)S(1)} %collective-permute-done.9.rest_2_) | copy-start | bytes 1376260
  103.0 17.6 %collective-permute-start.10 = (bf16[256,896]{1,0:T(8,128)(2,1)S(1)}, bf16[256,896]{1,0:T(8,128)(2,1)S(1)}, u32[]{:S(2)}, u32[]{:S(2)}) collective-permute-start(bf16[256,896]{1,0:T(8,128)(2,1)S(1)} %collective-permute-done.9.rest_2_), channel_id=1, source_target_pairs={{0,56},{8,0},{16,8},{24,16},{32,24},{40,32},{48,40},{56,48},{64,12... | collective-permute-start | bytes 1376264 | tf_op jit(solution)/shard_map/ppermute | solution.py:70
  111.5 16.3 %collective-permute-start.6 = (bf16[128,896]{1,0:T(8,128)(2,1)S(1)}, bf16[128,896]{1,0:T(8,128)(2,1)S(1)}, u32[]{:S(2)}, u32[]{:S(2)}) collective-permute-start(bf16[128,896]{1,0:T(8,128)(2,1)S(1)} %slice.113), channel_id=1, source_target_pairs={{0,64},{8,72},{16,80},{24,88},{32,96},{40,104},{48,112},{56,120},{... | collective-permute-start | bytes 688136 | tf_op jit(solution)/shard_map/ppermute | solution.py:71
  113.5 14.3 %collective-permute-start.7 = (bf16[128,896]{1,0:T(8,128)(2,1)S(1)}, bf16[128,896]{1,0:T(8,128)(2,1)S(1)}, u32[]{:S(2)}, u32[]{:S(2)}) collective-permute-start(bf16[128,896]{1,0:T(8,128)(2,1)S(1)} %slice.114), channel_id=1, source_target_pairs={{0,448},{8,456},{16,464},{24,472},{32,480},{40,488},{48,496},{56,5... | collective-permute-start | bytes 688136 | tf_op jit(solution)/shard_map/ppermute | solution.py:72
  118.7 9.1 %collective-permute-start.14 = (bf16[128,896]{1,0:T(8,128)(2,1)S(1)}, bf16[128,896]{1,0:T(8,128)(2,1)S(1)}, u32[]{:S(2)}, u32[]{:S(2)}) collective-permute-start(bf16[128,896]{1,0:T(8,128)(2,1)S(1)} %slice.116), channel_id=1, source_target_pairs={{0,8},{8,16},{16,24},{24,32},{32,40},{40,48},{48,56},{56,0},{64,72... | collective-permute-start | bytes 688136 | tf_op jit(solution)/shard_map/ppermute | solution.py:71
  120.6 13.2 %collective-permute-start.15 = (bf16[128,896]{1,0:T(8,128)(2,1)S(1)}, bf16[128,896]{1,0:T(8,128)(2,1)S(1)}, u32[]{:S(2)}, u32[]{:S(2)}) collective-permute-start(bf16[128,896]{1,0:T(8,128)(2,1)S(1)} %slice.117), channel_id=1, source_target_pairs={{0,56},{8,0},{16,8},{24,16},{32,24},{40,32},{48,40},{56,48},{64,12... | collective-permute-start | bytes 688136 | tf_op jit(solution)/shard_map/ppermute | solution.py:72
  133.9 2.3 copy-start.1
  136.2 15.6 %collective-permute-start.16 = (bf16[256,2048]{1,0:T(8,128)(2,1)}, bf16[256,2048]{1,0:T(8,128)(2,1)}, u32[]{:S(2)}, u32[]{:S(2)}) collective-permute-start(bf16[256,2048]{1,0:T(8,128)(2,1)} %down_project.3), channel_id=1, source_target_pairs={{0,1},{1,0},{2,3},{3,2},{4,5},{5,4},{6,7},{7,6},{8,9},{9,8},{10,11... | collective-permute-start | bytes 3145736 | tf_op jit(solution)/shard_map/ppermute | solution.py:161
  138.1 44.4 %collective-permute-start.18 = (s32[1]{0:T(128)}, s32[1]{0:T(128)}, u32[]{:S(2)}, u32[]{:S(2)}) collective-permute-start(s32[1]{0:T(128)} %param.20), channel_id=1, source_target_pairs={{0,8},{8,16},{16,24},{24,32},{32,40},{40,48},{48,56},{56,64},{64,7... | collective-permute-start | bytes 20 | tf_op jit(solution)/shard_map/ppermute | solution.py:26
  144.4 1.0 copy-start.2
  145.4 1.0 copy-start.4
  146.5 1.0 copy-start.6
  147.5 1.0 copy-start.8
  148.5 1.0 copy-start.10
  149.5 1.0 copy-start.11
  154.4 4.4 %copy-start.15 = (bf16[64,2048]{0,1:T(8,128)(2,1)S(1)}, bf16[64,2048]{0,1:T(8,128)(2,1)}, u32[]{:S(2)}) copy-start(bf16[64,2048]{0,1:T(8,128)(2,1)} %copy.46) | copy-start | bytes 786436
  154.4 4.8 %copy-start.19 = (bf16[2048]{0:T(1024)(128)(2,1)S(1)}, bf16[2048]{0:T(1024)(128)(2,1)}, u32[]{:S(2)}) copy-start(bf16[2048]{0:T(1024)(128)(2,1)} %param.15) | copy-start | bytes 12292
  154.4 20.5 %all-to-all-start.3 = ((bf16[4,64,2048]{2,1,0:T(8,128)(2,1)}), bf16[4,64,2048]{2,1,0:T(8,128)(2,1)}, u32[]{:S(2)}, u32[]{:S(2)}) async-start(bf16[4,64,2048]{2,1,0:T(8,128)(2,1)} %bitcast.15), calls=%async_computation.3 | async-start | bytes 2097152 | tf_op jit(solution)/shard_map/all_to_all | solution.py:164
  177.5 5.0 %copy-start.20 = (s32[1024]{0:T(1024)S(1)}, s32[1024]{0:T(1024)}, u32[]{:S(2)}) copy-start(s32[1024]{0:T(1024)} %param.21) | copy-start | bytes 12292
  177.5 5.0 %copy-start.16 = (f32[1024,128]{0,1:T(8,128)S(1)}, f32[1024,128]{0,1:T(8,128)}, u32[]{:S(2)}) copy-start(f32[1024,128]{0,1:T(8,128)} %get-tuple-element.24) | copy-start | bytes 1572868
  177.5 53.9 %all-to-all-start = ((bf16[4,2048,256]{1,2,0:T(8,128)(2,1)}), bf16[4,2048,256]{1,2,0:T(8,128)(2,1)}, u32[]{:S(2)}, u32[]{:S(2)}) async-start(bf16[4,2048,256]{1,2,0:T(8,128)(2,1)} %broadcast_in_dim.17), calls=%async_computation | async-start | bytes 8388608 | tf_op jit(solution)/shard_map/all_to_all | solution.py:32
  183.3 8.9 %collective-permute-start.20 = (s32[1]{0:T(128)}, s32[1]{0:T(128)}, u32[]{:S(2)}, u32[]{:S(2)}) collective-permute-start(s32[1]{0:T(128)} %collective-permute-done.18), channel_id=1, source_target_pairs={{0,8},{8,16},{16,24},{24,32},{32,40},{40,48},{48,56},{56,64},{64,7... | collective-permute-start | bytes 20 | tf_op jit(solution)/shard_map/ppermute | solution.py:26
  196.3 35.0 %collective-permute-start.17 = (bf16[64,2048]{1,0:T(8,128)(2,1)S(1)}, bf16[64,2048]{1,0:T(8,128)(2,1)}, u32[]{:S(2)}, u32[]{:S(2)}) collective-permute-start(bf16[64,2048]{1,0:T(8,128)(2,1)S(1)} %multiply_convert_fusion.1), channel_id=1, source_target_pairs={{0,1},{1,0},{2,3},{3,2},{4,5},{5,4},{6,7},{7,6},{8,9},{9,8},{10,11... | collective-permute-start | bytes 786440 | tf_op jit(solution)/shard_map/ppermute | solution.py:170
  199.6 39.6 %collective-permute-start.22 = (s32[2]{0:T(128)S(1)}, s32[2]{0:T(128)S(1)}, u32[]{:S(2)}, u32[]{:S(2)}) collective-permute-start(s32[2]{0:T(128)S(1)} %pad_add_fusion), channel_id=1, source_target_pairs={{0,16},{8,24},{16,32},{24,40},{32,48},{40,56},{48,64},{56,72},{64,... | collective-permute-start | bytes 32 | tf_op jit(solution)/shard_map/ppermute | solution.py:26
  234.9 10.9 %copy-start.17 = (bf16[128,1024]{1,0:T(8,128)(2,1)S(1)}, bf16[128,1024]{1,0:T(8,128)(2,1)}, u32[]{:S(2)}) copy-start(bf16[128,1024]{1,0:T(8,128)(2,1)} %param.19) | copy-start | bytes 786436
  235.8 10.1 %all-to-all-start.4 = ((bf16[4,128,256]{1,2,0:T(8,128)(2,1)}), bf16[4,128,256]{1,2,0:T(8,128)(2,1)S(1)}, u32[]{:S(2)}, u32[]{:S(2)}) async-start(bf16[4,128,256]{1,2,0:T(8,128)(2,1)} %pad_maximum_fusion), calls=%async_computation.4 | async-start | bytes 524288 | tf_op jit(solution)/shard_map/all_to_all | solution.py:180
  247.4 48.0 %all-to-all-start.6 = ((bf16[8,128,1024]{2,1,0:T(8,128)(2,1)}), bf16[8,128,1024]{2,1,0:T(8,128)(2,1)}, u32[]{:S(2)}, u32[]{:S(2)}) async-start(bf16[8,128,1024]{2,1,0:T(8,128)(2,1)} %broadcast_in_dim.21), calls=%async_computation.6 | async-start | bytes 4194304 | tf_op jit(solution)/shard_map/all_to_all | solution.py:32
  251.9 20.6 %collective-permute-start.21 = (bf16[512,256]{1,0:T(8,128)(2,1)S(1)}, bf16[512,256]{1,0:T(8,128)(2,1)S(1)}, u32[]{:S(2)}, u32[]{:S(2)}) collective-permute-start(bf16[512,256]{1,0:T(8,128)(2,1)S(1)} %bitcast.111), channel_id=1, source_target_pairs={{0,16},{8,24},{16,32},{24,40},{32,48},{40,56},{48,64},{56,72},{64,... | collective-permute-start | bytes 786440 | tf_op jit(solution)/shard_map/ppermute | solution.py:26
  253.9 22.8 %collective-permute-start.19 = (bf16[512,256]{1,0:T(8,128)(2,1)S(1)}, bf16[512,256]{1,0:T(8,128)(2,1)S(1)}, u32[]{:S(2)}, u32[]{:S(2)}) collective-permute-start(bf16[512,256]{1,0:T(8,128)(2,1)S(1)} %bitcast.112), channel_id=1, source_target_pairs={{0,8},{8,16},{16,24},{24,32},{32,40},{40,48},{48,56},{56,64},{64,7... | collective-permute-start | bytes 786440 | tf_op jit(solution)/shard_map/ppermute | solution.py:26
  277.1 15.7 %collective-permute-start.23 = (bf16[512,256]{1,0:T(8,128)(2,1)S(1)}, bf16[512,256]{1,0:T(8,128)(2,1)S(1)}, u32[]{:S(2)}, u32[]{:S(2)}) collective-permute-start(bf16[512,256]{1,0:T(8,128)(2,1)S(1)} %fusion.24), channel_id=1, source_target_pairs={{0,16},{8,24},{16,32},{24,40},{32,48},{40,56},{48,64},{56,72},{64,... | collective-permute-start | bytes 786440 | tf_op jit(solution)/shard_map/ppermute | solution.py:26

commit v4 on v2

v4 whole, which is shorter than its diff:
```python
import functools
import math

import jax
import jax.numpy as jnp
from jax import lax
from jax.sharding import PartitionSpec as P
from jax.experimental import pallas as pl
from jax.experimental.pallas import tpu as pltpu

HS = 128
WIN = 1024


def scale_rows(values, gain):
    return values * lax.rsqrt(jnp.mean(values * values, axis=-1, keepdims=True) + 1e-05) * gain


def unit_rows(values):
    return values * lax.rsqrt(jnp.mean(values * values, axis=-1, keepdims=True) + 1e-06)


def from_behind(value, steps):
    count = lax.axis_size("seq")
    return lax.ppermute(value, "seq", [(source, source + steps) for source in range(count - steps)])


def spread(value, groups=None):
    size = lax.axis_size("mp") if groups is None else len(groups[0])
    copies = jnp.broadcast_to(value[None], (size,) + value.shape)
    return lax.all_to_all(copies, "mp", 0, 0, axis_index_groups=groups)


WHOLE = pl.BlockSpec(memory_space=pltpu.VMEM)
ANYWHERE = pl.BlockSpec(memory_space=pl.ANY)
SCALARS = pl.BlockSpec(memory_space=pltpu.SMEM)


def activate(preact):
    return (0.5 * preact * (1.0 + lax.erf(preact * math.sqrt(0.5)))).astype(jnp.bfloat16)


def flat(block):
    return block.reshape(-1, block.shape[-1])


def dot_rows(left, right):
    return lax.dot_general(
        left, right, (((1,), (1,)), ((), ())), preferred_element_type=jnp.float32
    )


def load(weights, kind, target, sems):
    parts = sems.shape[0]
    each = target.shape[0] // parts
    copies = []
    for part in range(parts):
        span = pl.ds(part * each, each)
        copies.append(
            pltpu.make_async_copy(weights.at[span, kind], target.at[span], sems.at[part])
        )
    for copy in copies:
        copy.start()
    return copies


def up_product(normed, up, copies, preact):
    each, wide = up.shape[0] // len(copies), normed.shape[1] // len(copies)
    for part, copy in enumerate(copies):
        copy.wait()
        product = jnp.dot(
            normed[:, part * wide : (part + 1) * wide],
            flat(up[part * each : (part + 1) * each]),
            preferred_element_type=jnp.float32,
        )
        if part == 0:
            preact[...] = product
        else:
            preact[...] += product


def down_product(hidden, down, copies, out, added=None):
    each, wide = down.shape[0] // len(copies), out.shape[1] // len(copies)
    for part, copy in enumerate(copies):
        copy.wait()
        span = slice(part * wide, (part + 1) * wide)
        made = dot_rows(hidden[...], flat(down[part * each : (part + 1) * each]))
        if added is not None:
            made = made + added[:, span].astype(jnp.float32)
        out[:, span] = made.astype(out.dtype)


def first_kernel(n_early, normed, weights, *rest):
    out, up, down, preact, hidden, up_sems, down_sems = rest[n_early:]
    up_copies = load(weights, 0, up, up_sems)
    down_copies = load(weights, 1, down, down_sems)
    up_product(normed, up, up_copies, preact)
    hidden[...] = activate(preact[...])
    down_product(hidden, down, down_copies, out)


def up_kernel(normed, weights, hidden, up, preact, sems):
    up_product(normed, up, load(weights, 0, up, sems), preact)
    hidden[...] = activate(preact[...])


def down_kernel(hidden, weights, arrived, out, down, sems):
    down_product(hidden, down, load(weights, 1, down, sems), out, arrived)


def kv_kernel(core, terms, rows, gain, same, other, out, held, sems):
    chips = same.shape[0]
    copies = []
    for index in range(2 * chips):
        source = (same, other)[index // chips].at[index % chips]
        copies.append(pltpu.make_async_copy(source, held.at[index], sems.at[index]))
    for copy in copies:
        copy.start()
    mixed = jnp.sum(terms[...].astype(jnp.float32), axis=0)
    state = rows[...].astype(jnp.float32) + mixed
    kv_in = scale_rows(state, gain[...].astype(jnp.float32)).astype(jnp.bfloat16)
    for index, copy in enumerate(copies):
        copy.wait()
        made = jnp.dot(kv_in, held[index], preferred_element_type=jnp.float32)
        parity = core[0] if index < chips else 1 - core[0]
        head = 2 * (index % chips) + parity
        out[head, :, :HS] = unit_rows(made[:, :HS]).astype(jnp.bfloat16)
        out[head, :, HS:] = made[:, HS:].astype(jnp.bfloat16)


def call(kernel, name, shape, in_specs, args, flops, scratch, limit=None):
    moved = math.prod(shape) + sum(arg.size for arg in args)
    return pl.pallas_call(
        kernel,
        out_shape=jax.ShapeDtypeStruct(shape, jnp.bfloat16),
        in_specs=in_specs,
        out_specs=WHOLE,
        scratch_shapes=scratch,
        compiler_params=pltpu.CompilerParams(vmem_limit_bytes=limit),
        cost_estimate=pl.CostEstimate(flops=flops, bytes_accessed=2 * moved, transcendentals=0),
        name=name,
    )(*args)


def on_device(
    patch_states,
    mlp_gain,
    up_weight,
    down_weight,
    kv_gain,
    kv_weight,
    byte_states,
    query_weight,
    out_weight,
    patch_counts,
    byte_patch,
):
    rows, features = patch_states.shape
    n_mp = lax.axis_size("mp")
    me = lax.axis_index("mp")
    core = lax.rem(me, 2)
    chips = n_mp // 2
    own = rows // n_mp
    same_core = [list(range(parity, n_mp, 2)) for parity in range(2)]
    core_swap = [(source, source ^ 1) for source in range(n_mp)]

    joined = jnp.concatenate([up_weight, down_weight.T], axis=0)
    with jax.named_scope("gather_w"):
        weights_all = lax.all_gather(joined, "seq", axis=0, tiled=True).reshape(
        lax.axis_size("seq"), 2, up_weight.shape[0], up_weight.shape[1]
    )

    with jax.named_scope("spread_kv"):
        kv_same = spread(kv_weight, same_core)
    with jax.named_scope("swap_kv"):
        kv_other = lax.ppermute(kv_same, "mp", core_swap)
    with jax.named_scope("spread_out"):
        out_all = spread(out_weight)

    depth_back = (WIN + rows // 2 - 2) // (rows // 2)
    own_count = patch_counts[0]
    with jax.named_scope("counts"):
        prior = [from_behind(patch_counts, k) for k in range(1, depth_back + 1)]

    with jax.named_scope("queries"):
        queries = unit_rows(
            jnp.dot(byte_states, query_weight, preferred_element_type=jnp.float32)
        ).astype(jnp.bfloat16)

    by_core = patch_states.reshape(chips, 2, own, features)
    mlp_scale = mlp_gain.astype(jnp.float32)

    def normed_half(parity):
        half = lax.dynamic_index_in_dim(by_core, parity, 1, keepdims=False).reshape(-1, features)
        return scale_rows(half.astype(jnp.float32), mlp_scale).astype(jnp.bfloat16)

    early = (jnp.concatenate(prior), kv_same, kv_other, out_all, queries)
    half_rows, width, parts = rows // 2, up_weight.shape[1], 4
    flops = 2 * half_rows * features * width
    stored = pltpu.VMEM(weights_all.shape[:1] + weights_all.shape[2:], jnp.bfloat16)
    preact = pltpu.VMEM((half_rows, width), jnp.float32)
    sems = pltpu.SemaphoreType.DMA((parts,))
    theirs = call(
        functools.partial(first_kernel, len(early)),
        "feed_forward_first",
        (half_rows, features),
        [WHOLE, ANYWHERE, SCALARS] + [ANYWHERE] * (len(early) - 1),
        (normed_half(1 - core), weights_all) + early,
        2 * flops,
        [stored, stored, preact, pltpu.VMEM((half_rows, width), jnp.bfloat16), sems, sems],
    )
    arrived = lax.ppermute(theirs, "mp", core_swap)
    hidden = call(
        up_kernel,
        "feed_forward_up",
        (half_rows, width),
        [WHOLE, ANYWHERE],
        (normed_half(core), weights_all),
        flops,
        [stored, preact, sems],
    )
    paired = call(
        down_kernel,
        "feed_forward_down",
        (half_rows, features),
        [WHOLE, ANYWHERE, WHOLE],
        (hidden, weights_all, arrived),
        flops,
        [stored, sems],
    )
    terms = lax.all_to_all(
        paired.reshape(chips, own, features), "mp", 0, 0, axis_index_groups=same_core
    )

    by_head = call(
        kv_kernel,
        "keys_values",
        (n_mp, own, 2 * HS),
        [SCALARS, WHOLE, WHOLE, WHOLE, ANYWHERE, ANYWHERE],
        (
            core.astype(jnp.int32).reshape(1),
            terms,
            lax.dynamic_slice_in_dim(patch_states, me * own, own, 0),
            kv_gain.reshape(1, features),
            kv_same,
            kv_other,
        ),
        2 * own * features * 2 * HS * n_mp,
        [
            pltpu.VMEM((n_mp, features, 2 * HS), jnp.bfloat16),
            pltpu.SemaphoreType.DMA((n_mp,)),
        ],
        limit=24 * 2**20,
    )
    kv_pack = lax.all_to_all(by_head, "mp", 0, 0).reshape(rows, 2 * HS)

    c1, c2, c3, c4 = (count[0] for count in prior)
    before2 = from_behind(kv_pack, 2)
    before1 = from_behind(kv_pack, 1)
    slot = jnp.arange(rows, dtype=jnp.int32)
    source = slot[:, None] + (c1 - rows)
    pick2 = (slot[None, :] == source + c2) & (source < 0)
    pick1 = slot[None, :] == source
    packed = jnp.dot(
        jnp.concatenate([pick2, pick1], axis=1).astype(jnp.bfloat16),
        jnp.concatenate([before2, before1], axis=0),
        preferred_element_type=jnp.float32,
    ).astype(jnp.bfloat16)
    before34 = from_behind(packed, 2)
    blocks = [
        (kv_pack, slot, slot < own_count),
        (before1, slot - c1, slot < c1),
        (before2, slot - (c1 + c2), slot < c2),
        (before34, slot - (c1 + c2 + rows), slot >= rows - (c3 + c4)),
    ]

    score_scale = 2.0 / math.sqrt(HS)
    numerator = denominator = 0.0
    for kv_block, key_ids, live in blocks:
        usable = (
            live[None, :]
            & (key_ids[None, :] <= byte_patch[:, None])
            & (key_ids[None, :] > byte_patch[:, None] - WIN)
        )
        scores = (
            lax.dot_general(
                queries,
                kv_block[:, :HS],
                (((1,), (1,)), ((), ())),
                preferred_element_type=jnp.float32,
            )
            * score_scale
        )
        weights = jnp.where(usable, jnp.exp(scores), 0.0)
        numerator = numerator + jnp.dot(
            weights.astype(jnp.bfloat16), kv_block[:, HS:], preferred_element_type=jnp.float32
        )
        denominator = denominator + jnp.sum(weights, axis=-1)
    attended = (numerator / denominator[:, None]).astype(jnp.bfloat16)

    bytes_own = attended.shape[0] // n_mp
    gathered = lax.all_to_all(attended.reshape(n_mp, bytes_own, HS), "mp", 0, 0)
    return jnp.einsum(
        "hrd,hdo->ro", gathered, out_all, preferred_element_type=jnp.float32
    ).astype(jnp.bfloat16)


def solution(mesh):
    in_specs = (
        P("seq", None),
        P(),
        P("seq", "mp"),
        P("mp", "seq"),
        P(),
        P(None, "mp"),
        P("seq", None),
        P(None, "mp"),
        P("mp", None),
        P("seq"),
        P("seq"),
    )
    return jax.shard_map(
        on_device,
        mesh=mesh,
        in_specs=in_specs,
        out_specs=P(("seq", "mp"), None),
        check_vma=False,
    )
```

time: 234 us -> 243 us (1.038)
  the two profiles are of different devices: /device:TPU:32 before, /device:TPU:24 now
where the time goes in v4:
time: 243 us; the launch traced here: 241 us
  blocking collectives  63 us (26%)
  waiting for transfers between devices  53.8 us (22%)
  starting transfers between devices  51.7 us (21%)
  Pallas kernels  23.5 us (10%)
  between operations  17.7 us (7%)
  other arithmetic  14.7 us (6%)
  matrix products  11 us (5%)
  local copies, waits for them, and re-layouts  6.11 us (3%)
    all_to_all x1, blocking collectives, spread(): return lax.all_to_all(copies, 'mp', 0, 0, axis_index_groups=groups)  53.1 us
    ppermute x7, starting transfers between devices, from_behind(): lax.ppermute(value, 'seq', [(source, source + steps) for source in range(...  36.6 us
    pallas_call x4, Pallas kernels, call(): pl.pallas_call(kernel, out_shape=jax.ShapeDtypeStruct(shape, jnp.bfloat16...  23.5 us
    ppermute x7, waiting for transfers between devices, from_behind(): lax.ppermute(value, 'seq', [(source, source + steps) for source in range(...  20.7 us
    all_to_all x1, waiting for transfers between devices, spread(): return lax.all_to_all(copies, 'mp', 0, 0, axis_index_groups=groups)  15.7 us
    all_to_all x1, waiting for transfers between devices, on_device(): lax.all_to_all(paired.reshape(chips, own, features), 'mp', 0, 0, axis_ind...  10.3 us
    all_to_all x1, blocking collectives, on_device(): gathered = lax.all_to_all(attended.reshape(n_mp, bytes_own, HS), 'mp', 0, 0)  9.91 us
    all_to_all x1, waiting for transfers between devices, on_device(): kv_pack = lax.all_to_all(by_head, 'mp', 0, 0).reshape(rows, 2 * HS)  7.04 us
  transfers between devices with their start and end apart: 13, of which 6 were waited for; matrix products, arithmetic and copies ran while one was open for 10% of the time, Pallas kernels for 2%

profile of v4, /device:TPU:24, one launch (start us, length us, event | category | flops | bytes accessed | tf_op | source)
XLA Modules:
  0.0 241.5 jit_solution(18303289033053983313)
XLA Ops:
  6.5 1.7 pad_maximum_fusion
  8.2 0.0 all-gather.2.cloned.1.call-update
  8.2 1.5 broadcast_in_dim.10
  9.7 0.0 copy-start.4
  9.7 53.1 %all_to_all.25.rest_1_.same = bf16[4,2048,256]{2,1,0:T(8,128)(2,1)} all-to-all(bf16[4,2048,256]{2,1,0:T(8,128)(2,1)S(1)} %broadcast_in_dim.10), channel_id=1, replica_groups={{0,2,4,6},{1,3,5,7},{8,10,12,14},{9,11,13,15},{16,18,20,22},{17,19,21,2..., dimensions={0} | all-to-all | bytes 8388608 | tf_op jit(solution)/shard_map/spread_kv/all_to_all | solution.py:31
  62.9 1.9 collective-permute-start.4
  64.8 6.1 %collective-permute-start.1 = (s32[1]{0:T(128)}, s32[1]{0:T(128)}, u32[]{:S(2)}, u32[]{:S(2)}) collective-permute-start(s32[1]{0:T(128)} %param.20), channel_id=1, source_target_pairs={{0,16},{8,24},{16,32},{24,40},{32,48},{40,56},{48,64},{56,72},{64,... | collective-permute-start | bytes 20 | tf_op jit(solution)/shard_map/counts/ppermute | solution.py:25
  70.9 4.3 %collective-permute-start = (s32[1]{0:T(128)}, s32[1]{0:T(128)}, u32[]{:S(2)}, u32[]{:S(2)}) collective-permute-start(s32[1]{0:T(128)} %param.20), channel_id=1, source_target_pairs={{0,8},{8,16},{16,24},{24,32},{32,40},{40,48},{48,56},{56,64},{64,7... | collective-permute-start | bytes 20 | tf_op jit(solution)/shard_map/counts/ppermute | solution.py:25
  75.2 8.2 %collective-permute-start.3 = (s32[1]{0:T(128)}, s32[1]{0:T(128)}, u32[]{:S(2)}, u32[]{:S(2)}) collective-permute-start(s32[1]{0:T(128)} %param.20), channel_id=1, source_target_pairs={{0,32},{8,40},{16,48},{24,56},{32,64},{40,72},{48,80},{56,88},{64,... | collective-permute-start | bytes 20 | tf_op jit(solution)/shard_map/counts/ppermute | solution.py:25
  83.4 1.9 collective-permute-start.2
  85.4 1.6 broadcast_in_dim.11
  87.0 4.4 %all-to-all-start.1 = ((bf16[8,128,1024]{2,1,0:T(8,128)(2,1)}), bf16[8,128,1024]{2,1,0:T(8,128)(2,1)}, u32[]{:S(2)}, u32[]{:S(2)}) async-start(bf16[8,128,1024]{2,1,0:T(8,128)(2,1)} %broadcast_in_dim.11), calls=%async_computation.1 | async-start | bytes 4194304 | tf_op jit(solution)/shard_map/spread_out/all_to_all | solution.py:31
  91.3 0.0 copy-start.6
  91.3 0.0 copy-start.5
  91.4 2.1 multiply_reduce_fusion
  93.5 0.1 rsqrt.34
  93.6 0.1 rsqrt.32
  93.7 0.8 multiply_reduce_fusion.2
  94.5 0.2 copy.12
  94.7 0.9 multiply_convert_fusion.rest_4_
  95.7 2.1 bitcast_convert_fusion
  97.8 1.8 fusion.1
  99.5 0.0 collective-permute-done.1
  99.5 0.0 collective-permute-done
  99.6 0.0 collective-permute-done.2
  99.6 3.2 %pad_add_fusion.rest_0_ = s32[4]{0:T(128)} fusion(s32[1]{0:T(128)} %collective-permute-done.3, s32[1]{0:T(128)} %collective-permute-done.2, s32[1]{0:T(128)} %collective-permute-done.1, s32[1]{0:T(128)} %collective-permute-done), kind=kLoop, calls=%fused_computation.69 | loop fusion | flops 12 | bytes 32 | tf_op jit(solution)/shard_map/concatenate | solution.py:197
  102.8 15.7 %all-to-all-done.1.rest_3_ = bf16[8,128,1024]{2,1,0:T(8,128)(2,1)} async-done(((bf16[8,128,1024]{2,1,0:T(8,128)(2,1)}), bf16[8,128,1024]{2,1,0:T(8,128)(2,1)}, u32[]{:S(2)}, u32[]{:S(2)}) %all-to-all-start.1) | async-done | bytes 2097184 | tf_op jit(solution)/shard_map/spread_out/all_to_all | solution.py:31
  118.5 0.0 collective-permute-done.4.rest_2_.other
  118.5 7.5 %feed_forward_first.1 = bf16[256,2048]{1,0:T(8,128)(2,1)} custom-call(bf16[256,2048]{1,0:T(8,128)(2,1)} %get-tuple-element.9.normed, bf16[64,2,32,896]{3,2,1,0:T(8,128)(2,1)} %bitcast.48, s32[4]{0:T(128)} %pad_add_fusion.rest_0_, bf16[4,2048,256]{2,1,0:T(8,128)(2,1)} %all_to_all.25.rest_1_.same, bf16[4,2048,256]{2,1,0:T(8,128)(2,1)} %collective-permute-done.4.rest_2_.other, ...), custom_call_target="tpu_custom_call" | custom-call | flops 1879048192 | bytes 20185096 | tf_op jit(solution)/shard_map/feed_forward_first/pallas_call | solution.py:133
  126.0 1.9 collective-permute-start.5
  128.7 1.0 constant_dynamic-slice_fusion.rows
  129.6 5.0 %feed_forward_up.1.hidden = bf16[256,896]{1,0:T(8,128)(2,1)} custom-call(bf16[256,2048]{1,0:T(8,128)(2,1)} %get-tuple-element.10.normed, bf16[64,2,32,896]{3,2,1,0:T(8,128)(2,1)} %bitcast.49), custom_call_target="tpu_custom_call" | custom-call | flops 939524096 | bytes 8847360 | tf_op jit(solution)/shard_map/feed_forward_up/pallas_call | solution.py:133
  134.6 0.0 collective-permute-done.5.arrived
  134.6 1.0 copy-done.3
  135.6 5.5 %feed_forward_down.1 = bf16[256,2048]{1,0:T(8,128)(2,1)} custom-call(bf16[256,896]{1,0:T(8,128)(2,1)} %feed_forward_up.1.hidden, bf16[64,2,32,896]{3,2,1,0:T(8,128)(2,1)} %bitcast.50, bf16[256,2048]{1,0:T(8,128)(2,1)} %copy-done.3), custom_call_target="tpu_custom_call" | custom-call | flops 939524096 | bytes 9895936 | tf_op jit(solution)/shard_map/feed_forward_down/pallas_call | solution.py:133
  141.1 3.5 %all-to-all-start.2 = ((bf16[4,64,2048]{2,1,0:T(8,128)(2,1)}), bf16[4,64,2048]{2,1,0:T(8,128)(2,1)S(1)}, u32[]{:S(2)}, u32[]{:S(2)}) async-start(bf16[4,64,2048]{2,1,0:T(8,128)(2,1)} %bitcast.53), calls=%async_computation.2 | async-start | bytes 2097152 | tf_op jit(solution)/shard_map/all_to_all | solution.py:231
  144.6 0.7 iota_compare_fusion.5
  148.4 0.6 iota_compare_fusion.6
  149.0 0.7 fusion.36
  149.7 0.6 iota_subtract_fusion.2
  150.3 10.3 %all-to-all-done.2.terms = bf16[4,64,2048]{2,1,0:T(8,128)(2,1)S(1)} async-done(((bf16[4,64,2048]{2,1,0:T(8,128)(2,1)}), bf16[4,64,2048]{2,1,0:T(8,128)(2,1)S(1)}, u32[]{:S(2)}, u32[]{:S(2)}) %all-to-all-start.2) | async-done | bytes 1048608 | tf_op jit(solution)/shard_map/all_to_all | solution.py:231
  160.6 5.6 %keys_values.1 = bf16[8,64,256]{2,1,0:T(8,128)(2,1)S(1)} custom-call(s32[1]{0:T(128)} %bitcast.1.core, bf16[4,64,2048]{2,1,0:T(8,128)(2,1)S(1)} %all-to-all-done.2.terms, bf16[64,2048]{1,0:T(8,128)(2,1)S(1)} %constant_dynamic-slice_fusion.rows, bf16[1,2048]{1,0:T(2,128)(2,1)S(1)} %reshape.138.gain, bf16[4,2048,256]{2,1,0:T(8,128)(2,1)} %all_to_all.25.rest_1_.same, ...), custom_call_target="tpu_custom_call" | custom-call | flops 536870912 | bytes 9965570 | tf_op jit(solution)/shard_map/keys_values/pallas_call | solution.py:133
  166.2 0.7 copy-done.1
  166.9 3.4 %all-to-all-start.3 = ((bf16[8,64,256]{2,1,0:T(8,128)(2,1)}), bf16[8,64,256]{2,1,0:T(8,128)(2,1)S(1)}, u32[]{:S(2)}, u32[]{:S(2)}) async-start(bf16[8,64,256]{2,1,0:T(8,128)(2,1)} %copy-done.1), calls=%async_computation.3 | async-start | bytes 524288 | tf_op jit(solution)/shard_map/all_to_all | solution.py:255
  170.3 0.4 iota_compare_fusion.2
  170.7 7.0 %all-to-all-done.3 = bf16[8,64,256]{2,1,0:T(8,128)(2,1)S(1)} async-done(((bf16[8,64,256]{2,1,0:T(8,128)(2,1)}), bf16[8,64,256]{2,1,0:T(8,128)(2,1)S(1)}, u32[]{:S(2)}, u32[]{:S(2)}) %all-to-all-start.3) | async-done | bytes 262176 | tf_op jit(solution)/shard_map/all_to_all | solution.py:255
  177.7 7.3 %collective-permute-start.7 = (bf16[512,256]{1,0:T(8,128)(2,1)S(1)}, bf16[512,256]{1,0:T(8,128)(2,1)S(1)}, u32[]{:S(2)}, u32[]{:S(2)}) collective-permute-start(bf16[512,256]{1,0:T(8,128)(2,1)S(1)} %bitcast.54), channel_id=1, source_target_pairs={{0,16},{8,24},{16,32},{24,40},{32,48},{40,56},{48,64},{56,72},{64,... | collective-permute-start | bytes 786440 | tf_op jit(solution)/shard_map/ppermute | solution.py:25
  185.0 3.6 %collective-permute-start.6 = (bf16[512,256]{1,0:T(8,128)(2,1)S(1)}, bf16[512,256]{1,0:T(8,128)(2,1)S(1)}, u32[]{:S(2)}, u32[]{:S(2)}) collective-permute-start(bf16[512,256]{1,0:T(8,128)(2,1)S(1)} %bitcast.55), channel_id=1, source_target_pairs={{0,8},{8,16},{16,24},{24,32},{32,40},{40,48},{48,56},{56,64},{64,7... | collective-permute-start | bytes 786440 | tf_op jit(solution)/shard_map/ppermute | solution.py:25
  188.6 2.0 fusion.41
  190.6 0.0 copy-start.2
  190.6 5.8 %collective-permute-done.7 = bf16[512,256]{1,0:T(8,128)(2,1)S(1)} collective-permute-done((bf16[512,256]{1,0:T(8,128)(2,1)S(1)}, bf16[512,256]{1,0:T(8,128)(2,1)S(1)}, u32[]{:S(2)}, u32[]{:S(2)}) %collective-permute-start.7) | collective-permute-done | bytes 262176 | tf_op jit(solution)/shard_map/ppermute | solution.py:25
  196.4 5.1 %collective-permute-done.6 = bf16[512,256]{1,0:T(8,128)(2,1)S(1)} collective-permute-done((bf16[512,256]{1,0:T(8,128)(2,1)S(1)}, bf16[512,256]{1,0:T(8,128)(2,1)S(1)}, u32[]{:S(2)}, u32[]{:S(2)}) %collective-permute-start.6) | collective-permute-done | bytes 262176 | tf_op jit(solution)/shard_map/ppermute | solution.py:25
  201.5 0.4 fusion.14
  202.0 5.2 %collective-permute-start.8 = (bf16[512,256]{1,0:T(8,128)(2,1)S(1)}, bf16[512,256]{1,0:T(8,128)(2,1)S(1)}, u32[]{:S(2)}, u32[]{:S(2)}) collective-permute-start(bf16[512,256]{1,0:T(8,128)(2,1)S(1)} %fusion.14), channel_id=1, source_target_pairs={{0,16},{8,24},{16,32},{24,40},{32,48},{40,56},{48,64},{56,72},{64,... | collective-permute-start | bytes 786440 | tf_op jit(solution)/shard_map/ppermute | solution.py:25
  207.2 1.0 fusion.42
  208.2 0.5 fusion.20
  208.6 0.5 convolution_add_fusion.1
  209.1 1.0 fusion.40
  210.1 9.8 %collective-permute-done.8 = bf16[512,256]{1,0:T(8,128)(2,1)S(1)} collective-permute-done((bf16[512,256]{1,0:T(8,128)(2,1)S(1)}, bf16[512,256]{1,0:T(8,128)(2,1)S(1)}, u32[]{:S(2)}, u32[]{:S(2)}) %collective-permute-start.8) | collective-permute-done | bytes 262176 | tf_op jit(solution)/shard_map/ppermute | solution.py:25
  220.0 1.0 fusion.39
  221.0 0.5 fusion.17
  221.5 0.5 fusion.13
  222.0 9.9 %all_to_all.26 = bf16[8,128,128]{2,1,0:T(8,128)(2,1)S(1)} all-to-all(bf16[8,128,128]{2,1,0:T(8,128)(2,1)S(1)} %bitcast.58), channel_id=1, replica_groups=mesh['seq'=64,'mp'=8] {'mp'}, dimensions={0} | all-to-all | bytes 524288 | tf_op jit(solution)/shard_map/all_to_all | solution.py:302
  231.9 2.7 %fusion.12 = bf16[128,1024]{1,0:T(8,128)(2,1)} fusion(bf16[8,128,128]{2,1,0:T(8,128)(2,1)S(1)} %all_to_all.26, bf16[8,128,1024]{2,1,0:T(8,128)(2,1)} %all-to-all-done.1.rest_3_), kind=kOutput, calls=%fused_computation.25 | convolution fusion | flops 268566528 | bytes 2621440 | tf_op jit(solution)/shard_map/hrd,hdo->ro/dot_general | solution.py:303
  (27 shorter events, 0.1 us)
Async XLA Ops:
  6.5 87.2 %copy-start = (bf16[1024,1024]{1,0:T(8,128)(2,1)S(1)}, bf16[1024,1024]{1,0:T(8,128)(2,1)}, u32[]{:S(2)}) copy-start(bf16[1024,1024]{1,0:T(8,128)(2,1)} %param.17) | copy-start | bytes 6291460
  6.5 112.0 %all-gather.2.cloned.1.call-start = ((), (), s32[]{:S(2)}) async-start(), calls=%async_computation.5 | async-start | bytes 7454720 | tf_op jit(solution)/shard_map/gather_w/all_gather | solution.py:169
  9.7 75.6 %copy-start.4 = (bf16[128,1024]{1,0:T(8,128)(2,1)S(1)}, bf16[128,1024]{1,0:T(8,128)(2,1)}, u32[]{:S(2)}) copy-start(bf16[128,1024]{1,0:T(8,128)(2,1)} %param.19) | copy-start | bytes 786436
  62.9 55.6 %collective-permute-start.4 = (bf16[4,2048,256]{2,1,0:T(8,128)(2,1)}, bf16[4,2048,256]{2,1,0:T(8,128)(2,1)}, u32[]{:S(2)}, u32[]{:S(2)}) collective-permute-start(bf16[4,2048,256]{2,1,0:T(8,128)(2,1)} %all_to_all.25.rest_1_.same), channel_id=1, source_target_pairs={{0,1},{1,0},{2,3},{3,2},{4,5},{5,4},{6,7},{7,6},{8,9},{9,8},{10,11... | collective-permute-start | bytes 12582920 | tf_op jit(solution)/shard_map/swap_kv/ppermute | solution.py:176
  64.8 34.8 %collective-permute-start.1 = (s32[1]{0:T(128)}, s32[1]{0:T(128)}, u32[]{:S(2)}, u32[]{:S(2)}) collective-permute-start(s32[1]{0:T(128)} %param.20), channel_id=1, source_target_pairs={{0,16},{8,24},{16,32},{24,40},{32,48},{40,56},{48,64},{56,72},{64,... | collective-permute-start | bytes 20 | tf_op jit(solution)/shard_map/counts/ppermute | solution.py:25
  70.9 28.7 %collective-permute-start = (s32[1]{0:T(128)}, s32[1]{0:T(128)}, u32[]{:S(2)}, u32[]{:S(2)}) collective-permute-start(s32[1]{0:T(128)} %param.20), channel_id=1, source_target_pairs={{0,8},{8,16},{16,24},{24,32},{32,40},{40,48},{48,56},{56,64},{64,7... | collective-permute-start | bytes 20 | tf_op jit(solution)/shard_map/counts/ppermute | solution.py:25
  75.2 24.4 %collective-permute-start.3 = (s32[1]{0:T(128)}, s32[1]{0:T(128)}, u32[]{:S(2)}, u32[]{:S(2)}) collective-permute-start(s32[1]{0:T(128)} %param.20), channel_id=1, source_target_pairs={{0,32},{8,40},{16,48},{24,56},{32,64},{40,72},{48,80},{56,88},{64,... | collective-permute-start | bytes 20 | tf_op jit(solution)/shard_map/counts/ppermute | solution.py:25
  83.4 16.1 %collective-permute-start.2 = (s32[1]{0:T(128)}, s32[1]{0:T(128)}, u32[]{:S(2)}, u32[]{:S(2)}) collective-permute-start(s32[1]{0:T(128)} %param.20), channel_id=1, source_target_pairs={{0,24},{8,32},{16,40},{24,48},{32,56},{40,64},{48,72},{56,80},{64,... | collective-permute-start | bytes 20 | tf_op jit(solution)/shard_map/counts/ppermute | solution.py:25
  87.0 31.5 %all-to-all-start.1 = ((bf16[8,128,1024]{2,1,0:T(8,128)(2,1)}), bf16[8,128,1024]{2,1,0:T(8,128)(2,1)}, u32[]{:S(2)}, u32[]{:S(2)}) async-start(bf16[8,128,1024]{2,1,0:T(8,128)(2,1)} %broadcast_in_dim.11), calls=%async_computation.1 | async-start | bytes 4194304 | tf_op jit(solution)/shard_map/spread_out/all_to_all | solution.py:31
  91.3 2.3 copy-start.6
  91.3 2.3 copy-start.5
  118.5 10.1 %copy-start.7 = (bf16[2048]{0:T(1024)(128)(2,1)S(1)}, bf16[2048]{0:T(1024)(128)(2,1)}, u32[]{:S(2)}) copy-start(bf16[2048]{0:T(1024)(128)(2,1)} %param.15) | copy-start | bytes 12292
  118.5 10.1 %copy-start.8 = (s32[1024]{0:T(1024)S(1)}, s32[1024]{0:T(1024)}, u32[]{:S(2)}) copy-start(s32[1024]{0:T(1024)} %param.21) | copy-start | bytes 12292
  126.0 8.6 %collective-permute-start.5 = (bf16[256,2048]{1,0:T(8,128)(2,1)}, bf16[256,2048]{1,0:T(8,128)(2,1)S(1)}, u32[]{:S(2)}, u32[]{:S(2)}) collective-permute-start(bf16[256,2048]{1,0:T(8,128)(2,1)} %feed_forward_first.1), channel_id=1, source_target_pairs={{0,1},{1,0},{2,3},{3,2},{4,5},{5,4},{6,7},{7,6},{8,9},{9,8},{10,11... | collective-permute-start | bytes 3145736 | tf_op jit(solution)/shard_map/ppermute | solution.py:212
  134.6 1.0 copy-start.3
  141.1 19.5 %all-to-all-start.2 = ((bf16[4,64,2048]{2,1,0:T(8,128)(2,1)}), bf16[4,64,2048]{2,1,0:T(8,128)(2,1)S(1)}, u32[]{:S(2)}, u32[]{:S(2)}) async-start(bf16[4,64,2048]{2,1,0:T(8,128)(2,1)} %bitcast.53), calls=%async_computation.2 | async-start | bytes 2097152 | tf_op jit(solution)/shard_map/all_to_all | solution.py:231
  166.2 0.7 copy-start.1
  166.9 10.8 %all-to-all-start.3 = ((bf16[8,64,256]{2,1,0:T(8,128)(2,1)}), bf16[8,64,256]{2,1,0:T(8,128)(2,1)S(1)}, u32[]{:S(2)}, u32[]{:S(2)}) async-start(bf16[8,64,256]{2,1,0:T(8,128)(2,1)} %copy-done.1), calls=%async_computation.3 | async-start | bytes 524288 | tf_op jit(solution)/shard_map/all_to_all | solution.py:255
  177.7 18.7 %collective-permute-start.7 = (bf16[512,256]{1,0:T(8,128)(2,1)S(1)}, bf16[512,256]{1,0:T(8,128)(2,1)S(1)}, u32[]{:S(2)}, u32[]{:S(2)}) collective-permute-start(bf16[512,256]{1,0:T(8,128)(2,1)S(1)} %bitcast.54), channel_id=1, source_target_pairs={{0,16},{8,24},{16,32},{24,40},{32,48},{40,56},{48,64},{56,72},{64,... | collective-permute-start | bytes 786440 | tf_op jit(solution)/shard_map/ppermute | solution.py:25
  185.0 16.5 %collective-permute-start.6 = (bf16[512,256]{1,0:T(8,128)(2,1)S(1)}, bf16[512,256]{1,0:T(8,128)(2,1)S(1)}, u32[]{:S(2)}, u32[]{:S(2)}) collective-permute-start(bf16[512,256]{1,0:T(8,128)(2,1)S(1)} %bitcast.55), channel_id=1, source_target_pairs={{0,8},{8,16},{16,24},{24,32},{32,40},{40,48},{48,56},{56,64},{64,7... | collective-permute-start | bytes 786440 | tf_op jit(solution)/shard_map/ppermute | solution.py:25
  190.6 16.6 %copy-start.2 = (bf16[1024,128]{1,0:T(8,128)(2,1)S(1)}, bf16[1024,128]{1,0:T(8,128)(2,1)}, u32[]{:S(2)}) copy-start(bf16[1024,128]{1,0:T(8,128)(2,1)} %multiply_convert_fusion.rest_4_) | copy-start | bytes 786436
  202.0 18.0 %collective-permute-start.8 = (bf16[512,256]{1,0:T(8,128)(2,1)S(1)}, bf16[512,256]{1,0:T(8,128)(2,1)S(1)}, u32[]{:S(2)}, u32[]{:S(2)}) collective-permute-start(bf16[512,256]{1,0:T(8,128)(2,1)S(1)} %fusion.14), channel_id=1, source_target_pairs={{0,16},{8,24},{16,32},{24,40},{32,48},{40,56},{48,64},{56,72},{64,... | collective-permute-start | bytes 786440 | tf_op jit(solution)/shard_map/ppermute | solution.py:25
Sparse Core Ops, SparseCore 0:
  10.4 99.0 all-gather.1

commit v5 on v4

--- a/solution.py
+++ b/solution.py
@@ -5,6 +5,7 @@
 import jax.numpy as jnp
 from jax import lax
 from jax.sharding import PartitionSpec as P
+
 from jax.experimental import pallas as pl
 from jax.experimental.pallas import tpu as pltpu
 
@@ -64,48 +65,34 @@
     return copies
 
 
-def up_product(normed, up, copies, preact):
-    each, wide = up.shape[0] // len(copies), normed.shape[1] // len(copies)
-    for part, copy in enumerate(copies):
-        copy.wait()
-        product = jnp.dot(
-            normed[:, part * wide : (part + 1) * wide],
-            flat(up[part * each : (part + 1) * each]),
-            preferred_element_type=jnp.float32,
-        )
-        if part == 0:
-            preact[...] = product
-        else:
-            preact[...] += product
-
-
-def down_product(hidden, down, copies, out, added=None):
-    each, wide = down.shape[0] // len(copies), out.shape[1] // len(copies)
-    for part, copy in enumerate(copies):
-        copy.wait()
-        span = slice(part * wide, (part + 1) * wide)
-        made = dot_rows(hidden[...], flat(down[part * each : (part + 1) * each]))
-        if added is not None:
-            made = made + added[:, span].astype(jnp.float32)
-        out[:, span] = made.astype(out.dtype)
-
-
-def first_kernel(n_early, normed, weights, *rest):
-    out, up, down, preact, hidden, up_sems, down_sems = rest[n_early:]
+def feed_forward_kernel(n_early, normed, weights, *rest):
+    theirs, mine, rows, up, down, hidden, row_sem, up_sems, down_sems = rest[n_early:]
+    row_copy = pltpu.make_async_copy(normed, rows, row_sem)
+    row_copy.start()
     up_copies = load(weights, 0, up, up_sems)
     down_copies = load(weights, 1, down, down_sems)
-    up_product(normed, up, up_copies, preact)
-    hidden[...] = activate(preact[...])
-    down_product(hidden, down, down_copies, out)
-
-
-def up_kernel(normed, weights, hidden, up, preact, sems):
-    up_product(normed, up, load(weights, 0, up, sems), preact)
-    hidden[...] = activate(preact[...])
-
-
-def down_kernel(hidden, weights, arrived, out, down, sems):
-    down_product(hidden, down, load(weights, 1, down, sems), out, arrived)
+    for copy in [row_copy] + up_copies:
+        copy.wait()
+    step = 256
+    for start in range(0, hidden.shape[1], step):
+        span = slice(start, min(start + step, hidden.shape[1]))
+        preact = jnp.dot(rows[...], flat(up[:, :, span]), preferred_element_type=jnp.float32)
+        hidden[:, span] = activate(preact)
+    half, features = mine.shape
+    each, wide = down.shape[0] // len(down_copies), features // len(down_copies)
+    for part, copy in enumerate(down_copies):
+        copy.wait()
+        made = dot_rows(hidden[...], flat(down[part * each : (part + 1) * each]))
+        span = slice(part * wide, (part + 1) * wide)
+        theirs[:, span] = made[:half].astype(theirs.dtype)
+        mine[:, span] = made[half:].astype(mine.dtype)
+
+
+def out_kernel(gathered, weights, out):
+    left = jnp.concatenate([gathered[head] for head in range(gathered.shape[0])], axis=1)
+    out[...] = jnp.dot(left, flat(weights[...]), preferred_element_type=jnp.float32).astype(
+        out.dtype
+    )
 
 
 def kv_kernel(core, terms, rows, gain, same, other, out, held, sems):
@@ -128,21 +115,20 @@
         out[head, :, HS:] = made[:, HS:].astype(jnp.bfloat16)
 
 
-def call(kernel, name, shape, in_specs, args, flops, scratch, limit=None):
-    moved = math.prod(shape) + sum(arg.size for arg in args)
+def call(kernel, shape, in_specs, args, flops, scratch, count=1, limit=None):
+    moved = count * math.prod(shape) + sum(arg.size for arg in args)
     return pl.pallas_call(
         kernel,
-        out_shape=jax.ShapeDtypeStruct(shape, jnp.bfloat16),
+        out_shape=[jax.ShapeDtypeStruct(shape, jnp.bfloat16)] * count,
         in_specs=in_specs,
-        out_specs=WHOLE,
+        out_specs=[WHOLE] * count,
         scratch_shapes=scratch,
         compiler_params=pltpu.CompilerParams(vmem_limit_bytes=limit),
         cost_estimate=pl.CostEstimate(flops=flops, bytes_accessed=2 * moved, transcendentals=0),
-        name=name,
     )(*args)
 
 
-def on_device(
+def block(
     patch_states,
     mlp_gain,
     up_weight,
@@ -165,76 +151,62 @@
     core_swap = [(source, source ^ 1) for source in range(n_mp)]
 
     joined = jnp.concatenate([up_weight, down_weight.T], axis=0)
-    with jax.named_scope("gather_w"):
-        weights_all = lax.all_gather(joined, "seq", axis=0, tiled=True).reshape(
+    weights_all = lax.all_gather(joined, "seq", axis=0, tiled=True).reshape(
         lax.axis_size("seq"), 2, up_weight.shape[0], up_weight.shape[1]
     )
 
-    with jax.named_scope("spread_kv"):
-        kv_same = spread(kv_weight, same_core)
-    with jax.named_scope("swap_kv"):
-        kv_other = lax.ppermute(kv_same, "mp", core_swap)
-    with jax.named_scope("spread_out"):
-        out_all = spread(out_weight)
+    kv_same = spread(kv_weight, same_core)
+    kv_other = lax.ppermute(kv_same, "mp", core_swap)
+    out_all = spread(out_weight)
 
     depth_back = (WIN + rows // 2 - 2) // (rows // 2)
     own_count = patch_counts[0]
-    with jax.named_scope("counts"):
-        prior = [from_behind(patch_counts, k) for k in range(1, depth_back + 1)]
-
-    with jax.named_scope("queries"):
-        queries = unit_rows(
-            jnp.dot(byte_states, query_weight, preferred_element_type=jnp.float32)
-        ).astype(jnp.bfloat16)
+    prior = [from_behind(patch_counts, k) for k in range(1, depth_back + 1)]
+
+    queries = unit_rows(
+        jnp.dot(byte_states, query_weight, preferred_element_type=jnp.float32)
+    ).astype(jnp.bfloat16)
 
     by_core = patch_states.reshape(chips, 2, own, features)
     mlp_scale = mlp_gain.astype(jnp.float32)
 
-    def normed_half(parity):
-        half = lax.dynamic_index_in_dim(by_core, parity, 1, keepdims=False).reshape(-1, features)
-        return scale_rows(half.astype(jnp.float32), mlp_scale).astype(jnp.bfloat16)
-
+    halves = [
+        lax.dynamic_index_in_dim(by_core, parity, 1, keepdims=False).reshape(-1, features)
+        for parity in (1 - core, core)
+    ]
+    normed = scale_rows(jnp.concatenate(halves, axis=0).astype(jnp.float32), mlp_scale).astype(
+        jnp.bfloat16
+    )
     early = (jnp.concatenate(prior), kv_same, kv_other, out_all, queries)
     half_rows, width, parts = rows // 2, up_weight.shape[1], 4
-    flops = 2 * half_rows * features * width
     stored = pltpu.VMEM(weights_all.shape[:1] + weights_all.shape[2:], jnp.bfloat16)
-    preact = pltpu.VMEM((half_rows, width), jnp.float32)
-    sems = pltpu.SemaphoreType.DMA((parts,))
-    theirs = call(
-        functools.partial(first_kernel, len(early)),
-        "feed_forward_first",
+    theirs, mine = call(
+        functools.partial(feed_forward_kernel, len(early)),
         (half_rows, features),
-        [WHOLE, ANYWHERE, SCALARS] + [ANYWHERE] * (len(early) - 1),
-        (normed_half(1 - core), weights_all) + early,
-        2 * flops,
-        [stored, stored, preact, pltpu.VMEM((half_rows, width), jnp.bfloat16), sems, sems],
+        [ANYWHERE, ANYWHERE, SCALARS] + [ANYWHERE] * (len(early) - 1),
+        (normed, weights_all) + early,
+        4 * rows * features * width,
+        [
+            pltpu.VMEM((rows, features), jnp.bfloat16),
+            stored,
+            stored,
+            pltpu.VMEM((rows, width), jnp.bfloat16),
+            pltpu.SemaphoreType.DMA(()),
+            pltpu.SemaphoreType.DMA((parts,)),
+            pltpu.SemaphoreType.DMA((parts,)),
+        ],
+        count=2,
     )
     arrived = lax.ppermute(theirs, "mp", core_swap)
-    hidden = call(
-        up_kernel,
-        "feed_forward_up",
-        (half_rows, width),
-        [WHOLE, ANYWHERE],
-        (normed_half(core), weights_all),
-        flops,
-        [stored, preact, sems],
-    )
-    paired = call(
-        down_kernel,
-        "feed_forward_down",
-        (half_rows, features),
-        [WHOLE, ANYWHERE, WHOLE],
-        (hidden, weights_all, arrived),
-        flops,
-        [stored, sems],
+    paired = (mine.astype(jnp.float32) + arrived.astype(jnp.float32)).astype(
+        jnp.bfloat16
     )
     terms = lax.all_to_all(
         paired.reshape(chips, own, features), "mp", 0, 0, axis_index_groups=same_core
     )
 
-    by_head = call(
+    (by_head,) = call(
         kv_kernel,
-        "keys_values",
         (n_mp, own, 2 * HS),
         [SCALARS, WHOLE, WHOLE, WHOLE, ANYWHERE, ANYWHERE],
         (
@@ -300,9 +272,16 @@
 
     bytes_own = attended.shape[0] // n_mp
     gathered = lax.all_to_all(attended.reshape(n_mp, bytes_own, HS), "mp", 0, 0)
-    return jnp.einsum(
-        "hrd,hdo->ro", gathered, out_all, preferred_element_type=jnp.float32
-    ).astype(jnp.bfloat16)
+    (decoded,) = call(
+        out_kernel,
+        (bytes_own, out_all.shape[-1]),
+        [WHOLE, WHOLE],
+        (gathered, out_all),
+        2 * bytes_own * n_mp * HS * out_all.shape[-1],
+        [],
+        limit=24 * 2**20,
+    )
+    return decoded
 
 
 def solution(mesh):
@@ -320,7 +299,7 @@
         P("seq"),
     )
     return jax.shard_map(
-        on_device,
+        block,
         mesh=mesh,
         in_specs=in_specs,
         out_specs=P(("seq", "mp"), None),

time: 243 us -> 238 us (0.979)
  Pallas kernels: 23.5 us -> 19.3 us
  matrix products: 11 us -> 8.22 us
  waiting for transfers between devices: 53.8 us -> 56.5 us
    pallas_call x4 -> x3, Pallas kernels: 23.5 us -> 19.3 us  [call(): pl.pallas_call(kernel, out_shape=[jax.ShapeDtypeStruct(shape, jnp.bfloat1...]
    dot_general x11 -> x10, matrix products: 11 us -> 8.22 us  [the longest x4 4.98 us: block(): lax.dot_general(queries, kv_block[:, :HS], (((1,), (1,)), ((), ())), pref...]
  transfers between devices with their start and end apart: 13 -> 13, of which waited for: 6 -> 7; matrix products, arithmetic and copies ran while one was open for 10% -> 9% of each run, Pallas kernels for 2% -> 0%
where the time goes in v5:
time: 238 us; the launch traced here: 237 us
  blocking collectives  63 us (26%)
  waiting for transfers between devices  56.5 us (24%)
  starting transfers between devices  51.8 us (22%)
  Pallas kernels  19.3 us (8%)
  between operations  17.6 us (7%)
  other arithmetic  13.7 us (6%)
  matrix products  8.22 us (3%)
  local copies, waits for them, and re-layouts  6.86 us (3%)
    all_to_all x1, blocking collectives, spread(): return lax.all_to_all(copies, 'mp', 0, 0, axis_index_groups=groups)  53.1 us
    ppermute x7, starting transfers between devices, from_behind(): lax.ppermute(value, 'seq', [(source, source + steps) for source in range(...  36.6 us
    ppermute x7, waiting for transfers between devices, from_behind(): lax.ppermute(value, 'seq', [(source, source + steps) for source in range(...  20.7 us
    pallas_call x3, Pallas kernels, call(): pl.pallas_call(kernel, out_shape=[jax.ShapeDtypeStruct(shape, jnp.bfloat1...  19.3 us
    all_to_all x1, waiting for transfers between devices, spread(): return lax.all_to_all(copies, 'mp', 0, 0, axis_index_groups=groups)  17.7 us
    all_to_all x1, waiting for transfers between devices, block(): lax.all_to_all(paired.reshape(chips, own, features), 'mp', 0, 0, axis_ind...  9.92 us
    all_to_all x1, blocking collectives, block(): gathered = lax.all_to_all(attended.reshape(n_mp, bytes_own, HS), 'mp', 0, 0)  9.91 us
    all_to_all x1, waiting for transfers between devices, block(): kv_pack = lax.all_to_all(by_head, 'mp', 0, 0).reshape(rows, 2 * HS)  7.04 us
  transfers between devices with their start and end apart: 13, of which 7 were waited for; matrix products, arithmetic and copies ran while one was open for 9% of the time, Pallas kernels for 0%

profile of v5, /device:TPU:24, one launch (start us, length us, event | category | flops | bytes accessed | tf_op | source)
XLA Modules:
  0.0 237.2 jit_solution(3404150942789275341)
XLA Ops:
  6.5 0.0 copy-start
  6.5 0.0 all-gather.2.cloned.1.call-start
  6.5 1.7 pad_maximum_fusion.1
  8.2 0.0 all-gather.2.cloned.1.call-update
  8.2 1.5 broadcast_in_dim.10
  9.7 0.0 copy-start.3
  9.7 53.1 %all_to_all.25.rest_1_.same = bf16[4,2048,256]{2,1,0:T(8,128)(2,1)} all-to-all(bf16[4,2048,256]{2,1,0:T(8,128)(2,1)S(1)} %broadcast_in_dim.10), channel_id=1, replica_groups={{0,2,4,6},{1,3,5,7},{8,10,12,14},{9,11,13,15},{16,18,20,22},{17,19,21,2..., dimensions={0} | all-to-all | bytes 8388608 | tf_op jit(solution)/shard_map/all_to_all | solution.py:32
  62.9 1.9 collective-permute-start.4
  64.8 4.3 %collective-permute-start = (s32[1]{0:T(128)}, s32[1]{0:T(128)}, u32[]{:S(2)}, u32[]{:S(2)}) collective-permute-start(s32[1]{0:T(128)} %param.20), channel_id=1, source_target_pairs={{0,8},{8,16},{16,24},{24,32},{32,40},{40,48},{48,56},{56,64},{64,7... | collective-permute-start | bytes 20 | tf_op jit(solution)/shard_map/ppermute | solution.py:26
  69.1 6.1 %collective-permute-start.1 = (s32[1]{0:T(128)}, s32[1]{0:T(128)}, u32[]{:S(2)}, u32[]{:S(2)}) collective-permute-start(s32[1]{0:T(128)} %param.20), channel_id=1, source_target_pairs={{0,16},{8,24},{16,32},{24,40},{32,48},{40,56},{48,64},{56,72},{64,... | collective-permute-start | bytes 20 | tf_op jit(solution)/shard_map/ppermute | solution.py:26
  75.2 7.3 %collective-permute-start.2 = (s32[1]{0:T(128)}, s32[1]{0:T(128)}, u32[]{:S(2)}, u32[]{:S(2)}) collective-permute-start(s32[1]{0:T(128)} %param.20), channel_id=1, source_target_pairs={{0,24},{8,32},{16,40},{24,48},{32,56},{40,64},{48,72},{56,80},{64,... | collective-permute-start | bytes 20 | tf_op jit(solution)/shard_map/ppermute | solution.py:26
  82.5 2.9 %collective-permute-start.3 = (s32[1]{0:T(128)}, s32[1]{0:T(128)}, u32[]{:S(2)}, u32[]{:S(2)}) collective-permute-start(s32[1]{0:T(128)} %param.20), channel_id=1, source_target_pairs={{0,32},{8,40},{16,48},{24,56},{32,64},{40,72},{48,80},{56,88},{64,... | collective-permute-start | bytes 20 | tf_op jit(solution)/shard_map/ppermute | solution.py:26
  85.4 0.0 copy-done.3
  85.4 1.6 broadcast_in_dim.11
  87.0 4.5 %all-to-all-start.1 = ((bf16[8,128,1024]{2,1,0:T(8,128)(2,1)}), bf16[8,128,1024]{2,1,0:T(8,128)(2,1)}, u32[]{:S(2)}, u32[]{:S(2)}) async-start(bf16[8,128,1024]{2,1,0:T(8,128)(2,1)} %broadcast_in_dim.11), calls=%async_computation.1 | async-start | bytes 4194304 | tf_op jit(solution)/shard_map/all_to_all | solution.py:32
  91.5 0.0 copy-start.5
  91.5 0.8 multiply_reduce_fusion
  92.4 0.2 copy.12
  92.6 1.8 constant_dynamic-slice_fusion.2
  94.5 0.5 fusion
  95.0 0.9 multiply_convert_fusion.rest_4_
  95.9 1.9 fusion.2.normed
  97.8 0.0 collective-permute-done
  97.8 0.0 collective-permute-done.1
  97.8 0.0 collective-permute-done.2
  97.8 0.0 collective-permute-done.3
  97.8 3.2 %pad_add_fusion.rest_0_ = s32[4]{0:T(128)} fusion(s32[1]{0:T(128)} %collective-permute-done.3, s32[1]{0:T(128)} %collective-permute-done.2, s32[1]{0:T(128)} %collective-permute-done.1, s32[1]{0:T(128)} %collective-permute-done), kind=kLoop, calls=%fused_computation.65 | loop fusion | flops 12 | bytes 32 | tf_op jit(solution)/shard_map/concatenate | solution.py:180
  101.0 17.7 %all-to-all-done.1.rest_3_.weights = bf16[8,128,1024]{2,1,0:T(8,128)(2,1)} async-done(((bf16[8,128,1024]{2,1,0:T(8,128)(2,1)}), bf16[8,128,1024]{2,1,0:T(8,128)(2,1)}, u32[]{:S(2)}, u32[]{:S(2)}) %all-to-all-start.1) | async-done | bytes 2097184 | tf_op jit(solution)/shard_map/all_to_all | solution.py:32
  118.7 0.0 collective-permute-done.4.rest_2_.other
  118.7 11.0 %shard_map.109 = (bf16[256,2048]{1,0:T(8,128)(2,1)}, bf16[256,2048]{1,0:T(8,128)(2,1)}) custom-call(bf16[512,2048]{1,0:T(8,128)(2,1)} %fusion.2.normed, bf16[64,2,32,896]{3,2,1,0:T(8,128)(2,1)} %bitcast.32, s32[4]{0:T(128)} %pad_add_fusion.rest_0_, bf16[4,2048,256]{2,1,0:T(8,128)(2,1)} %all_to_all.25.rest_1_.same, ...), custom_call_target="tpu_custom_call" | custom-call | flops 3758096384 | bytes 22282248 | tf_op jit(solution)/shard_map/pallas_call | solution.py:120
  129.7 1.9 collective-permute-start.5
  132.3 0.0 copy-done.6
  132.4 1.0 constant_dynamic-slice_fusion.rows
  133.3 1.2 collective-permute-done.5
  134.5 2.6 %add_convert_fusion = bf16[256,2048]{1,0:T(8,128)(2,1)} fusion(bf16[256,2048]{1,0:T(8,128)(2,1)S(1)} %collective-permute-done.5, bf16[256,2048]{1,0:T(8,128)(2,1)} %get-tuple-element.7), kind=kLoop, calls=%fused_computation.10 | loop fusion | flops 2097152 | bytes 3145728 | tf_op jit(solution)/shard_map/convert_element_type | solution.py:201
  137.1 3.5 %all-to-all-start.2 = ((bf16[4,64,2048]{2,1,0:T(8,128)(2,1)}), bf16[4,64,2048]{2,1,0:T(8,128)(2,1)S(1)}, u32[]{:S(2)}, u32[]{:S(2)}) async-start(bf16[4,64,2048]{2,1,0:T(8,128)(2,1)} %bitcast.33), calls=%async_computation.2 | async-start | bytes 2097152 | tf_op jit(solution)/shard_map/all_to_all | solution.py:204
  140.6 0.7 iota_compare_fusion.5
  144.5 0.6 iota_compare_fusion.6
  145.1 0.6 iota_subtract_fusion.2
  145.6 0.7 fusion.34
  146.3 9.9 %all-to-all-done.2.terms = bf16[4,64,2048]{2,1,0:T(8,128)(2,1)S(1)} async-done(((bf16[4,64,2048]{2,1,0:T(8,128)(2,1)}), bf16[4,64,2048]{2,1,0:T(8,128)(2,1)S(1)}, u32[]{:S(2)}, u32[]{:S(2)}) %all-to-all-start.2) | async-done | bytes 1048608 | tf_op jit(solution)/shard_map/all_to_all | solution.py:204
  156.3 5.6 %shard_map.110 = bf16[8,64,256]{2,1,0:T(8,128)(2,1)S(1)} custom-call(s32[1]{0:T(128)} %bitcast.1.core, bf16[4,64,2048]{2,1,0:T(8,128)(2,1)S(1)} %all-to-all-done.2.terms, bf16[64,2048]{1,0:T(8,128)(2,1)S(1)} %constant_dynamic-slice_fusion.rows, bf16[1,2048]{1,0:T(2,128)(2,1)S(1)} %reshape.110.gain, bf16[4,2048,256]{2,1,0:T(8,128)(2,1)} %all_to_all.25.rest_1_.same, ...), custom_call_target="tpu_custom_call" | custom-call | flops 536870912 | bytes 9965570 | tf_op jit(solution)/shard_map/pallas_call | solution.py:120
  161.8 0.7 copy-done.1
  162.5 3.4 %all-to-all-start.3 = ((bf16[8,64,256]{2,1,0:T(8,128)(2,1)}), bf16[8,64,256]{2,1,0:T(8,128)(2,1)S(1)}, u32[]{:S(2)}, u32[]{:S(2)}) async-start(bf16[8,64,256]{2,1,0:T(8,128)(2,1)} %copy-done.1), calls=%async_computation.3 | async-start | bytes 524288 | tf_op jit(solution)/shard_map/all_to_all | solution.py:227
  165.9 0.4 iota_compare_fusion.2
  166.3 7.0 %all-to-all-done.3 = bf16[8,64,256]{2,1,0:T(8,128)(2,1)S(1)} async-done(((bf16[8,64,256]{2,1,0:T(8,128)(2,1)}), bf16[8,64,256]{2,1,0:T(8,128)(2,1)S(1)}, u32[]{:S(2)}, u32[]{:S(2)}) %all-to-all-start.3) | async-done | bytes 262176 | tf_op jit(solution)/shard_map/all_to_all | solution.py:227
  173.4 7.3 %collective-permute-start.7 = (bf16[512,256]{1,0:T(8,128)(2,1)S(1)}, bf16[512,256]{1,0:T(8,128)(2,1)S(1)}, u32[]{:S(2)}, u32[]{:S(2)}) collective-permute-start(bf16[512,256]{1,0:T(8,128)(2,1)S(1)} %bitcast.35), channel_id=1, source_target_pairs={{0,16},{8,24},{16,32},{24,40},{32,48},{40,56},{48,64},{56,72},{64,... | collective-permute-start | bytes 786440 | tf_op jit(solution)/shard_map/ppermute | solution.py:26
  180.7 3.4 %collective-permute-start.6 = (bf16[512,256]{1,0:T(8,128)(2,1)S(1)}, bf16[512,256]{1,0:T(8,128)(2,1)S(1)}, u32[]{:S(2)}, u32[]{:S(2)}) collective-permute-start(bf16[512,256]{1,0:T(8,128)(2,1)S(1)} %bitcast.36), channel_id=1, source_target_pairs={{0,8},{8,16},{16,24},{24,32},{32,40},{40,48},{48,56},{56,64},{64,7... | collective-permute-start | bytes 786440 | tf_op jit(solution)/shard_map/ppermute | solution.py:26
  184.1 2.0 fusion.39
  186.1 0.0 copy-start.2
  186.1 5.9 %collective-permute-done.7 = bf16[512,256]{1,0:T(8,128)(2,1)S(1)} collective-permute-done((bf16[512,256]{1,0:T(8,128)(2,1)S(1)}, bf16[512,256]{1,0:T(8,128)(2,1)S(1)}, u32[]{:S(2)}, u32[]{:S(2)}) %collective-permute-start.7) | collective-permute-done | bytes 262176 | tf_op jit(solution)/shard_map/ppermute | solution.py:26
  192.1 5.1 %collective-permute-done.6 = bf16[512,256]{1,0:T(8,128)(2,1)S(1)} collective-permute-done((bf16[512,256]{1,0:T(8,128)(2,1)S(1)}, bf16[512,256]{1,0:T(8,128)(2,1)S(1)}, u32[]{:S(2)}, u32[]{:S(2)}) %collective-permute-start.6) | collective-permute-done | bytes 262176 | tf_op jit(solution)/shard_map/ppermute | solution.py:26
  197.2 0.4 fusion.12
  197.6 5.4 %collective-permute-start.8 = (bf16[512,256]{1,0:T(8,128)(2,1)S(1)}, bf16[512,256]{1,0:T(8,128)(2,1)S(1)}, u32[]{:S(2)}, u32[]{:S(2)}) collective-permute-start(bf16[512,256]{1,0:T(8,128)(2,1)S(1)} %fusion.12), channel_id=1, source_target_pairs={{0,16},{8,24},{16,32},{24,40},{32,48},{40,56},{48,64},{56,72},{64,... | collective-permute-start | bytes 786440 | tf_op jit(solution)/shard_map/ppermute | solution.py:26
  203.0 1.0 fusion.40
  204.0 0.5 fusion.18
  204.5 0.5 convolution_add_fusion.1
  205.0 1.0 fusion.38
  206.0 9.6 %collective-permute-done.8 = bf16[512,256]{1,0:T(8,128)(2,1)S(1)} collective-permute-done((bf16[512,256]{1,0:T(8,128)(2,1)S(1)}, bf16[512,256]{1,0:T(8,128)(2,1)S(1)}, u32[]{:S(2)}, u32[]{:S(2)}) %collective-permute-start.8) | collective-permute-done | bytes 262176 | tf_op jit(solution)/shard_map/ppermute | solution.py:26
  215.6 1.0 fusion.37
  216.6 0.5 fusion.15
  217.1 0.5 fusion.11
  217.6 9.9 %all_to_all.26.gathered = bf16[8,128,128]{2,1,0:T(8,128)(2,1)S(1)} all-to-all(bf16[8,128,128]{2,1,0:T(8,128)(2,1)S(1)} %bitcast.39), channel_id=1, replica_groups=mesh['seq'=64,'mp'=8] {'mp'}, dimensions={0} | all-to-all | bytes 524288 | tf_op jit(solution)/shard_map/all_to_all | solution.py:274
  227.6 2.8 %shard_map.111 = bf16[128,1024]{1,0:T(8,128)(2,1)} custom-call(bf16[8,128,128]{2,1,0:T(8,128)(2,1)S(1)} %all_to_all.26.gathered, bf16[8,128,1024]{2,1,0:T(8,128)(2,1)} %all-to-all-done.1.rest_3_.weights), custom_call_target="tpu_custom_call" | custom-call | flops 268435456 | bytes 2621440 | tf_op jit(solution)/shard_map/pallas_call | solution.py:120
  (22 shorter events, 0.1 us)
Async XLA Ops:
  6.5 85.0 %copy-start = (bf16[1024,1024]{1,0:T(8,128)(2,1)S(1)}, bf16[1024,1024]{1,0:T(8,128)(2,1)}, u32[]{:S(2)}) copy-start(bf16[1024,1024]{1,0:T(8,128)(2,1)} %param.17) | copy-start | bytes 6291460
  6.5 112.1 %all-gather.2.cloned.1.call-start = ((), (), s32[]{:S(2)}) async-start(), calls=%async_computation.5 | async-start | bytes 7454720 | tf_op jit(solution)/shard_map/all_gather | solution.py:154
  9.7 75.6 %copy-start.3 = (bf16[128,1024]{1,0:T(8,128)(2,1)S(1)}, bf16[128,1024]{1,0:T(8,128)(2,1)}, u32[]{:S(2)}) copy-start(bf16[128,1024]{1,0:T(8,128)(2,1)} %param.19) | copy-start | bytes 786436
  62.9 55.8 %collective-permute-start.4 = (bf16[4,2048,256]{2,1,0:T(8,128)(2,1)}, bf16[4,2048,256]{2,1,0:T(8,128)(2,1)}, u32[]{:S(2)}, u32[]{:S(2)}) collective-permute-start(bf16[4,2048,256]{2,1,0:T(8,128)(2,1)} %all_to_all.25.rest_1_.same), channel_id=1, source_target_pairs={{0,1},{1,0},{2,3},{3,2},{4,5},{5,4},{6,7},{7,6},{8,9},{9,8},{10,11... | collective-permute-start | bytes 12582920 | tf_op jit(solution)/shard_map/ppermute | solution.py:159
  64.8 33.0 %collective-permute-start = (s32[1]{0:T(128)}, s32[1]{0:T(128)}, u32[]{:S(2)}, u32[]{:S(2)}) collective-permute-start(s32[1]{0:T(128)} %param.20), channel_id=1, source_target_pairs={{0,8},{8,16},{16,24},{24,32},{32,40},{40,48},{48,56},{56,64},{64,7... | collective-permute-start | bytes 20 | tf_op jit(solution)/shard_map/ppermute | solution.py:26
  69.1 28.7 %collective-permute-start.1 = (s32[1]{0:T(128)}, s32[1]{0:T(128)}, u32[]{:S(2)}, u32[]{:S(2)}) collective-permute-start(s32[1]{0:T(128)} %param.20), channel_id=1, source_target_pairs={{0,16},{8,24},{16,32},{24,40},{32,48},{40,56},{48,64},{56,72},{64,... | collective-permute-start | bytes 20 | tf_op jit(solution)/shard_map/ppermute | solution.py:26
  75.2 22.6 %collective-permute-start.2 = (s32[1]{0:T(128)}, s32[1]{0:T(128)}, u32[]{:S(2)}, u32[]{:S(2)}) collective-permute-start(s32[1]{0:T(128)} %param.20), channel_id=1, source_target_pairs={{0,24},{8,32},{16,40},{24,48},{32,56},{40,64},{48,72},{56,80},{64,... | collective-permute-start | bytes 20 | tf_op jit(solution)/shard_map/ppermute | solution.py:26
  82.5 15.3 %collective-permute-start.3 = (s32[1]{0:T(128)}, s32[1]{0:T(128)}, u32[]{:S(2)}, u32[]{:S(2)}) collective-permute-start(s32[1]{0:T(128)} %param.20), channel_id=1, source_target_pairs={{0,32},{8,40},{16,48},{24,56},{32,64},{40,72},{48,80},{56,88},{64,... | collective-permute-start | bytes 20 | tf_op jit(solution)/shard_map/ppermute | solution.py:26
  87.0 4.5 %copy-start.4 = (bf16[1024,128]{1,0:T(8,128)(2,1)S(1)}, bf16[1024,128]{1,0:T(8,128)(2,1)}, u32[]{:S(2)}) copy-start(bf16[1024,128]{1,0:T(8,128)(2,1)} %param.18) | copy-start | bytes 786436
  87.0 31.7 %all-to-all-start.1 = ((bf16[8,128,1024]{2,1,0:T(8,128)(2,1)}), bf16[8,128,1024]{2,1,0:T(8,128)(2,1)}, u32[]{:S(2)}, u32[]{:S(2)}) async-start(bf16[8,128,1024]{2,1,0:T(8,128)(2,1)} %broadcast_in_dim.11), calls=%async_computation.1 | async-start | bytes 4194304 | tf_op jit(solution)/shard_map/all_to_all | solution.py:32
  91.5 0.9 copy-start.5
  118.7 13.6 %copy-start.6 = (bf16[2048]{0:T(1024)(128)(2,1)S(1)}, bf16[2048]{0:T(1024)(128)(2,1)}, u32[]{:S(2)}) copy-start(bf16[2048]{0:T(1024)(128)(2,1)} %param.15) | copy-start | bytes 12292
  118.7 13.7 %copy-start.7 = (s32[1024]{0:T(1024)S(1)}, s32[1024]{0:T(1024)}, u32[]{:S(2)}) copy-start(s32[1024]{0:T(1024)} %param.21) | copy-start | bytes 12292
  129.7 4.8 %collective-permute-start.5 = (bf16[256,2048]{1,0:T(8,128)(2,1)}, bf16[256,2048]{1,0:T(8,128)(2,1)S(1)}, u32[]{:S(2)}, u32[]{:S(2)}) collective-permute-start(bf16[256,2048]{1,0:T(8,128)(2,1)} %get-tuple-element.8), channel_id=1, source_target_pairs={{0,1},{1,0},{2,3},{3,2},{4,5},{5,4},{6,7},{7,6},{8,9},{9,8},{10,11... | collective-permute-start | bytes 3145736 | tf_op jit(solution)/shard_map/ppermute | solution.py:200
  137.1 19.2 %all-to-all-start.2 = ((bf16[4,64,2048]{2,1,0:T(8,128)(2,1)}), bf16[4,64,2048]{2,1,0:T(8,128)(2,1)S(1)}, u32[]{:S(2)}, u32[]{:S(2)}) async-start(bf16[4,64,2048]{2,1,0:T(8,128)(2,1)} %bitcast.33), calls=%async_computation.2 | async-start | bytes 2097152 | tf_op jit(solution)/shard_map/all_to_all | solution.py:204
  161.8 0.7 copy-start.1
  162.5 10.8 %all-to-all-start.3 = ((bf16[8,64,256]{2,1,0:T(8,128)(2,1)}), bf16[8,64,256]{2,1,0:T(8,128)(2,1)S(1)}, u32[]{:S(2)}, u32[]{:S(2)}) async-start(bf16[8,64,256]{2,1,0:T(8,128)(2,1)} %copy-done.1), calls=%async_computation.3 | async-start | bytes 524288 | tf_op jit(solution)/shard_map/all_to_all | solution.py:227
  173.4 18.7 %collective-permute-start.7 = (bf16[512,256]{1,0:T(8,128)(2,1)S(1)}, bf16[512,256]{1,0:T(8,128)(2,1)S(1)}, u32[]{:S(2)}, u32[]{:S(2)}) collective-permute-start(bf16[512,256]{1,0:T(8,128)(2,1)S(1)} %bitcast.35), channel_id=1, source_target_pairs={{0,16},{8,24},{16,32},{24,40},{32,48},{40,56},{48,64},{56,72},{64,... | collective-permute-start | bytes 786440 | tf_op jit(solution)/shard_map/ppermute | solution.py:26
  180.7 16.5 %collective-permute-start.6 = (bf16[512,256]{1,0:T(8,128)(2,1)S(1)}, bf16[512,256]{1,0:T(8,128)(2,1)S(1)}, u32[]{:S(2)}, u32[]{:S(2)}) collective-permute-start(bf16[512,256]{1,0:T(8,128)(2,1)S(1)} %bitcast.36), channel_id=1, source_target_pairs={{0,8},{8,16},{16,24},{24,32},{32,40},{40,48},{48,56},{56,64},{64,7... | collective-permute-start | bytes 786440 | tf_op jit(solution)/shard_map/ppermute | solution.py:26
  186.1 16.9 %copy-start.2 = (bf16[1024,128]{1,0:T(8,128)(2,1)S(1)}, bf16[1024,128]{1,0:T(8,128)(2,1)}, u32[]{:S(2)}) copy-start(bf16[1024,128]{1,0:T(8,128)(2,1)} %multiply_convert_fusion.rest_4_) | copy-start | bytes 786436
  197.6 18.0 %collective-permute-start.8 = (bf16[512,256]{1,0:T(8,128)(2,1)S(1)}, bf16[512,256]{1,0:T(8,128)(2,1)S(1)}, u32[]{:S(2)}, u32[]{:S(2)}) collective-permute-start(bf16[512,256]{1,0:T(8,128)(2,1)S(1)} %fusion.12), channel_id=1, source_target_pairs={{0,16},{8,24},{16,32},{24,40},{32,48},{40,56},{48,64},{56,72},{64,... | collective-permute-start | bytes 786440 | tf_op jit(solution)/shard_map/ppermute | solution.py:26
Sparse Core Ops, SparseCore 0:
  10.4 99.0 all-gather.1

commit v6 on v5

--- a/solution.py
+++ b/solution.py
@@ -51,48 +51,75 @@
     )
 
 
-def load(weights, kind, target, sems):
-    parts = sems.shape[0]
-    each = target.shape[0] // parts
-    copies = []
-    for part in range(parts):
-        span = pl.ds(part * each, each)
-        copies.append(
-            pltpu.make_async_copy(weights.at[span, kind], target.at[span], sems.at[part])
-        )
+def feed_forward_kernel(n_early, normed, weights, *rest):
+    theirs, mine, rows, up, down, hidden, made, row_sem, up_sems, down_sems, out_sems = rest[
+        n_early:
+    ]
+    half, features = mine.shape
+    width, parts, step = hidden.shape[1], down_sems.shape[0], 256
+    each, wide = down.shape[0] // parts, features // parts
+    row_copy = pltpu.make_async_copy(normed, rows, row_sem)
+    spans = [pl.ds(at, min(step, width - at)) for at in range(0, width, step)]
+    up_copies = [
+        pltpu.make_async_copy(weights.at[:, 0, :, span], up.at[:, :, span], up_sems.at[index])
+        for index, span in enumerate(spans)
+    ]
+    shards = [pl.ds(part * each, each) for part in range(parts)]
+    down_copies = [
+        pltpu.make_async_copy(weights.at[shard, 1], down.at[shard], down_sems.at[part])
+        for part, shard in enumerate(shards)
+    ]
+    for copy in [row_copy] + up_copies + down_copies:
+        copy.start()
+    row_copy.wait()
+    previous = None
+    for span, copy in zip(spans, up_copies):
+        copy.wait()
+        preact = jnp.dot(rows[...], flat(up[:, :, span]), preferred_element_type=jnp.float32)
+        if previous is not None:
+            hidden[:, previous[0]] = activate(previous[1])
+        previous = (span, preact)
+    hidden[:, previous[0]] = activate(previous[1])
+    stores = []
+    for part, copy in enumerate(down_copies):
+        copy.wait()
+        span = pl.ds(part * wide, wide)
+        made[:, span] = dot_rows(hidden[...], flat(down[shards[part]])).astype(made.dtype)
+        for side, target in enumerate((theirs, mine)):
+            stores.append(
+                pltpu.make_async_copy(
+                    made.at[pl.ds(side * half, half), span],
+                    target.at[:, span],
+                    out_sems.at[side * parts + part],
+                )
+            )
+            stores[-1].start()
+    for store in stores:
+        store.wait()
+
+
+def out_kernel(gathered, weights, out, held, sems):
+    heads, parts = gathered.shape[0], sems.shape[0]
+    each = heads // parts
+    copies = [
+        pltpu.make_async_copy(
+            weights.at[pl.ds(part * each, each)], held.at[pl.ds(part * each, each)], sems.at[part]
+        )
+        for part in range(parts)
+    ]
     for copy in copies:
         copy.start()
-    return copies
-
-
-def feed_forward_kernel(n_early, normed, weights, *rest):
-    theirs, mine, rows, up, down, hidden, row_sem, up_sems, down_sems = rest[n_early:]
-    row_copy = pltpu.make_async_copy(normed, rows, row_sem)
-    row_copy.start()
-    up_copies = load(weights, 0, up, up_sems)
-    down_copies = load(weights, 1, down, down_sems)
-    for copy in [row_copy] + up_copies:
+    total = None
+    for part, copy in enumerate(copies):
         copy.wait()
-    step = 256
-    for start in range(0, hidden.shape[1], step):
-        span = slice(start, min(start + step, hidden.shape[1]))
-        preact = jnp.dot(rows[...], flat(up[:, :, span]), preferred_element_type=jnp.float32)
-        hidden[:, span] = activate(preact)
-    half, features = mine.shape
-    each, wide = down.shape[0] // len(down_copies), features // len(down_copies)
-    for part, copy in enumerate(down_copies):
-        copy.wait()
-        made = dot_rows(hidden[...], flat(down[part * each : (part + 1) * each]))
-        span = slice(part * wide, (part + 1) * wide)
-        theirs[:, span] = made[:half].astype(theirs.dtype)
-        mine[:, span] = made[half:].astype(mine.dtype)
-
-
-def out_kernel(gathered, weights, out):
-    left = jnp.concatenate([gathered[head] for head in range(gathered.shape[0])], axis=1)
-    out[...] = jnp.dot(left, flat(weights[...]), preferred_element_type=jnp.float32).astype(
-        out.dtype
-    )
+        left = jnp.concatenate([gathered[part * each + head] for head in range(each)], axis=1)
+        term = jnp.dot(
+            left,
+            flat(held[part * each : (part + 1) * each]),
+            preferred_element_type=jnp.float32,
+        )
+        total = term if total is None else total + term
+    out[...] = total.astype(out.dtype)
 
 
 def kv_kernel(core, terms, rows, gain, same, other, out, held, sems):
@@ -115,13 +142,13 @@
         out[head, :, HS:] = made[:, HS:].astype(jnp.bfloat16)
 
 
-def call(kernel, shape, in_specs, args, flops, scratch, count=1, limit=None):
+def call(kernel, shape, in_specs, args, flops, scratch, count=1, limit=None, out=WHOLE):
     moved = count * math.prod(shape) + sum(arg.size for arg in args)
     return pl.pallas_call(
         kernel,
         out_shape=[jax.ShapeDtypeStruct(shape, jnp.bfloat16)] * count,
         in_specs=in_specs,
-        out_specs=[WHOLE] * count,
+        out_specs=[out] * count,
         scratch_shapes=scratch,
         compiler_params=pltpu.CompilerParams(vmem_limit_bytes=limit),
         cost_estimate=pl.CostEstimate(flops=flops, bytes_accessed=2 * moved, transcendentals=0),
@@ -191,16 +218,17 @@
             stored,
             stored,
             pltpu.VMEM((rows, width), jnp.bfloat16),
+            pltpu.VMEM((rows, features), jnp.bfloat16),
             pltpu.SemaphoreType.DMA(()),
+            pltpu.SemaphoreType.DMA((pl.cdiv(width, 256),)),
             pltpu.SemaphoreType.DMA((parts,)),
-            pltpu.SemaphoreType.DMA((parts,)),
+            pltpu.SemaphoreType.DMA((2 * parts,)),
         ],
         count=2,
+        out=ANYWHERE,
     )
     arrived = lax.ppermute(theirs, "mp", core_swap)
-    paired = (mine.astype(jnp.float32) + arrived.astype(jnp.float32)).astype(
-        jnp.bfloat16
-    )
+    paired = (mine.astype(jnp.float32) + arrived.astype(jnp.float32)).astype(jnp.bfloat16)
     terms = lax.all_to_all(
         paired.reshape(chips, own, features), "mp", 0, 0, axis_index_groups=same_core
     )
@@ -275,10 +303,10 @@
     (decoded,) = call(
         out_kernel,
         (bytes_own, out_all.shape[-1]),
-        [WHOLE, WHOLE],
+        [WHOLE, ANYWHERE],
         (gathered, out_all),
         2 * bytes_own * n_mp * HS * out_all.shape[-1],
-        [],
+        [pltpu.VMEM(out_all.shape, jnp.bfloat16), pltpu.SemaphoreType.DMA((4,))],
         limit=24 * 2**20,
     )
     return decoded

time: 238 us -> 239 us (level)
  no operation moved by 1% of the time
where the time goes in v6:
time: 239 us; the launch traced here: 238 us
  blocking collectives  63 us (26%)
  waiting for transfers between devices  56.6 us (24%)
  starting transfers between devices  51.8 us (22%)
  Pallas kernels  20 us (8%)
  between operations  17.7 us (7%)
  other arithmetic  13.7 us (6%)
  matrix products  8.2 us (3%)
  local copies, waits for them, and re-layouts  6.86 us (3%)
    all_to_all x1, blocking collectives, spread(): return lax.all_to_all(copies, 'mp', 0, 0, axis_index_groups=groups)  53.1 us
    ppermute x7, starting transfers between devices, from_behind(): lax.ppermute(value, 'seq', [(source, source + steps) for source in range(...  36.6 us
    ppermute x7, waiting for transfers between devices, from_behind(): lax.ppermute(value, 'seq', [(source, source + steps) for source in range(...  20.7 us
    pallas_call x3, Pallas kernels, call(): pl.pallas_call(kernel, out_shape=[jax.ShapeDtypeStruct(shape, jnp.bfloat1...  20 us
    all_to_all x1, waiting for transfers between devices, spread(): return lax.all_to_all(copies, 'mp', 0, 0, axis_index_groups=groups)  17.7 us
    all_to_all x1, waiting for transfers between devices, block(): lax.all_to_all(paired.reshape(chips, own, features), 'mp', 0, 0, axis_ind...  9.92 us
    all_to_all x1, blocking collectives, block(): gathered = lax.all_to_all(attended.reshape(n_mp, bytes_own, HS), 'mp', 0, 0)  9.91 us
    all_to_all x1, waiting for transfers between devices, block(): kv_pack = lax.all_to_all(by_head, 'mp', 0, 0).reshape(rows, 2 * HS)  7.04 us
  transfers between devices with their start and end apart: 13, of which 7 were waited for; matrix products, arithmetic and copies ran while one was open for 9% of the time, Pallas kernels for 0%

profile of v6, /device:TPU:24, one launch (start us, length us, event | category | flops | bytes accessed | tf_op | source)
XLA Modules:
  0.0 237.8 jit_solution(11395685955229048396)
XLA Ops:
  6.5 0.0 copy-start
  6.5 0.0 all-gather.2.cloned.1.call-start
  6.5 1.7 pad_maximum_fusion.1
  8.2 0.0 all-gather.2.cloned.1.call-update
  8.2 1.5 broadcast_in_dim.10
  9.7 0.0 copy-start.3
  9.7 53.1 %all_to_all.25.rest_1_.same = bf16[4,2048,256]{2,1,0:T(8,128)(2,1)} all-to-all(bf16[4,2048,256]{2,1,0:T(8,128)(2,1)S(1)} %broadcast_in_dim.10), channel_id=1, replica_groups={{0,2,4,6},{1,3,5,7},{8,10,12,14},{9,11,13,15},{16,18,20,22},{17,19,21,2..., dimensions={0} | all-to-all | bytes 8388608 | tf_op jit(solution)/shard_map/all_to_all | solution.py:32
  62.9 1.9 collective-permute-start.4
  64.8 4.3 %collective-permute-start = (s32[1]{0:T(128)}, s32[1]{0:T(128)}, u32[]{:S(2)}, u32[]{:S(2)}) collective-permute-start(s32[1]{0:T(128)} %param.20), channel_id=1, source_target_pairs={{0,8},{8,16},{16,24},{24,32},{32,40},{40,48},{48,56},{56,64},{64,7... | collective-permute-start | bytes 20 | tf_op jit(solution)/shard_map/ppermute | solution.py:26
  69.1 6.1 %collective-permute-start.1 = (s32[1]{0:T(128)}, s32[1]{0:T(128)}, u32[]{:S(2)}, u32[]{:S(2)}) collective-permute-start(s32[1]{0:T(128)} %param.20), channel_id=1, source_target_pairs={{0,16},{8,24},{16,32},{24,40},{32,48},{40,56},{48,64},{56,72},{64,... | collective-permute-start | bytes 20 | tf_op jit(solution)/shard_map/ppermute | solution.py:26
  75.2 7.3 %collective-permute-start.2 = (s32[1]{0:T(128)}, s32[1]{0:T(128)}, u32[]{:S(2)}, u32[]{:S(2)}) collective-permute-start(s32[1]{0:T(128)} %param.20), channel_id=1, source_target_pairs={{0,24},{8,32},{16,40},{24,48},{32,56},{40,64},{48,72},{56,80},{64,... | collective-permute-start | bytes 20 | tf_op jit(solution)/shard_map/ppermute | solution.py:26
  82.5 2.9 %collective-permute-start.3 = (s32[1]{0:T(128)}, s32[1]{0:T(128)}, u32[]{:S(2)}, u32[]{:S(2)}) collective-permute-start(s32[1]{0:T(128)} %param.20), channel_id=1, source_target_pairs={{0,32},{8,40},{16,48},{24,56},{32,64},{40,72},{48,80},{56,88},{64,... | collective-permute-start | bytes 20 | tf_op jit(solution)/shard_map/ppermute | solution.py:26
  85.4 0.0 copy-done.3
  85.4 1.6 broadcast_in_dim.11
  87.0 4.5 %all-to-all-start.1 = ((bf16[8,128,1024]{2,1,0:T(8,128)(2,1)}), bf16[8,128,1024]{2,1,0:T(8,128)(2,1)}, u32[]{:S(2)}, u32[]{:S(2)}) async-start(bf16[8,128,1024]{2,1,0:T(8,128)(2,1)} %broadcast_in_dim.11), calls=%async_computation.1 | async-start | bytes 4194304 | tf_op jit(solution)/shard_map/all_to_all | solution.py:32
  91.5 0.0 copy-start.5
  91.5 0.8 multiply_reduce_fusion
  92.4 0.2 copy.12
  92.6 1.8 constant_dynamic-slice_fusion.2
  94.5 0.5 fusion
  95.0 0.9 multiply_convert_fusion.rest_4_
  95.9 1.9 fusion.2.normed
  97.8 0.0 collective-permute-done
  97.8 0.0 collective-permute-done.1
  97.8 0.0 collective-permute-done.2
  97.8 0.0 collective-permute-done.3
  97.8 3.2 %pad_add_fusion.rest_0_ = s32[4]{0:T(128)} fusion(s32[1]{0:T(128)} %collective-permute-done.3, s32[1]{0:T(128)} %collective-permute-done.2, s32[1]{0:T(128)} %collective-permute-done.1, s32[1]{0:T(128)} %collective-permute-done), kind=kLoop, calls=%fused_computation.65 | loop fusion | flops 12 | bytes 32 | tf_op jit(solution)/shard_map/concatenate | solution.py:207
  101.0 17.7 %all-to-all-done.1.rest_3_.weights = bf16[8,128,1024]{2,1,0:T(8,128)(2,1)} async-done(((bf16[8,128,1024]{2,1,0:T(8,128)(2,1)}), bf16[8,128,1024]{2,1,0:T(8,128)(2,1)}, u32[]{:S(2)}, u32[]{:S(2)}) %all-to-all-start.1) | async-done | bytes 2097184 | tf_op jit(solution)/shard_map/all_to_all | solution.py:32
  118.7 0.0 collective-permute-done.4.rest_2_.other
  118.7 11.9 %shard_map.109 = (bf16[256,2048]{1,0:T(8,128)(2,1)}, bf16[256,2048]{1,0:T(8,128)(2,1)}) custom-call(bf16[512,2048]{1,0:T(8,128)(2,1)} %fusion.2.normed, bf16[64,2,32,896]{3,2,1,0:T(8,128)(2,1)} %bitcast.32, s32[4]{0:T(128)} %pad_add_fusion.rest_0_, bf16[4,2048,256]{2,1,0:T(8,128)(2,1)} %all_to_all.25.rest_1_.same, ...), custom_call_target="tpu_custom_call" | custom-call | flops 3758096384 | bytes 22282248 | tf_op jit(solution)/shard_map/pallas_call | solution.py:147
  130.6 1.9 collective-permute-start.5
  133.2 0.0 copy-done.6
  133.2 1.0 constant_dynamic-slice_fusion.rows
  134.2 1.2 collective-permute-done.5
  135.4 2.6 %add_convert_fusion = bf16[256,2048]{1,0:T(8,128)(2,1)} fusion(bf16[256,2048]{1,0:T(8,128)(2,1)S(1)} %collective-permute-done.5, bf16[256,2048]{1,0:T(8,128)(2,1)} %get-tuple-element.7), kind=kLoop, calls=%fused_computation.10 | loop fusion | flops 2097152 | bytes 3145728 | tf_op jit(solution)/shard_map/convert_element_type | solution.py:231
  138.0 3.5 %all-to-all-start.2 = ((bf16[4,64,2048]{2,1,0:T(8,128)(2,1)}), bf16[4,64,2048]{2,1,0:T(8,128)(2,1)S(1)}, u32[]{:S(2)}, u32[]{:S(2)}) async-start(bf16[4,64,2048]{2,1,0:T(8,128)(2,1)} %bitcast.33), calls=%async_computation.2 | async-start | bytes 2097152 | tf_op jit(solution)/shard_map/all_to_all | solution.py:232
  141.5 0.7 iota_compare_fusion.5
  145.4 0.6 iota_compare_fusion.6
  145.9 0.6 iota_subtract_fusion.2
  146.5 0.7 fusion.34
  147.2 9.9 %all-to-all-done.2.terms = bf16[4,64,2048]{2,1,0:T(8,128)(2,1)S(1)} async-done(((bf16[4,64,2048]{2,1,0:T(8,128)(2,1)}), bf16[4,64,2048]{2,1,0:T(8,128)(2,1)S(1)}, u32[]{:S(2)}, u32[]{:S(2)}) %all-to-all-start.2) | async-done | bytes 1048608 | tf_op jit(solution)/shard_map/all_to_all | solution.py:232
  157.1 5.6 %shard_map.110 = bf16[8,64,256]{2,1,0:T(8,128)(2,1)S(1)} custom-call(s32[1]{0:T(128)} %bitcast.1.core, bf16[4,64,2048]{2,1,0:T(8,128)(2,1)S(1)} %all-to-all-done.2.terms, bf16[64,2048]{1,0:T(8,128)(2,1)S(1)} %constant_dynamic-slice_fusion.rows, bf16[1,2048]{1,0:T(2,128)(2,1)S(1)} %reshape.110.gain, bf16[4,2048,256]{2,1,0:T(8,128)(2,1)} %all_to_all.25.rest_1_.same, ...), custom_call_target="tpu_custom_call" | custom-call | flops 536870912 | bytes 9965570 | tf_op jit(solution)/shard_map/pallas_call | solution.py:147
  162.7 0.7 copy-done.1
  163.4 3.4 %all-to-all-start.3 = ((bf16[8,64,256]{2,1,0:T(8,128)(2,1)}), bf16[8,64,256]{2,1,0:T(8,128)(2,1)S(1)}, u32[]{:S(2)}, u32[]{:S(2)}) async-start(bf16[8,64,256]{2,1,0:T(8,128)(2,1)} %copy-done.1), calls=%async_computation.3 | async-start | bytes 524288 | tf_op jit(solution)/shard_map/all_to_all | solution.py:255
  166.8 0.4 iota_compare_fusion.2
  167.2 7.0 %all-to-all-done.3 = bf16[8,64,256]{2,1,0:T(8,128)(2,1)S(1)} async-done(((bf16[8,64,256]{2,1,0:T(8,128)(2,1)}), bf16[8,64,256]{2,1,0:T(8,128)(2,1)S(1)}, u32[]{:S(2)}, u32[]{:S(2)}) %all-to-all-start.3) | async-done | bytes 262176 | tf_op jit(solution)/shard_map/all_to_all | solution.py:255
  174.3 7.3 %collective-permute-start.7 = (bf16[512,256]{1,0:T(8,128)(2,1)S(1)}, bf16[512,256]{1,0:T(8,128)(2,1)S(1)}, u32[]{:S(2)}, u32[]{:S(2)}) collective-permute-start(bf16[512,256]{1,0:T(8,128)(2,1)S(1)} %bitcast.35), channel_id=1, source_target_pairs={{0,16},{8,24},{16,32},{24,40},{32,48},{40,56},{48,64},{56,72},{64,... | collective-permute-start | bytes 786440 | tf_op jit(solution)/shard_map/ppermute | solution.py:26
  181.6 3.6 %collective-permute-start.6 = (bf16[512,256]{1,0:T(8,128)(2,1)S(1)}, bf16[512,256]{1,0:T(8,128)(2,1)S(1)}, u32[]{:S(2)}, u32[]{:S(2)}) collective-permute-start(bf16[512,256]{1,0:T(8,128)(2,1)S(1)} %bitcast.36), channel_id=1, source_target_pairs={{0,8},{8,16},{16,24},{24,32},{32,40},{40,48},{48,56},{56,64},{64,7... | collective-permute-start | bytes 786440 | tf_op jit(solution)/shard_map/ppermute | solution.py:26
  185.1 2.0 fusion.39
  187.2 0.0 copy-start.2
  187.2 5.8 %collective-permute-done.7 = bf16[512,256]{1,0:T(8,128)(2,1)S(1)} collective-permute-done((bf16[512,256]{1,0:T(8,128)(2,1)S(1)}, bf16[512,256]{1,0:T(8,128)(2,1)S(1)}, u32[]{:S(2)}, u32[]{:S(2)}) %collective-permute-start.7) | collective-permute-done | bytes 262176 | tf_op jit(solution)/shard_map/ppermute | solution.py:26
  192.9 5.1 %collective-permute-done.6 = bf16[512,256]{1,0:T(8,128)(2,1)S(1)} collective-permute-done((bf16[512,256]{1,0:T(8,128)(2,1)S(1)}, bf16[512,256]{1,0:T(8,128)(2,1)S(1)}, u32[]{:S(2)}, u32[]{:S(2)}) %collective-permute-start.6) | collective-permute-done | bytes 262176 | tf_op jit(solution)/shard_map/ppermute | solution.py:26
  198.1 0.4 fusion.12
  198.5 5.2 %collective-permute-start.8 = (bf16[512,256]{1,0:T(8,128)(2,1)S(1)}, bf16[512,256]{1,0:T(8,128)(2,1)S(1)}, u32[]{:S(2)}, u32[]{:S(2)}) collective-permute-start(bf16[512,256]{1,0:T(8,128)(2,1)S(1)} %fusion.12), channel_id=1, source_target_pairs={{0,16},{8,24},{16,32},{24,40},{32,48},{40,56},{48,64},{56,72},{64,... | collective-permute-start | bytes 786440 | tf_op jit(solution)/shard_map/ppermute | solution.py:26
  203.7 1.0 fusion.40
  204.7 0.5 fusion.18
  205.2 0.5 convolution_add_fusion.1
  205.7 1.0 fusion.38
  206.7 9.8 %collective-permute-done.8 = bf16[512,256]{1,0:T(8,128)(2,1)S(1)} collective-permute-done((bf16[512,256]{1,0:T(8,128)(2,1)S(1)}, bf16[512,256]{1,0:T(8,128)(2,1)S(1)}, u32[]{:S(2)}, u32[]{:S(2)}) %collective-permute-start.8) | collective-permute-done | bytes 262176 | tf_op jit(solution)/shard_map/ppermute | solution.py:26
  216.5 1.0 fusion.37
  217.5 0.5 fusion.15
  218.0 0.5 fusion.11
  218.5 9.9 %all_to_all.26.gathered = bf16[8,128,128]{2,1,0:T(8,128)(2,1)S(1)} all-to-all(bf16[8,128,128]{2,1,0:T(8,128)(2,1)S(1)} %bitcast.39), channel_id=1, replica_groups=mesh['seq'=64,'mp'=8] {'mp'}, dimensions={0} | all-to-all | bytes 524288 | tf_op jit(solution)/shard_map/all_to_all | solution.py:302
  228.4 2.5 %shard_map.111 = bf16[128,1024]{1,0:T(8,128)(2,1)} custom-call(bf16[8,128,128]{2,1,0:T(8,128)(2,1)S(1)} %all_to_all.26.gathered, bf16[8,128,1024]{2,1,0:T(8,128)(2,1)} %all-to-all-done.1.rest_3_.weights), custom_call_target="tpu_custom_call" | custom-call | flops 268435456 | bytes 2621440 | tf_op jit(solution)/shard_map/pallas_call | solution.py:147
  (22 shorter events, 0.1 us)
Async XLA Ops:
  6.5 85.0 %copy-start = (bf16[1024,1024]{1,0:T(8,128)(2,1)S(1)}, bf16[1024,1024]{1,0:T(8,128)(2,1)}, u32[]{:S(2)}) copy-start(bf16[1024,1024]{1,0:T(8,128)(2,1)} %param.17) | copy-start | bytes 6291460
  6.5 112.1 %all-gather.2.cloned.1.call-start = ((), (), s32[]{:S(2)}) async-start(), calls=%async_computation.5 | async-start | bytes 7454720 | tf_op jit(solution)/shard_map/all_gather | solution.py:181
  9.7 75.6 %copy-start.3 = (bf16[128,1024]{1,0:T(8,128)(2,1)S(1)}, bf16[128,1024]{1,0:T(8,128)(2,1)}, u32[]{:S(2)}) copy-start(bf16[128,1024]{1,0:T(8,128)(2,1)} %param.19) | copy-start | bytes 786436
  62.9 55.8 %collective-permute-start.4 = (bf16[4,2048,256]{2,1,0:T(8,128)(2,1)}, bf16[4,2048,256]{2,1,0:T(8,128)(2,1)}, u32[]{:S(2)}, u32[]{:S(2)}) collective-permute-start(bf16[4,2048,256]{2,1,0:T(8,128)(2,1)} %all_to_all.25.rest_1_.same), channel_id=1, source_target_pairs={{0,1},{1,0},{2,3},{3,2},{4,5},{5,4},{6,7},{7,6},{8,9},{9,8},{10,11... | collective-permute-start | bytes 12582920 | tf_op jit(solution)/shard_map/ppermute | solution.py:186
  64.8 33.0 %collective-permute-start = (s32[1]{0:T(128)}, s32[1]{0:T(128)}, u32[]{:S(2)}, u32[]{:S(2)}) collective-permute-start(s32[1]{0:T(128)} %param.20), channel_id=1, source_target_pairs={{0,8},{8,16},{16,24},{24,32},{32,40},{40,48},{48,56},{56,64},{64,7... | collective-permute-start | bytes 20 | tf_op jit(solution)/shard_map/ppermute | solution.py:26
  69.1 28.7 %collective-permute-start.1 = (s32[1]{0:T(128)}, s32[1]{0:T(128)}, u32[]{:S(2)}, u32[]{:S(2)}) collective-permute-start(s32[1]{0:T(128)} %param.20), channel_id=1, source_target_pairs={{0,16},{8,24},{16,32},{24,40},{32,48},{40,56},{48,64},{56,72},{64,... | collective-permute-start | bytes 20 | tf_op jit(solution)/shard_map/ppermute | solution.py:26
  75.2 22.6 %collective-permute-start.2 = (s32[1]{0:T(128)}, s32[1]{0:T(128)}, u32[]{:S(2)}, u32[]{:S(2)}) collective-permute-start(s32[1]{0:T(128)} %param.20), channel_id=1, source_target_pairs={{0,24},{8,32},{16,40},{24,48},{32,56},{40,64},{48,72},{56,80},{64,... | collective-permute-start | bytes 20 | tf_op jit(solution)/shard_map/ppermute | solution.py:26
  82.5 15.3 %collective-permute-start.3 = (s32[1]{0:T(128)}, s32[1]{0:T(128)}, u32[]{:S(2)}, u32[]{:S(2)}) collective-permute-start(s32[1]{0:T(128)} %param.20), channel_id=1, source_target_pairs={{0,32},{8,40},{16,48},{24,56},{32,64},{40,72},{48,80},{56,88},{64,... | collective-permute-start | bytes 20 | tf_op jit(solution)/shard_map/ppermute | solution.py:26
  87.0 4.5 %copy-start.4 = (bf16[1024,128]{1,0:T(8,128)(2,1)S(1)}, bf16[1024,128]{1,0:T(8,128)(2,1)}, u32[]{:S(2)}) copy-start(bf16[1024,128]{1,0:T(8,128)(2,1)} %param.18) | copy-start | bytes 786436
  87.0 31.7 %all-to-all-start.1 = ((bf16[8,128,1024]{2,1,0:T(8,128)(2,1)}), bf16[8,128,1024]{2,1,0:T(8,128)(2,1)}, u32[]{:S(2)}, u32[]{:S(2)}) async-start(bf16[8,128,1024]{2,1,0:T(8,128)(2,1)} %broadcast_in_dim.11), calls=%async_computation.1 | async-start | bytes 4194304 | tf_op jit(solution)/shard_map/all_to_all | solution.py:32
  91.5 0.9 copy-start.5
  118.7 14.5 %copy-start.6 = (bf16[2048]{0:T(1024)(128)(2,1)S(1)}, bf16[2048]{0:T(1024)(128)(2,1)}, u32[]{:S(2)}) copy-start(bf16[2048]{0:T(1024)(128)(2,1)} %param.15) | copy-start | bytes 12292
  118.7 14.5 %copy-start.7 = (s32[1024]{0:T(1024)S(1)}, s32[1024]{0:T(1024)}, u32[]{:S(2)}) copy-start(s32[1024]{0:T(1024)} %param.21) | copy-start | bytes 12292
  130.6 4.8 %collective-permute-start.5 = (bf16[256,2048]{1,0:T(8,128)(2,1)}, bf16[256,2048]{1,0:T(8,128)(2,1)S(1)}, u32[]{:S(2)}, u32[]{:S(2)}) collective-permute-start(bf16[256,2048]{1,0:T(8,128)(2,1)} %get-tuple-element.8), channel_id=1, source_target_pairs={{0,1},{1,0},{2,3},{3,2},{4,5},{5,4},{6,7},{7,6},{8,9},{9,8},{10,11... | collective-permute-start | bytes 3145736 | tf_op jit(solution)/shard_map/ppermute | solution.py:230
  138.0 19.2 %all-to-all-start.2 = ((bf16[4,64,2048]{2,1,0:T(8,128)(2,1)}), bf16[4,64,2048]{2,1,0:T(8,128)(2,1)S(1)}, u32[]{:S(2)}, u32[]{:S(2)}) async-start(bf16[4,64,2048]{2,1,0:T(8,128)(2,1)} %bitcast.33), calls=%async_computation.2 | async-start | bytes 2097152 | tf_op jit(solution)/shard_map/all_to_all | solution.py:232
  162.7 0.7 copy-start.1
  163.4 10.8 %all-to-all-start.3 = ((bf16[8,64,256]{2,1,0:T(8,128)(2,1)}), bf16[8,64,256]{2,1,0:T(8,128)(2,1)S(1)}, u32[]{:S(2)}, u32[]{:S(2)}) async-start(bf16[8,64,256]{2,1,0:T(8,128)(2,1)} %copy-done.1), calls=%async_computation.3 | async-start | bytes 524288 | tf_op jit(solution)/shard_map/all_to_all | solution.py:255
  174.3 18.7 %collective-permute-start.7 = (bf16[512,256]{1,0:T(8,128)(2,1)S(1)}, bf16[512,256]{1,0:T(8,128)(2,1)S(1)}, u32[]{:S(2)}, u32[]{:S(2)}) collective-permute-start(bf16[512,256]{1,0:T(8,128)(2,1)S(1)} %bitcast.35), channel_id=1, source_target_pairs={{0,16},{8,24},{16,32},{24,40},{32,48},{40,56},{48,64},{56,72},{64,... | collective-permute-start | bytes 786440 | tf_op jit(solution)/shard_map/ppermute | solution.py:26
  181.6 16.5 %collective-permute-start.6 = (bf16[512,256]{1,0:T(8,128)(2,1)S(1)}, bf16[512,256]{1,0:T(8,128)(2,1)S(1)}, u32[]{:S(2)}, u32[]{:S(2)}) collective-permute-start(bf16[512,256]{1,0:T(8,128)(2,1)S(1)} %bitcast.36), channel_id=1, source_target_pairs={{0,8},{8,16},{16,24},{24,32},{32,40},{40,48},{48,56},{56,64},{64,7... | collective-permute-start | bytes 786440 | tf_op jit(solution)/shard_map/ppermute | solution.py:26
  187.2 16.6 %copy-start.2 = (bf16[1024,128]{1,0:T(8,128)(2,1)S(1)}, bf16[1024,128]{1,0:T(8,128)(2,1)}, u32[]{:S(2)}) copy-start(bf16[1024,128]{1,0:T(8,128)(2,1)} %multiply_convert_fusion.rest_4_) | copy-start | bytes 786436
  198.5 18.0 %collective-permute-start.8 = (bf16[512,256]{1,0:T(8,128)(2,1)S(1)}, bf16[512,256]{1,0:T(8,128)(2,1)S(1)}, u32[]{:S(2)}, u32[]{:S(2)}) collective-permute-start(bf16[512,256]{1,0:T(8,128)(2,1)S(1)} %fusion.12), channel_id=1, source_target_pairs={{0,16},{8,24},{16,32},{24,40},{32,48},{40,56},{48,64},{56,72},{64,... | collective-permute-start | bytes 786440 | tf_op jit(solution)/shard_map/ppermute | solution.py:26
Sparse Core Ops, SparseCore 0:
  10.4 99.0 all-gather.1

commit v7 on v5

--- a/solution.py
+++ b/solution.py
@@ -65,34 +65,58 @@
     return copies
 
 
-def feed_forward_kernel(n_early, normed, weights, *rest):
-    theirs, mine, rows, up, down, hidden, row_sem, up_sems, down_sems = rest[n_early:]
+def down_product(hidden, down, copies, out):
+    each, wide = down.shape[0] // len(copies), out.shape[1] // len(copies)
+    for part, copy in enumerate(copies):
+        copy.wait()
+        made = dot_rows(hidden, flat(down[part * each : (part + 1) * each]))
+        out[:, part * wide : (part + 1) * wide] = made.astype(out.dtype)
+
+
+def first_kernel(n_early, normed, weights, *rest):
+    theirs, kept, rows, up, down, hidden, row_sem, up_sems, down_sems = rest[n_early:]
     row_copy = pltpu.make_async_copy(normed, rows, row_sem)
     row_copy.start()
     up_copies = load(weights, 0, up, up_sems)
     down_copies = load(weights, 1, down, down_sems)
     for copy in [row_copy] + up_copies:
         copy.wait()
-    step = 256
+    half, step = theirs.shape[0], 256
     for start in range(0, hidden.shape[1], step):
         span = slice(start, min(start + step, hidden.shape[1]))
         preact = jnp.dot(rows[...], flat(up[:, :, span]), preferred_element_type=jnp.float32)
-        hidden[:, span] = activate(preact)
-    half, features = mine.shape
-    each, wide = down.shape[0] // len(down_copies), features // len(down_copies)
-    for part, copy in enumerate(down_copies):
+        active = activate(preact)
+        hidden[:, span] = active[:half]
+        kept[:, span] = active[half:]
+    down_product(hidden[...], down, down_copies, theirs)
+
+
+def second_kernel(hidden, weights, mine, down, sems):
+    down_product(hidden[...], down, load(weights, 1, down, sems), mine)
+
+
+def out_kernel(gathered, weights, out, held, sems):
+    heads, parts = gathered.shape[0], sems.shape[0]
+    each = heads // parts
+    copies = [
+        pltpu.make_async_copy(
+            weights.at[pl.ds(part * each, each)], held.at[pl.ds(part * each, each)], sems.at[part]
+        )
+        for part in range(parts)
+    ]
+    for copy in copies:
+        copy.start()
+    total = None
+    for part, copy in enumerate(copies):
         copy.wait()
-        made = dot_rows(hidden[...], flat(down[part * each : (part + 1) * each]))
-        span = slice(part * wide, (part + 1) * wide)
-        theirs[:, span] = made[:half].astype(theirs.dtype)
-        mine[:, span] = made[half:].astype(mine.dtype)
-
-
-def out_kernel(gathered, weights, out):
-    left = jnp.concatenate([gathered[head] for head in range(gathered.shape[0])], axis=1)
-    out[...] = jnp.dot(left, flat(weights[...]), preferred_element_type=jnp.float32).astype(
-        out.dtype
-    )
+        left = jnp.concatenate([gathered[part * each + head] for head in range(each)], axis=1)
+        term = jnp.dot(
+            left,
+            flat(held[part * each : (part + 1) * each]),
+            preferred_element_type=jnp.float32,
+        )
+        total = term if total is None else total + term
+    out[...] = total.astype(out.dtype)
 
 
 def kv_kernel(core, terms, rows, gain, same, other, out, held, sems):
@@ -115,13 +139,13 @@
         out[head, :, HS:] = made[:, HS:].astype(jnp.bfloat16)
 
 
-def call(kernel, shape, in_specs, args, flops, scratch, count=1, limit=None):
-    moved = count * math.prod(shape) + sum(arg.size for arg in args)
+def call(kernel, shapes, in_specs, args, flops, scratch, limit=None):
+    moved = sum(math.prod(shape) for shape in shapes) + sum(arg.size for arg in args)
     return pl.pallas_call(
         kernel,
-        out_shape=[jax.ShapeDtypeStruct(shape, jnp.bfloat16)] * count,
+        out_shape=[jax.ShapeDtypeStruct(shape, jnp.bfloat16) for shape in shapes],
         in_specs=in_specs,
-        out_specs=[WHOLE] * count,
+        out_specs=[WHOLE] * len(shapes),
         scratch_shapes=scratch,
         compiler_params=pltpu.CompilerParams(vmem_limit_bytes=limit),
         cost_estimate=pl.CostEstimate(flops=flops, bytes_accessed=2 * moved, transcendentals=0),
@@ -180,34 +204,40 @@
     early = (jnp.concatenate(prior), kv_same, kv_other, out_all, queries)
     half_rows, width, parts = rows // 2, up_weight.shape[1], 4
     stored = pltpu.VMEM(weights_all.shape[:1] + weights_all.shape[2:], jnp.bfloat16)
-    theirs, mine = call(
-        functools.partial(feed_forward_kernel, len(early)),
-        (half_rows, features),
+    sems = pltpu.SemaphoreType.DMA((parts,))
+    theirs, hidden = call(
+        functools.partial(first_kernel, len(early)),
+        [(half_rows, features), (half_rows, width)],
         [ANYWHERE, ANYWHERE, SCALARS] + [ANYWHERE] * (len(early) - 1),
         (normed, weights_all) + early,
-        4 * rows * features * width,
+        3 * rows * features * width,
         [
             pltpu.VMEM((rows, features), jnp.bfloat16),
             stored,
             stored,
-            pltpu.VMEM((rows, width), jnp.bfloat16),
+            pltpu.VMEM((half_rows, width), jnp.bfloat16),
             pltpu.SemaphoreType.DMA(()),
-            pltpu.SemaphoreType.DMA((parts,)),
-            pltpu.SemaphoreType.DMA((parts,)),
+            sems,
+            sems,
         ],
-        count=2,
     )
     arrived = lax.ppermute(theirs, "mp", core_swap)
-    paired = (mine.astype(jnp.float32) + arrived.astype(jnp.float32)).astype(
-        jnp.bfloat16
-    )
+    (mine,) = call(
+        second_kernel,
+        [(half_rows, features)],
+        [WHOLE, ANYWHERE],
+        (hidden, weights_all),
+        rows * features * width,
+        [stored, sems],
+    )
+    paired = (mine.astype(jnp.float32) + arrived.astype(jnp.float32)).astype(jnp.bfloat16)
     terms = lax.all_to_all(
         paired.reshape(chips, own, features), "mp", 0, 0, axis_index_groups=same_core
     )
 
     (by_head,) = call(
         kv_kernel,
-        (n_mp, own, 2 * HS),
+        [(n_mp, own, 2 * HS)],
         [SCALARS, WHOLE, WHOLE, WHOLE, ANYWHERE, ANYWHERE],
         (
             core.astype(jnp.int32).reshape(1),
@@ -274,11 +304,11 @@
     gathered = lax.all_to_all(attended.reshape(n_mp, bytes_own, HS), "mp", 0, 0)
     (decoded,) = call(
         out_kernel,
-        (bytes_own, out_all.shape[-1]),
-        [WHOLE, WHOLE],
+        [(bytes_own, out_all.shape[-1])],
+        [WHOLE, ANYWHERE],
         (gathered, out_all),
         2 * bytes_own * n_mp * HS * out_all.shape[-1],
-        [],
+        [pltpu.VMEM(out_all.shape, jnp.bfloat16), pltpu.SemaphoreType.DMA((4,))],
         limit=24 * 2**20,
     )
     return decoded

time: 238 us -> 241 us (1.013)
  Pallas kernels: 19.3 us -> 22.8 us
    pallas_call x3 -> x4, Pallas kernels: 19.3 us -> 22.8 us  [call(): pl.pallas_call(kernel, out_shape=[jax.ShapeDtypeStruct(shape, jnp.bfloat1...]
  transfers between devices with their start and end apart: 13 -> 13, of which waited for: 7 -> 6; matrix products, arithmetic and copies ran while one was open for 9% -> 9% of each run, Pallas kernels for 0% -> 2%
where the time goes in v7:
time: 241 us; the launch traced here: 240 us
  blocking collectives  63 us (26%)
  waiting for transfers between devices  55.7 us (23%)
  starting transfers between devices  51.9 us (22%)
  Pallas kernels  22.8 us (9%)
  between operations  17.7 us (7%)
  other arithmetic  13.7 us (6%)
  matrix products  8.22 us (3%)
  local copies, waits for them, and re-layouts  6.86 us (3%)
    all_to_all x1, blocking collectives, spread(): return lax.all_to_all(copies, 'mp', 0, 0, axis_index_groups=groups)  53.1 us
    ppermute x7, starting transfers between devices, from_behind(): lax.ppermute(value, 'seq', [(source, source + steps) for source in range(...  36.6 us
    pallas_call x4, Pallas kernels, call(): pl.pallas_call(kernel, out_shape=[jax.ShapeDtypeStruct(shape, jnp.bfloat1...  22.8 us
    ppermute x7, waiting for transfers between devices, from_behind(): lax.ppermute(value, 'seq', [(source, source + steps) for source in range(...  20.7 us
    all_to_all x1, waiting for transfers between devices, spread(): return lax.all_to_all(copies, 'mp', 0, 0, axis_index_groups=groups)  17.7 us
    all_to_all x1, waiting for transfers between devices, block(): lax.all_to_all(paired.reshape(chips, own, features), 'mp', 0, 0, axis_ind...  10.3 us
    all_to_all x1, blocking collectives, block(): gathered = lax.all_to_all(attended.reshape(n_mp, bytes_own, HS), 'mp', 0, 0)  9.91 us
    all_to_all x1, waiting for transfers between devices, block(): kv_pack = lax.all_to_all(by_head, 'mp', 0, 0).reshape(rows, 2 * HS)  7.04 us
  transfers between devices with their start and end apart: 13, of which 6 were waited for; matrix products, arithmetic and copies ran while one was open for 9% of the time, Pallas kernels for 2%

profile of v7, /device:TPU:24, one launch (start us, length us, event | category | flops | bytes accessed | tf_op | source)
XLA Modules:
  0.0 239.9 jit_solution(14111679004148118872)
XLA Ops:
  6.5 0.0 copy-start
  6.5 0.0 all-gather.2.cloned.1.call-start
  6.5 1.7 pad_maximum_fusion.1
  8.2 0.0 all-gather.2.cloned.1.call-update
  8.2 1.5 broadcast_in_dim.10
  9.7 0.0 copy-start.3
  9.7 53.1 %all_to_all.25.rest_1_.same = bf16[4,2048,256]{2,1,0:T(8,128)(2,1)} all-to-all(bf16[4,2048,256]{2,1,0:T(8,128)(2,1)S(1)} %broadcast_in_dim.10), channel_id=1, replica_groups={{0,2,4,6},{1,3,5,7},{8,10,12,14},{9,11,13,15},{16,18,20,22},{17,19,21,2..., dimensions={0} | all-to-all | bytes 8388608 | tf_op jit(solution)/shard_map/all_to_all | solution.py:32
  62.9 1.9 collective-permute-start.4
  64.8 4.3 %collective-permute-start = (s32[1]{0:T(128)}, s32[1]{0:T(128)}, u32[]{:S(2)}, u32[]{:S(2)}) collective-permute-start(s32[1]{0:T(128)} %param.20), channel_id=1, source_target_pairs={{0,8},{8,16},{16,24},{24,32},{32,40},{40,48},{48,56},{56,64},{64,7... | collective-permute-start | bytes 20 | tf_op jit(solution)/shard_map/ppermute | solution.py:26
  69.1 6.1 %collective-permute-start.1 = (s32[1]{0:T(128)}, s32[1]{0:T(128)}, u32[]{:S(2)}, u32[]{:S(2)}) collective-permute-start(s32[1]{0:T(128)} %param.20), channel_id=1, source_target_pairs={{0,16},{8,24},{16,32},{24,40},{32,48},{40,56},{48,64},{56,72},{64,... | collective-permute-start | bytes 20 | tf_op jit(solution)/shard_map/ppermute | solution.py:26
  75.2 7.3 %collective-permute-start.2 = (s32[1]{0:T(128)}, s32[1]{0:T(128)}, u32[]{:S(2)}, u32[]{:S(2)}) collective-permute-start(s32[1]{0:T(128)} %param.20), channel_id=1, source_target_pairs={{0,24},{8,32},{16,40},{24,48},{32,56},{40,64},{48,72},{56,80},{64,... | collective-permute-start | bytes 20 | tf_op jit(solution)/shard_map/ppermute | solution.py:26
  82.5 2.9 %collective-permute-start.3 = (s32[1]{0:T(128)}, s32[1]{0:T(128)}, u32[]{:S(2)}, u32[]{:S(2)}) collective-permute-start(s32[1]{0:T(128)} %param.20), channel_id=1, source_target_pairs={{0,32},{8,40},{16,48},{24,56},{32,64},{40,72},{48,80},{56,88},{64,... | collective-permute-start | bytes 20 | tf_op jit(solution)/shard_map/ppermute | solution.py:26
  85.4 0.0 copy-done.3
  85.4 1.6 broadcast_in_dim.11
  87.0 4.5 %all-to-all-start.1 = ((bf16[8,128,1024]{2,1,0:T(8,128)(2,1)}), bf16[8,128,1024]{2,1,0:T(8,128)(2,1)}, u32[]{:S(2)}, u32[]{:S(2)}) async-start(bf16[8,128,1024]{2,1,0:T(8,128)(2,1)} %broadcast_in_dim.11), calls=%async_computation.1 | async-start | bytes 4194304 | tf_op jit(solution)/shard_map/all_to_all | solution.py:32
  91.5 0.0 copy-start.5
  91.5 0.8 multiply_reduce_fusion
  92.4 0.2 copy.12
  92.6 1.8 constant_dynamic-slice_fusion.2
  94.5 0.5 fusion
  95.0 0.9 multiply_convert_fusion.rest_4_
  95.9 1.9 fusion.2.normed
  97.8 0.0 collective-permute-done
  97.8 0.0 collective-permute-done.1
  97.8 0.0 collective-permute-done.2
  97.8 0.0 collective-permute-done.3
  97.8 3.2 %pad_add_fusion.rest_0_ = s32[4]{0:T(128)} fusion(s32[1]{0:T(128)} %collective-permute-done.3, s32[1]{0:T(128)} %collective-permute-done.2, s32[1]{0:T(128)} %collective-permute-done.1, s32[1]{0:T(128)} %collective-permute-done), kind=kLoop, calls=%fused_computation.65 | loop fusion | flops 12 | bytes 32 | tf_op jit(solution)/shard_map/concatenate | solution.py:204
  101.0 17.7 %all-to-all-done.1.rest_3_.weights = bf16[8,128,1024]{2,1,0:T(8,128)(2,1)} async-done(((bf16[8,128,1024]{2,1,0:T(8,128)(2,1)}), bf16[8,128,1024]{2,1,0:T(8,128)(2,1)}, u32[]{:S(2)}, u32[]{:S(2)}) %all-to-all-start.1) | async-done | bytes 2097184 | tf_op jit(solution)/shard_map/all_to_all | solution.py:32
  118.7 0.0 collective-permute-done.4.rest_2_.other
  118.7 9.7 %shard_map.109 = (bf16[256,2048]{1,0:T(8,128)(2,1)}, bf16[256,896]{1,0:T(8,128)(2,1)}) custom-call(bf16[512,2048]{1,0:T(8,128)(2,1)} %fusion.2.normed, bf16[64,2,32,896]{3,2,1,0:T(8,128)(2,1)} %bitcast.28, s32[4]{0:T(128)} %pad_add_fusion.rest_0_, bf16[4,2048,256]{2,1,0:T(8,128)(2,1)} %all_to_all.25.rest_1_.same, ...), custom_call_target="tpu_custom_call" | custom-call | flops 2818572288 | bytes 21692424 | tf_op jit(solution)/shard_map/pallas_call | solution.py:144
  128.4 1.9 collective-permute-start.5
  131.0 1.0 constant_dynamic-slice_fusion.rows
  132.0 5.1 %shard_map.110 = bf16[256,2048]{1,0:T(8,128)(2,1)} custom-call(bf16[256,896]{1,0:T(8,128)(2,1)} %get-tuple-element.7.hidden, bf16[64,2,32,896]{3,2,1,0:T(8,128)(2,1)} %bitcast.29), custom_call_target="tpu_custom_call" | custom-call | flops 939524096 | bytes 8847360 | tf_op jit(solution)/shard_map/pallas_call | solution.py:144
  137.1 0.0 collective-permute-done.5
  137.1 2.6 %add_convert_fusion = bf16[256,2048]{1,0:T(8,128)(2,1)} fusion(bf16[256,2048]{1,0:T(8,128)(2,1)S(1)} %collective-permute-done.5, bf16[256,2048]{1,0:T(8,128)(2,1)} %shard_map.110), kind=kLoop, calls=%fused_computation.10 | loop fusion | flops 2097152 | bytes 3145728 | tf_op jit(solution)/shard_map/convert_element_type | solution.py:233
  139.7 3.5 %all-to-all-start.2 = ((bf16[4,64,2048]{2,1,0:T(8,128)(2,1)}), bf16[4,64,2048]{2,1,0:T(8,128)(2,1)S(1)}, u32[]{:S(2)}, u32[]{:S(2)}) async-start(bf16[4,64,2048]{2,1,0:T(8,128)(2,1)} %bitcast.34), calls=%async_computation.2 | async-start | bytes 2097152 | tf_op jit(solution)/shard_map/all_to_all | solution.py:234
  143.2 0.7 iota_compare_fusion.5
  147.1 0.6 iota_compare_fusion.6
  147.7 0.6 iota_subtract_fusion.2
  148.2 0.7 fusion.34
  149.0 10.3 %all-to-all-done.2.terms = bf16[4,64,2048]{2,1,0:T(8,128)(2,1)S(1)} async-done(((bf16[4,64,2048]{2,1,0:T(8,128)(2,1)}), bf16[4,64,2048]{2,1,0:T(8,128)(2,1)S(1)}, u32[]{:S(2)}, u32[]{:S(2)}) %all-to-all-start.2) | async-done | bytes 1048608 | tf_op jit(solution)/shard_map/all_to_all | solution.py:234
  159.2 5.6 %shard_map.111 = bf16[8,64,256]{2,1,0:T(8,128)(2,1)S(1)} custom-call(s32[1]{0:T(128)} %bitcast.1.core, bf16[4,64,2048]{2,1,0:T(8,128)(2,1)S(1)} %all-to-all-done.2.terms, bf16[64,2048]{1,0:T(8,128)(2,1)S(1)} %constant_dynamic-slice_fusion.rows, bf16[1,2048]{1,0:T(2,128)(2,1)S(1)} %reshape.110.gain, bf16[4,2048,256]{2,1,0:T(8,128)(2,1)} %all_to_all.25.rest_1_.same, ...), custom_call_target="tpu_custom_call" | custom-call | flops 536870912 | bytes 9965570 | tf_op jit(solution)/shard_map/pallas_call | solution.py:144
  164.8 0.7 copy-done.1
  165.5 3.4 %all-to-all-start.3 = ((bf16[8,64,256]{2,1,0:T(8,128)(2,1)}), bf16[8,64,256]{2,1,0:T(8,128)(2,1)S(1)}, u32[]{:S(2)}, u32[]{:S(2)}) async-start(bf16[8,64,256]{2,1,0:T(8,128)(2,1)} %copy-done.1), calls=%async_computation.3 | async-start | bytes 524288 | tf_op jit(solution)/shard_map/all_to_all | solution.py:257
  168.9 0.4 iota_compare_fusion.2
  169.3 7.0 %all-to-all-done.3 = bf16[8,64,256]{2,1,0:T(8,128)(2,1)S(1)} async-done(((bf16[8,64,256]{2,1,0:T(8,128)(2,1)}), bf16[8,64,256]{2,1,0:T(8,128)(2,1)S(1)}, u32[]{:S(2)}, u32[]{:S(2)}) %all-to-all-start.3) | async-done | bytes 262176 | tf_op jit(solution)/shard_map/all_to_all | solution.py:257
  176.3 7.3 %collective-permute-start.7 = (bf16[512,256]{1,0:T(8,128)(2,1)S(1)}, bf16[512,256]{1,0:T(8,128)(2,1)S(1)}, u32[]{:S(2)}, u32[]{:S(2)}) collective-permute-start(bf16[512,256]{1,0:T(8,128)(2,1)S(1)} %bitcast.36), channel_id=1, source_target_pairs={{0,16},{8,24},{16,32},{24,40},{32,48},{40,56},{48,64},{56,72},{64,... | collective-permute-start | bytes 786440 | tf_op jit(solution)/shard_map/ppermute | solution.py:26
  183.7 3.6 %collective-permute-start.6 = (bf16[512,256]{1,0:T(8,128)(2,1)S(1)}, bf16[512,256]{1,0:T(8,128)(2,1)S(1)}, u32[]{:S(2)}, u32[]{:S(2)}) collective-permute-start(bf16[512,256]{1,0:T(8,128)(2,1)S(1)} %bitcast.37), channel_id=1, source_target_pairs={{0,8},{8,16},{16,24},{24,32},{32,40},{40,48},{48,56},{56,64},{64,7... | collective-permute-start | bytes 786440 | tf_op jit(solution)/shard_map/ppermute | solution.py:26
  187.2 2.0 fusion.39
  189.3 0.0 copy-start.2
  189.3 5.8 %collective-permute-done.7 = bf16[512,256]{1,0:T(8,128)(2,1)S(1)} collective-permute-done((bf16[512,256]{1,0:T(8,128)(2,1)S(1)}, bf16[512,256]{1,0:T(8,128)(2,1)S(1)}, u32[]{:S(2)}, u32[]{:S(2)}) %collective-permute-start.7) | collective-permute-done | bytes 262176 | tf_op jit(solution)/shard_map/ppermute | solution.py:26
  195.0 5.1 %collective-permute-done.6 = bf16[512,256]{1,0:T(8,128)(2,1)S(1)} collective-permute-done((bf16[512,256]{1,0:T(8,128)(2,1)S(1)}, bf16[512,256]{1,0:T(8,128)(2,1)S(1)}, u32[]{:S(2)}, u32[]{:S(2)}) %collective-permute-start.6) | collective-permute-done | bytes 262176 | tf_op jit(solution)/shard_map/ppermute | solution.py:26
  200.1 0.4 fusion.12
  200.6 5.2 %collective-permute-start.8 = (bf16[512,256]{1,0:T(8,128)(2,1)S(1)}, bf16[512,256]{1,0:T(8,128)(2,1)S(1)}, u32[]{:S(2)}, u32[]{:S(2)}) collective-permute-start(bf16[512,256]{1,0:T(8,128)(2,1)S(1)} %fusion.12), channel_id=1, source_target_pairs={{0,16},{8,24},{16,32},{24,40},{32,48},{40,56},{48,64},{56,72},{64,... | collective-permute-start | bytes 786440 | tf_op jit(solution)/shard_map/ppermute | solution.py:26
  205.8 1.0 fusion.40
  206.8 0.5 fusion.18
  207.3 0.5 convolution_add_fusion.1
  207.8 1.0 fusion.38
  208.8 9.8 %collective-permute-done.8 = bf16[512,256]{1,0:T(8,128)(2,1)S(1)} collective-permute-done((bf16[512,256]{1,0:T(8,128)(2,1)S(1)}, bf16[512,256]{1,0:T(8,128)(2,1)S(1)}, u32[]{:S(2)}, u32[]{:S(2)}) %collective-permute-start.8) | collective-permute-done | bytes 262176 | tf_op jit(solution)/shard_map/ppermute | solution.py:26
  218.6 1.0 fusion.37
  219.6 0.5 fusion.15
  220.1 0.5 fusion.11
  220.6 9.9 %all_to_all.26.gathered = bf16[8,128,128]{2,1,0:T(8,128)(2,1)S(1)} all-to-all(bf16[8,128,128]{2,1,0:T(8,128)(2,1)S(1)} %bitcast.40), channel_id=1, replica_groups=mesh['seq'=64,'mp'=8] {'mp'}, dimensions={0} | all-to-all | bytes 524288 | tf_op jit(solution)/shard_map/all_to_all | solution.py:304
  230.5 2.5 %shard_map.112 = bf16[128,1024]{1,0:T(8,128)(2,1)} custom-call(bf16[8,128,128]{2,1,0:T(8,128)(2,1)S(1)} %all_to_all.26.gathered, bf16[8,128,1024]{2,1,0:T(8,128)(2,1)} %all-to-all-done.1.rest_3_.weights), custom_call_target="tpu_custom_call" | custom-call | flops 268435456 | bytes 2621440 | tf_op jit(solution)/shard_map/pallas_call | solution.py:144
  (23 shorter events, 0.1 us)
Async XLA Ops:
  6.5 85.0 %copy-start = (bf16[1024,1024]{1,0:T(8,128)(2,1)S(1)}, bf16[1024,1024]{1,0:T(8,128)(2,1)}, u32[]{:S(2)}) copy-start(bf16[1024,1024]{1,0:T(8,128)(2,1)} %param.17) | copy-start | bytes 6291460
  6.5 112.1 %all-gather.2.cloned.1.call-start = ((), (), s32[]{:S(2)}) async-start(), calls=%async_computation.5 | async-start | bytes 7454720 | tf_op jit(solution)/shard_map/all_gather | solution.py:178
  9.7 75.6 %copy-start.3 = (bf16[128,1024]{1,0:T(8,128)(2,1)S(1)}, bf16[128,1024]{1,0:T(8,128)(2,1)}, u32[]{:S(2)}) copy-start(bf16[128,1024]{1,0:T(8,128)(2,1)} %param.19) | copy-start | bytes 786436
  62.9 55.8 %collective-permute-start.4 = (bf16[4,2048,256]{2,1,0:T(8,128)(2,1)}, bf16[4,2048,256]{2,1,0:T(8,128)(2,1)}, u32[]{:S(2)}, u32[]{:S(2)}) collective-permute-start(bf16[4,2048,256]{2,1,0:T(8,128)(2,1)} %all_to_all.25.rest_1_.same), channel_id=1, source_target_pairs={{0,1},{1,0},{2,3},{3,2},{4,5},{5,4},{6,7},{7,6},{8,9},{9,8},{10,11... | collective-permute-start | bytes 12582920 | tf_op jit(solution)/shard_map/ppermute | solution.py:183
  64.8 33.0 %collective-permute-start = (s32[1]{0:T(128)}, s32[1]{0:T(128)}, u32[]{:S(2)}, u32[]{:S(2)}) collective-permute-start(s32[1]{0:T(128)} %param.20), channel_id=1, source_target_pairs={{0,8},{8,16},{16,24},{24,32},{32,40},{40,48},{48,56},{56,64},{64,7... | collective-permute-start | bytes 20 | tf_op jit(solution)/shard_map/ppermute | solution.py:26
  69.1 28.7 %collective-permute-start.1 = (s32[1]{0:T(128)}, s32[1]{0:T(128)}, u32[]{:S(2)}, u32[]{:S(2)}) collective-permute-start(s32[1]{0:T(128)} %param.20), channel_id=1, source_target_pairs={{0,16},{8,24},{16,32},{24,40},{32,48},{40,56},{48,64},{56,72},{64,... | collective-permute-start | bytes 20 | tf_op jit(solution)/shard_map/ppermute | solution.py:26
  75.2 22.6 %collective-permute-start.2 = (s32[1]{0:T(128)}, s32[1]{0:T(128)}, u32[]{:S(2)}, u32[]{:S(2)}) collective-permute-start(s32[1]{0:T(128)} %param.20), channel_id=1, source_target_pairs={{0,24},{8,32},{16,40},{24,48},{32,56},{40,64},{48,72},{56,80},{64,... | collective-permute-start | bytes 20 | tf_op jit(solution)/shard_map/ppermute | solution.py:26
  82.5 15.3 %collective-permute-start.3 = (s32[1]{0:T(128)}, s32[1]{0:T(128)}, u32[]{:S(2)}, u32[]{:S(2)}) collective-permute-start(s32[1]{0:T(128)} %param.20), channel_id=1, source_target_pairs={{0,32},{8,40},{16,48},{24,56},{32,64},{40,72},{48,80},{56,88},{64,... | collective-permute-start | bytes 20 | tf_op jit(solution)/shard_map/ppermute | solution.py:26
  87.0 4.5 %copy-start.4 = (bf16[1024,128]{1,0:T(8,128)(2,1)S(1)}, bf16[1024,128]{1,0:T(8,128)(2,1)}, u32[]{:S(2)}) copy-start(bf16[1024,128]{1,0:T(8,128)(2,1)} %param.18) | copy-start | bytes 786436
  87.0 31.7 %all-to-all-start.1 = ((bf16[8,128,1024]{2,1,0:T(8,128)(2,1)}), bf16[8,128,1024]{2,1,0:T(8,128)(2,1)}, u32[]{:S(2)}, u32[]{:S(2)}) async-start(bf16[8,128,1024]{2,1,0:T(8,128)(2,1)} %broadcast_in_dim.11), calls=%async_computation.1 | async-start | bytes 4194304 | tf_op jit(solution)/shard_map/all_to_all | solution.py:32
  91.5 0.9 copy-start.5
  118.7 12.3 %copy-start.6 = (bf16[2048]{0:T(1024)(128)(2,1)S(1)}, bf16[2048]{0:T(1024)(128)(2,1)}, u32[]{:S(2)}) copy-start(bf16[2048]{0:T(1024)(128)(2,1)} %param.15) | copy-start | bytes 12292
  118.7 12.3 %copy-start.7 = (s32[1024]{0:T(1024)S(1)}, s32[1024]{0:T(1024)}, u32[]{:S(2)}) copy-start(s32[1024]{0:T(1024)} %param.21) | copy-start | bytes 12292
  128.4 8.7 %collective-permute-start.5 = (bf16[256,2048]{1,0:T(8,128)(2,1)}, bf16[256,2048]{1,0:T(8,128)(2,1)S(1)}, u32[]{:S(2)}, u32[]{:S(2)}) collective-permute-start(bf16[256,2048]{1,0:T(8,128)(2,1)} %get-tuple-element.8), channel_id=1, source_target_pairs={{0,1},{1,0},{2,3},{3,2},{4,5},{5,4},{6,7},{7,6},{8,9},{9,8},{10,11... | collective-permute-start | bytes 3145736 | tf_op jit(solution)/shard_map/ppermute | solution.py:224
  139.7 19.5 %all-to-all-start.2 = ((bf16[4,64,2048]{2,1,0:T(8,128)(2,1)}), bf16[4,64,2048]{2,1,0:T(8,128)(2,1)S(1)}, u32[]{:S(2)}, u32[]{:S(2)}) async-start(bf16[4,64,2048]{2,1,0:T(8,128)(2,1)} %bitcast.34), calls=%async_computation.2 | async-start | bytes 2097152 | tf_op jit(solution)/shard_map/all_to_all | solution.py:234
  164.8 0.7 copy-start.1
  165.5 10.8 %all-to-all-start.3 = ((bf16[8,64,256]{2,1,0:T(8,128)(2,1)}), bf16[8,64,256]{2,1,0:T(8,128)(2,1)S(1)}, u32[]{:S(2)}, u32[]{:S(2)}) async-start(bf16[8,64,256]{2,1,0:T(8,128)(2,1)} %copy-done.1), calls=%async_computation.3 | async-start | bytes 524288 | tf_op jit(solution)/shard_map/all_to_all | solution.py:257
  176.3 18.7 %collective-permute-start.7 = (bf16[512,256]{1,0:T(8,128)(2,1)S(1)}, bf16[512,256]{1,0:T(8,128)(2,1)S(1)}, u32[]{:S(2)}, u32[]{:S(2)}) collective-permute-start(bf16[512,256]{1,0:T(8,128)(2,1)S(1)} %bitcast.36), channel_id=1, source_target_pairs={{0,16},{8,24},{16,32},{24,40},{32,48},{40,56},{48,64},{56,72},{64,... | collective-permute-start | bytes 786440 | tf_op jit(solution)/shard_map/ppermute | solution.py:26
  183.7 16.5 %collective-permute-start.6 = (bf16[512,256]{1,0:T(8,128)(2,1)S(1)}, bf16[512,256]{1,0:T(8,128)(2,1)S(1)}, u32[]{:S(2)}, u32[]{:S(2)}) collective-permute-start(bf16[512,256]{1,0:T(8,128)(2,1)S(1)} %bitcast.37), channel_id=1, source_target_pairs={{0,8},{8,16},{16,24},{24,32},{32,40},{40,48},{48,56},{56,64},{64,7... | collective-permute-start | bytes 786440 | tf_op jit(solution)/shard_map/ppermute | solution.py:26
  189.3 16.6 %copy-start.2 = (bf16[1024,128]{1,0:T(8,128)(2,1)S(1)}, bf16[1024,128]{1,0:T(8,128)(2,1)}, u32[]{:S(2)}) copy-start(bf16[1024,128]{1,0:T(8,128)(2,1)} %multiply_convert_fusion.rest_4_) | copy-start | bytes 786436
  200.6 18.0 %collective-permute-start.8 = (bf16[512,256]{1,0:T(8,128)(2,1)S(1)}, bf16[512,256]{1,0:T(8,128)(2,1)S(1)}, u32[]{:S(2)}, u32[]{:S(2)}) collective-permute-start(bf16[512,256]{1,0:T(8,128)(2,1)S(1)} %fusion.12), channel_id=1, source_target_pairs={{0,16},{8,24},{16,32},{24,40},{32,48},{40,56},{48,64},{56,72},{64,... | collective-permute-start | bytes 786440 | tf_op jit(solution)/shard_map/ppermute | solution.py:26
Sparse Core Ops, SparseCore 0:
  10.4 99.0 all-gather.1
